TPU v7x, 512 devices: a whole 4x8x8 slice. The times are simulated.
512 devices in a mesh: mask: 4 (over z_hi), rows: 128 (over z_lo, x, y, core).
Axes of the slice: x: 4, y: 8, z: 8 (z_hi: 4, z_lo: 2; z = z_hi * 2 + z_lo), core: 2. Of those that a mesh axis runs over, the one named last changes fastest.
Arguments:
- object_field: float32 [2, 4096, 4096], P(None, 'rows'), may hold values from -6 to 6
- phases: int32 [4, 4096, 4096], P('mask', 'rows'), may hold values from 0 to 3
- intensity: float32 [4, 4096, 4096], P('mask', 'rows'), may hold values from 0.5 to 4
Outputs:
- updated: float32 [2, 4096, 4096], P(None, 'rows')
- gradient: float32 [2, 4096, 4096], P(None, 'rows')
Inputs may be any that keep to these rules, and one draw needn't show every extreme that they name: `phases`: index k stands for the mask entry i^k.
All inputs are finite; a program needn't handle non-finite values.
Results may differ from a plain program's by a relative error of at most 0.00011.
Values sent between devices are 32-bit elements; how exact they have to be, the bound alone decides.
No kernel may reach another device: no remote copies, remote signals or barrier semaphores. Data moves between devices by JAX's collectives and lax.ppermute only.
A program may use at most 64 MiB of HBM per device.

v0:
```python
import functools
import math

import jax
import jax.numpy as jnp
import ml_dtypes
import numpy as np
from jax import lax
from jax.experimental import pallas as pl
from jax.experimental.pallas import tpu as pltpu
from jax.sharding import PartitionSpec as P

N = 4096
LANES = 128
SHORT = 32
OCT = 8
MASKS = 4
step_size = 0.2


def _split(table):
    high = table.astype(np.float32).astype(ml_dtypes.bfloat16)
    low = (table - high.astype(np.float64)).astype(np.float32).astype(ml_dtypes.bfloat16)
    return high, low


@functools.lru_cache(maxsize=None)
def tables():
    i128 = np.arange(LANES)
    w = np.exp(-2j * math.pi * (np.outer(i128, i128) % LANES) / LANES) / 64.0
    left = np.block([[w.real, -w.imag], [w.imag, w.real]])
    t = np.exp(-2j * math.pi * np.outer(np.arange(SHORT), i128) / N)
    t = np.broadcast_to(t[:, None, :], (SHORT, OCT, LANES))
    row_tw = np.stack([t.real, t.imag]).astype(np.float32)
    rho = i128 % OCT
    row = np.arange(MASKS)[:, None] * OCT + rho[None, :]
    t = np.exp(-2j * math.pi * (i128[None, :, None] * row[:, None, :]) / N)
    col_tw = np.stack([t.real, t.imag]).astype(np.float32)
    blocks = []
    for e in range(4):
        r8 = np.arange(OCT)
        small = np.exp(-2j * math.pi * np.outer(r8, r8) / 8 - 2j * math.pi * r8[:, None] * e / 32)
        big = np.kron(np.eye(16), small)
        blocks.append(np.block([[big.real, big.imag], [-big.imag, big.real]]))
    lh, ll = _split(left)
    ih, il = _split(left.T)
    mh, ml = _split(np.stack(blocks))
    return dict(lh=lh, ll=ll, ih=ih, il=il, mh=mh, ml=ml, row_tw=row_tw, col_tw=col_tw)


def split(x):
    high = x.astype(jnp.bfloat16)
    return high, (x - high.astype(jnp.float32)).astype(jnp.bfloat16)


def dot3(a, b, dims):
    dot = functools.partial(
        lax.dot_general, dimension_numbers=(dims, ((), ())), preferred_element_type=jnp.float32
    )
    return dot(a[0], b[0]) + (dot(a[0], b[1]) + dot(a[1], b[0]))


NN = ((1,), (0,))
NT = ((1,), (1,))


def cmul(a, b):
    return a[0] * b[0] - a[1] * b[1], a[0] * b[1] + a[1] * b[0]


def cadd(a, b):
    return a[0] + b[0], a[1] + b[1]


def csub(a, b):
    return a[0] - b[0], a[1] - b[1]


def times_i(a, sign):
    return (-a[1], a[0]) if sign > 0 else (a[1], -a[0])


def rotate(a, turns, length, sign):
    turns = turns % length
    if turns == 0:
        return a
    eighths = turns * 8 % (length * 8) / length
    if eighths == 4:
        return -a[0], -a[1]
    if eighths == 2:
        return times_i(a, sign)
    if eighths == 6:
        return times_i(a, -sign)
    angle = sign * 2 * math.pi * turns / length
    c, s = float(np.float32(math.cos(angle))), float(np.float32(math.sin(angle)))
    if eighths in (1, 3, 5, 7):
        h = float(np.float32(math.sqrt(0.5)))
        cs, ss = (1 if c > 0 else -1), (1 if s > 0 else -1)
        re = (a[0] if cs > 0 else -a[0]) - (a[1] if ss > 0 else -a[1])
        im = (a[1] if cs > 0 else -a[1]) + (a[0] if ss > 0 else -a[0])
        return re * h, im * h
    return a[0] * c - a[1] * s, a[0] * s + a[1] * c


def fft4(x, sign):
    a, b = cadd(x[0], x[2]), csub(x[0], x[2])
    c, d = cadd(x[1], x[3]), times_i(csub(x[1], x[3]), sign)
    return [cadd(a, c), cadd(b, d), csub(a, c), csub(b, d)]


def fft8(x, sign):
    even, odd = fft4(x[0::2], sign), fft4(x[1::2], sign)
    odd = [rotate(o, j, 8, sign) for j, o in enumerate(odd)]
    return [cadd(u, v) for u, v in zip(even, odd)] + [csub(u, v) for u, v in zip(even, odd)]


def fft32(load, store, mid, sign):
    for p0 in range(8):
        y = fft4([load(8 * p1 + p0) for p1 in range(4)], sign)
        for k0 in range(4):
            v = rotate(y[k0], p0 * k0, 32, sign)
            mid[0, k0 * 8 + p0] = v[0]
            mid[1, k0 * 8 + p0] = v[1]
    for k0 in range(4):
        y = fft8([(mid[0, k0 * 8 + p0], mid[1, k0 * 8 + p0]) for p0 in range(8)], sign)
        for k1 in range(8):
            store(k0 + 4 * k1, y[k1])


def code_times(code, z):
    odd = (code & 1) == 1
    a = jnp.where(odd, z[1], z[0])
    b = jnp.where(odd, z[0], z[1])
    return jnp.where((code == 1) | (code == 2), -a, a), jnp.where(code >= 2, -b, b)


def conj_code_times(code, z):
    odd = (code & 1) == 1
    a = jnp.where(odd, z[1], z[0])
    b = jnp.where(odd, z[0], z[1])
    return jnp.where(code >= 2, -a, a), jnp.where((code == 1) | (code == 2), -b, b)


def rows_forward(obj, code, lh, ll, tw, out, mid, xs):
    for m in range(MASKS):
        rows = slice(OCT * m, OCT * m + OCT)

        def load(p):
            cols = slice(LANES * p, LANES * p + LANES)
            return code_times(code[0, rows, cols], (obj[0, rows, cols], obj[1, rows, cols]))

        def store(k, v):
            v = cmul(v, (tw[0, k], tw[1, k]))
            xs[OCT * k : OCT * k + OCT, :LANES] = v[0]
            xs[OCT * k : OCT * k + OCT, LANES:] = v[1]

        fft32(load, store, mid, -1)
        y = dot3((lh[...], ll[...]), split(xs[...]), NT)
        for ri in range(2):
            for h in range(2):
                out[pl.ds(ri * 8 + 2 * m + h, LANES, stride=16), :] = y[
                    LANES * ri : LANES * ri + LANES, LANES * h : LANES * h + LANES
                ]


def columns(rec, inten, lh, ll, ih, il, mh, ml, tw, out, s):
    for m in range(MASKS):
        x = jnp.concatenate(
            [
                jnp.concatenate(
                    [rec[pl.ds(ri * 8 + 2 * m + h, LANES, stride=16), :] for h in range(2)], axis=1
                )
                for ri in range(2)
            ],
            axis=0,
        )
        y = dot3((lh[...], ll[...]), split(x), NN)
        t = (tw[0, m], tw[1, m])
        for h in range(2):
            cols = slice(LANES * h, LANES * h + LANES)
            v = cmul((y[:LANES, cols], y[LANES:, cols]), t)
            s[m, 0, h] = v[0]
            s[m, 1, h] = v[1]

    for h in range(2):
        def turn(i, _):
            rows = pl.ds(pl.multiple_of(i * OCT, OCT), OCT)
            y = fft4([(s[m, 0, h, rows, :], s[m, 1, h, rows, :]) for m in range(4)], -1)
            for e in range(4):
                s[e, 0, h, rows, :] = y[e][0]
                s[e, 1, h, rows, :] = y[e][1]
            return 0

        lax.fori_loop(0, LANES // OCT, turn, 0, unroll=True)

    for e in range(4):
        x = jnp.concatenate(
            [jnp.concatenate([s[e, 0, h], s[e, 1, h]], axis=1) for h in range(2)], axis=0
        )
        table = (mh[e], ml[e])
        y = dot3(split(x), table, NN)
        wr, wi = y[:, :LANES], y[:, LANES:]
        weight = wr * wr + wi * wi - inten[e]
        v = jnp.concatenate([wr * weight, wi * weight], axis=1)
        y = dot3(split(v), table, NT)
        for h in range(2):
            rows = slice(LANES * h, LANES * h + LANES)
            s[e, 0, h] = y[rows, :LANES]
            s[e, 1, h] = y[rows, LANES:]

    for h in range(2):
        def turn_back(i, _):
            rows = pl.ds(pl.multiple_of(i * OCT, OCT), OCT)
            y = fft4([(s[e, 0, h, rows, :], s[e, 1, h, rows, :]) for e in range(4)], 1)
            for m in range(4):
                v = cmul(y[m], (tw[0, m, rows, :], -tw[1, m, rows, :]))
                s[m, 0, h, rows, :] = v[0]
                s[m, 1, h, rows, :] = v[1]
            return 0

        lax.fori_loop(0, LANES // OCT, turn_back, 0, unroll=True)

    for m in range(MASKS):
        x = jnp.concatenate(
            [jnp.concatenate([s[m, ri, 0], s[m, ri, 1]], axis=1) for ri in range(2)], axis=0
        )
        y = dot3((ih[...], il[...]), split(x), NN)
        for ri in range(2):
            for h in range(2):
                out[pl.ds(m * 512 + ri * 2 + h, LANES, stride=4), :] = y[
                    LANES * ri : LANES * ri + LANES, LANES * h : LANES * h + LANES
                ]


def rows_back(rec, code, lh, ll, tw, out, mid, ys):
    for l in range(MASKS):
        x = jnp.concatenate(
            [
                jnp.concatenate(
                    [
                        rec[pl.ds(l * 512 + ri * 2 + h, LANES, stride=4), :].T
                        for ri in range(2)
                    ],
                    axis=1,
                )
                for h in range(2)
            ],
            axis=0,
        )
        ys[...] = dot3(split(x), (lh[...], ll[...]), NN)

        def load(k):
            rows = slice(OCT * k, OCT * k + OCT)
            return cmul((ys[rows, :LANES], ys[rows, LANES:]), (tw[0, k], -tw[1, k]))

        def store(p, v):
            cols = slice(LANES * p, LANES * p + LANES)
            v = conj_code_times(code[l, :, cols], v)
            for ri in range(2):
                if l == 0:
                    out[ri, :, cols] = v[ri]
                elif l < MASKS - 1:
                    out[ri, :, cols] += v[ri]
                else:
                    out[ri, :, cols] = (out[ri, :, cols] + v[ri]) * (1.0 / MASKS)

        fft32(load, store, mid, 1)


def finish(index, own, before, after, far_re, far_im, obj, updated, direction):
    me = index[0]

    def put(shift, ri, value):
        rows = pl.ds(pl.multiple_of(lax.rem(me + shift, MASKS) * OCT, OCT), OCT)
        direction[ri, rows, :] = value
        updated[ri, rows, :] = obj[ri, rows, :] - step_size * value

    for ri in range(2):
        put(0, ri, own[ri])
        put(3, ri, before[ri])
        put(1, ri, after[ri])
    put(2, 0, far_re[0])
    put(2, 1, far_im[0])


VM = pl.BlockSpec(memory_space=pltpu.VMEM)
F32 = jnp.float32


def call(kernel, name, out_shape, n_in, scratch, flops, vmem=24, smem_first=False):
    specs = [VM] * n_in
    if smem_first:
        specs[0] = pl.BlockSpec(memory_space=pltpu.SMEM)
    outs = jax.tree.map(lambda _: VM, out_shape)
    return pl.pallas_call(
        kernel,
        name=name,
        out_shape=out_shape,
        in_specs=specs,
        out_specs=outs,
        scratch_shapes=scratch,
        compiler_params=pltpu.CompilerParams(vmem_limit_bytes=vmem << 20),
        cost_estimate=pl.CostEstimate(flops=flops, bytes_accessed=3 << 20, transcendentals=0),
    )


def body(object_field, phases, intensity):
    t = {k: jnp.asarray(v) for k, v in tables().items()}
    sds = jax.ShapeDtypeStruct
    codes = lax.all_to_all(phases.reshape(MASKS, OCT, N), "mask", 0, 0, tiled=True)
    sent = call(
        rows_forward, "rows_forward", sds((2048, LANES), F32), 5,
        [pltpu.VMEM((2, SHORT, OCT, LANES), F32), pltpu.VMEM((256, 256), F32)], 1 << 29,
    )(object_field, phases, t["lh"], t["ll"], t["row_tw"])
    inten = intensity.reshape(2, 16, 8, 4, LANES).transpose(3, 0, 4, 1, 2).reshape(4, 256, LANES)
    rec = lax.all_to_all(sent.reshape(LANES, 16, LANES), "rows", 0, 0, tiled=True)
    back = call(
        columns, "columns", sds((2048, LANES), F32), 9,
        [pltpu.VMEM((4, 2, 2, LANES, LANES), F32)], 3 << 29,
    )(rec.reshape(2048, LANES), inten, t["lh"], t["ll"], t["ih"], t["il"], t["mh"], t["ml"], t["col_tw"])
    rec = lax.all_to_all(back.reshape(512, 4, LANES), ("mask", "rows"), 0, 0, tiled=True)
    part = call(
        rows_back, "rows_back", sds((2, OCT, N), F32), 5,
        [pltpu.VMEM((2, SHORT, OCT, LANES), F32), pltpu.VMEM((256, 256), F32)], 1 << 29,
    )(rec.reshape(2048, LANES), codes, t["lh"], t["ll"], t["row_tw"])
    up = [(i, (i + 1) % MASKS) for i in range(MASKS)]
    down = [((i + 1) % MASKS, i) for i in range(MASKS)]
    before = lax.ppermute(part, "mask", up)
    after = lax.ppermute(part, "mask", down)
    far_re = lax.ppermute(before[:1], "mask", up)
    far_im = lax.ppermute(after[1:], "mask", down)
    index = lax.axis_index("mask").astype(jnp.int32).reshape(1)
    whole = sds((2, SHORT, N), F32)
    return call(finish, "finish", (whole, whole), 7, [], 1 << 20, smem_first=True)(
        index, part, before, after, far_re, far_im, object_field
    )


def solution(mesh):
    return jax.shard_map(
        body,
        mesh=mesh,
        in_specs=(P(None, "rows", None), P("mask", "rows", None), P("mask", "rows", None)),
        out_specs=(P(None, "rows", None), P(None, "rows", None)),
        check_vma=False,
    )
```

profile of v0, /device:TPU:1, one launch (start us, length us, event | category | flops | bytes accessed | tf_op | source)
XLA Modules:
  0.0 151.2 jit_solution(516126563877727426)
XLA Ops:
  0.6 0.0 copy-start
  0.6 1.2 copy-done
  1.9 0.0 copy-start.2
  1.9 0.9 copy-done.2
  2.8 0.0 copy-start.4
  2.8 0.9 copy-done.4
  3.7 0.0 copy-start.6
  3.7 0.9 copy-done.6
  4.6 2.3 %rows_forward.1 = f32[2048,128]{1,0:T(8,128)S(1)} custom-call(f32[2,32,4096]{2,1,0:T(8,128)S(1)} %copy-done, s32[1,32,4096]{2,1,0:T(8,128)} %code.1, bf16[256,256]{1,0:T(8,128)(2,1)S(1)} %copy-done.4, bf16[256,256]{1,0:T(8,128)(2,1)S(1)} %copy-done.6, f32[2,32,8,128]{3,2,1,0:T(8,128)S(1)} %copy-done.2), custom_call_target="tpu_custom_call" | custom-call | flops 536870912 | bytes 3145728 | tf_op jit(solution)/shard_map/rows_forward/pallas_call | solution.py:311
  6.9 42.8 %all_to_all.15 = f32[128,16,128]{2,1,0:T(8,128)S(1)} all-to-all(f32[128,16,128]{2,1,0:T(8,128)S(1)} %bitcast.11), channel_id=1, replica_groups=mesh['mask'=4,'rows'=128] {'rows'}, dimensions={0} | all-to-all | bytes 2097152 | tf_op jit(solution)/shard_map/all_to_all | solution.py:316
  49.7 0.0 copy-start.13
  49.7 9.2 %all-to-all-start.2 = ((s32[4,8,4096]{2,1,0:T(8,128)}), s32[4,8,4096]{2,1,0:T(8,128)S(1)}, u32[]{:S(2)}, u32[]{:S(2)}) async-start(s32[4,8,4096]{2,1,0:T(8,128)} %bitcast.6), calls=%async_computation.2 | async-start | bytes 1048576 | tf_op jit(solution)/shard_map/all_to_all | solution.py:310
  59.0 0.0 copy-done.13
  59.0 0.3 reshape.31
  59.3 0.4 copy.17
  59.7 0.4 reshape.32
  60.2 0.0 copy-start.5
  60.2 0.0 copy-start.7
  60.2 0.0 copy-start.11
  60.2 0.2 copy.15.inten
  60.4 0.7 copy-done.5
  61.1 0.1 copy-done.7
  61.1 0.1 copy-done.11
  61.2 0.0 copy-start.8
  61.2 1.0 copy-done.8
  62.2 0.0 copy-start.9
  62.2 1.0 copy-done.9
  63.3 0.0 copy-start.10
  63.3 1.0 copy-done.10
  64.3 0.0 copy-start.12
  64.3 0.9 copy-done.12
  65.2 2.8 %columns.1 = f32[2048,128]{1,0:T(8,128)S(1)} custom-call(f32[2048,128]{1,0:T(8,128)S(1)} %bitcast.13, f32[4,256,128]{2,1,0:T(8,128)S(1)} %copy.15.inten, bf16[256,256]{1,0:T(8,128)(2,1)S(1)} %copy-done.5, bf16[256,256]{1,0:T(8,128)(2,1)S(1)} %copy-done.7, bf16[256,256]{1,0:T(8,128)(2,1)S(1)} %copy-done.11, bf16[256,256]{1,0:T(8,128)(2,1)S(1)} %copy-done.12, ...), custom_call_target="tpu_custom_call" | custom-call | flops 1610612736 | bytes 3145728 | tf_op jit(solution)/shard_map/columns/pallas_call | solution.py:317
  68.0 1.9 %all-to-all-done.2.code = s32[4,8,4096]{2,1,0:T(8,128)S(1)} async-done(((s32[4,8,4096]{2,1,0:T(8,128)}), s32[4,8,4096]{2,1,0:T(8,128)S(1)}, u32[]{:S(2)}, u32[]{:S(2)}) %all-to-all-start.2) | async-done | bytes 524320 | tf_op jit(solution)/shard_map/all_to_all | solution.py:310
  69.9 0.0 copy-start.3
  69.9 48.7 %all_to_all.16 = f32[512,4,128]{2,1,0:T(4,128)S(1)} all-to-all(f32[512,4,128]{2,1,0:T(4,128)S(1)} %bitcast.14), channel_id=1, replica_groups=mesh['mask'=4,'rows'=128] {'mask','rows'}, dimensions={0} | all-to-all | bytes 2097152 | tf_op jit(solution)/shard_map/all_to_all | solution.py:321
  118.6 0.0 copy-done.3
  118.6 0.0 copy-start.1
  118.6 1.0 rows_back.1.own
  119.6 3.3 %collective-permute-start = (f32[2,8,4096]{2,1,0:T(8,128)S(1)}, f32[2,8,4096]{2,1,0:T(8,128)S(1)}, u32[]{:S(2)}, u32[]{:S(2)}) collective-permute-start(f32[2,8,4096]{2,1,0:T(8,128)S(1)} %rows_back.1.own), channel_id=1, source_target_pairs={{0,128},{128,256},{256,384},{384,0},{1,129},{129,257},{257,385},{3... | collective-permute-start | bytes 786440 | tf_op jit(solution)/shard_map/ppermute | solution.py:328
  122.9 4.1 %collective-permute-start.1 = (f32[2,8,4096]{2,1,0:T(8,128)S(1)}, f32[2,8,4096]{2,1,0:T(8,128)S(1)}, u32[]{:S(2)}, u32[]{:S(2)}) collective-permute-start(f32[2,8,4096]{2,1,0:T(8,128)S(1)} %rows_back.1.own), channel_id=1, source_target_pairs={{128,0},{256,128},{384,256},{0,384},{129,1},{257,129},{385,257},{1... | collective-permute-start | bytes 786440 | tf_op jit(solution)/shard_map/ppermute | solution.py:329
  127.0 9.8 %collective-permute-done.before = f32[2,8,4096]{2,1,0:T(8,128)S(1)} collective-permute-done((f32[2,8,4096]{2,1,0:T(8,128)S(1)}, f32[2,8,4096]{2,1,0:T(8,128)S(1)}, u32[]{:S(2)}, u32[]{:S(2)}) %collective-permute-start) | collective-permute-done | bytes 262176 | tf_op jit(solution)/shard_map/ppermute | solution.py:328
  136.8 2.6 %collective-permute-start.2 = (f32[1,8,4096]{2,1,0:T(8,128)S(1)}, f32[1,8,4096]{2,1,0:T(8,128)S(1)}, u32[]{:S(2)}, u32[]{:S(2)}) collective-permute-start(f32[1,8,4096]{2,1,0:T(8,128)S(1)} %slice.8), channel_id=1, source_target_pairs={{0,128},{128,256},{256,384},{384,0},{1,129},{129,257},{257,385},{3... | collective-permute-start | bytes 393224 | tf_op jit(solution)/shard_map/ppermute | solution.py:330
  139.5 0.0 collective-permute-done.1.after
  139.5 4.8 %collective-permute-start.3 = (f32[1,8,4096]{2,1,0:T(8,128)S(1)}, f32[1,8,4096]{2,1,0:T(8,128)S(1)}, u32[]{:S(2)}, u32[]{:S(2)}) collective-permute-start(f32[1,8,4096]{2,1,0:T(8,128)S(1)} %slice.9), channel_id=1, source_target_pairs={{128,0},{256,128},{384,256},{0,384},{129,1},{257,129},{385,257},{1... | collective-permute-start | bytes 393224 | tf_op jit(solution)/shard_map/ppermute | solution.py:331
  144.3 3.7 %collective-permute-done.2.far_re = f32[1,8,4096]{2,1,0:T(8,128)S(1)} collective-permute-done((f32[1,8,4096]{2,1,0:T(8,128)S(1)}, f32[1,8,4096]{2,1,0:T(8,128)S(1)}, u32[]{:S(2)}, u32[]{:S(2)}) %collective-permute-start.2) | collective-permute-done | bytes 131104 | tf_op jit(solution)/shard_map/ppermute | solution.py:330
  148.0 1.8 %collective-permute-done.3.far_im = f32[1,8,4096]{2,1,0:T(8,128)S(1)} collective-permute-done((f32[1,8,4096]{2,1,0:T(8,128)S(1)}, f32[1,8,4096]{2,1,0:T(8,128)S(1)}, u32[]{:S(2)}, u32[]{:S(2)}) %collective-permute-start.3) | collective-permute-done | bytes 131104 | tf_op jit(solution)/shard_map/ppermute | solution.py:331
  149.8 0.0 copy-done.1
  149.8 1.5 finish.1
  (2 shorter events, 0.0 us)
Async XLA Ops:
  0.6 1.2 copy-start
  1.9 0.9 copy-start.2
  2.8 0.9 copy-start.4
  3.7 0.9 copy-start.6
  49.7 9.3 %copy-start.13 = (f32[1,32,4096]{2,1,0:T(8,128)S(1)}, f32[1,32,4096]{2,1,0:T(8,128)}, u32[]{:S(2)}) copy-start(f32[1,32,4096]{2,1,0:T(8,128)} %param.13) | copy-start | bytes 1572868
  49.7 20.2 %all-to-all-start.2 = ((s32[4,8,4096]{2,1,0:T(8,128)}), s32[4,8,4096]{2,1,0:T(8,128)S(1)}, u32[]{:S(2)}, u32[]{:S(2)}) async-start(s32[4,8,4096]{2,1,0:T(8,128)} %bitcast.6), calls=%async_computation.2 | async-start | bytes 1048576 | tf_op jit(solution)/shard_map/all_to_all | solution.py:310
  60.2 0.9 copy-start.5
  60.2 1.0 copy-start.7
  60.2 1.0 copy-start.11
  61.2 1.0 copy-start.8
  62.2 1.0 copy-start.9
  63.3 1.0 copy-start.10
  64.3 0.9 copy-start.12
  69.9 48.7 %copy-start.3 = (f32[2,32,8,128]{3,2,1,0:T(8,128)S(1)}, f32[2,32,8,128]{3,2,1,0:T(8,128)}, u32[]{:S(2)}) copy-start(f32[2,32,8,128]{3,2,1,0:T(8,128)} %constant.28.clone.tw) | copy-start | bytes 786436
  118.6 31.2 %copy-start.1 = (f32[2,32,4096]{2,1,0:T(8,128)S(1)}, f32[2,32,4096]{2,1,0:T(8,128)}, u32[]{:S(2)}) copy-start(f32[2,32,4096]{2,1,0:T(8,128)} %obj.3) | copy-start | bytes 3145732
  119.6 17.2 %collective-permute-start = (f32[2,8,4096]{2,1,0:T(8,128)S(1)}, f32[2,8,4096]{2,1,0:T(8,128)S(1)}, u32[]{:S(2)}, u32[]{:S(2)}) collective-permute-start(f32[2,8,4096]{2,1,0:T(8,128)S(1)} %rows_back.1.own), channel_id=1, source_target_pairs={{0,128},{128,256},{256,384},{384,0},{1,129},{129,257},{257,385},{3... | collective-permute-start | bytes 786440 | tf_op jit(solution)/shard_map/ppermute | solution.py:328
  122.9 16.6 %collective-permute-start.1 = (f32[2,8,4096]{2,1,0:T(8,128)S(1)}, f32[2,8,4096]{2,1,0:T(8,128)S(1)}, u32[]{:S(2)}, u32[]{:S(2)}) collective-permute-start(f32[2,8,4096]{2,1,0:T(8,128)S(1)} %rows_back.1.own), channel_id=1, source_target_pairs={{128,0},{256,128},{384,256},{0,384},{129,1},{257,129},{385,257},{1... | collective-permute-start | bytes 786440 | tf_op jit(solution)/shard_map/ppermute | solution.py:329
  136.8 11.2 %collective-permute-start.2 = (f32[1,8,4096]{2,1,0:T(8,128)S(1)}, f32[1,8,4096]{2,1,0:T(8,128)S(1)}, u32[]{:S(2)}, u32[]{:S(2)}) collective-permute-start(f32[1,8,4096]{2,1,0:T(8,128)S(1)} %slice.8), channel_id=1, source_target_pairs={{0,128},{128,256},{256,384},{384,0},{1,129},{129,257},{257,385},{3... | collective-permute-start | bytes 393224 | tf_op jit(solution)/shard_map/ppermute | solution.py:330
  139.5 10.3 %collective-permute-start.3 = (f32[1,8,4096]{2,1,0:T(8,128)S(1)}, f32[1,8,4096]{2,1,0:T(8,128)S(1)}, u32[]{:S(2)}, u32[]{:S(2)}) collective-permute-start(f32[1,8,4096]{2,1,0:T(8,128)S(1)} %slice.9), channel_id=1, source_target_pairs={{128,0},{256,128},{384,256},{0,384},{129,1},{257,129},{385,257},{1... | collective-permute-start | bytes 393224 | tf_op jit(solution)/shard_map/ppermute | solution.py:331
where the time goes:
time: 152 us; the launch traced here: 151 us
  blocking collectives  91.5 us (60%)
  starting transfers between devices  24 us (16%)
  waiting for transfers between devices  17.2 us (11%)
  local copies, waits for them, and re-layouts  10.2 us (7%)
  Pallas kernels  7.54 us (5%)
    all_to_all x1, blocking collectives, body(): lax.all_to_all(back.reshape(512, 4, LANES), ('mask', 'rows'), 0, 0, tiled...  48.7 us
    all_to_all x1, blocking collectives, body(): lax.all_to_all(sent.reshape(LANES, 16, LANES), 'rows', 0, 0, tiled=True)  42.8 us
    ppermute x1, waiting for transfers between devices, body(): before = lax.ppermute(part, 'mask', up)  9.8 us
    all_to_all x1, starting transfers between devices, body(): lax.all_to_all(phases.reshape(MASKS, OCT, N), 'mask', 0, 0, tiled=True)  9.25 us
    unnamed x28, local copies, waits for them, and re-layouts  8.83 us
    ppermute x1, starting transfers between devices, body(): far_im = lax.ppermute(after[1:], 'mask', down)  4.76 us
    ppermute x1, starting transfers between devices, body(): after = lax.ppermute(part, 'mask', down)  4.12 us
    ppermute x1, waiting for transfers between devices, body(): far_re = lax.ppermute(before[:1], 'mask', up)  3.71 us
  transfers between devices with their start and end apart: 5, of which 4 were waited for; matrix products, arithmetic and copies ran while one was open for 1% of the time, Pallas kernels for 2%

commit v1 on v0

--- a/solution.py
+++ b/solution.py
@@ -30,7 +30,6 @@
     w = np.exp(-2j * math.pi * (np.outer(i128, i128) % LANES) / LANES) / 64.0
     left = np.block([[w.real, -w.imag], [w.imag, w.real]])
     t = np.exp(-2j * math.pi * np.outer(np.arange(SHORT), i128) / N)
-    t = np.broadcast_to(t[:, None, :], (SHORT, OCT, LANES))
     row_tw = np.stack([t.real, t.imag]).astype(np.float32)
     rho = i128 % OCT
     row = np.arange(MASKS)[:, None] * OCT + rho[None, :]
@@ -142,25 +141,24 @@
 
 
 def rows_forward(obj, code, lh, ll, tw, out, mid, xs):
-    for m in range(MASKS):
-        rows = slice(OCT * m, OCT * m + OCT)
-
-        def load(p):
-            cols = slice(LANES * p, LANES * p + LANES)
-            return code_times(code[0, rows, cols], (obj[0, rows, cols], obj[1, rows, cols]))
-
-        def store(k, v):
-            v = cmul(v, (tw[0, k], tw[1, k]))
-            xs[OCT * k : OCT * k + OCT, :LANES] = v[0]
-            xs[OCT * k : OCT * k + OCT, LANES:] = v[1]
-
-        fft32(load, store, mid, -1)
-        y = dot3((lh[...], ll[...]), split(xs[...]), NT)
-        for ri in range(2):
-            for h in range(2):
-                out[pl.ds(ri * 8 + 2 * m + h, LANES, stride=16), :] = y[
-                    LANES * ri : LANES * ri + LANES, LANES * h : LANES * h + LANES
-                ]
+    m = pl.program_id(0)
+
+    def load(p):
+        cols = slice(LANES * p, LANES * p + LANES)
+        return code_times(code[0, :, cols], (obj[0, :, cols], obj[1, :, cols]))
+
+    def store(k, v):
+        v = cmul(v, (tw[0, k : k + 1], tw[1, k : k + 1]))
+        xs[OCT * k : OCT * k + OCT, :LANES] = v[0]
+        xs[OCT * k : OCT * k + OCT, LANES:] = v[1]
+
+    fft32(load, store, mid, -1)
+    y = dot3((lh[...], ll[...]), split(xs[...]), NT)
+    for ri in range(2):
+        for h in range(2):
+            out[pl.ds(ri * 8 + 2 * m + h, LANES, stride=16), :] = y[
+                LANES * ri : LANES * ri + LANES, LANES * h : LANES * h + LANES
+            ]
 
 
 def columns(rec, inten, lh, ll, ih, il, mh, ml, tw, out, s):
@@ -251,7 +249,7 @@
 
         def load(k):
             rows = slice(OCT * k, OCT * k + OCT)
-            return cmul((ys[rows, :LANES], ys[rows, LANES:]), (tw[0, k], -tw[1, k]))
+            return cmul((ys[rows, :LANES], ys[rows, LANES:]), (tw[0, k : k + 1], -tw[1, k : k + 1]))
 
         def store(p, v):
             cols = slice(LANES * p, LANES * p + LANES)
@@ -287,10 +285,10 @@
 F32 = jnp.float32
 
 
-def call(kernel, name, out_shape, n_in, scratch, flops, vmem=24, smem_first=False):
+def call(kernel, name, out_shape, n_in, scratch, flops, vmem=24, smem=()):
     specs = [VM] * n_in
-    if smem_first:
-        specs[0] = pl.BlockSpec(memory_space=pltpu.SMEM)
+    for i in smem:
+        specs[i] = pl.BlockSpec(memory_space=pltpu.SMEM)
     outs = jax.tree.map(lambda _: VM, out_shape)
     return pl.pallas_call(
         kernel,
@@ -307,10 +305,29 @@
 def body(object_field, phases, intensity):
     t = {k: jnp.asarray(v) for k, v in tables().items()}
     sds = jax.ShapeDtypeStruct
-    codes = lax.all_to_all(phases.reshape(MASKS, OCT, N), "mask", 0, 0, tiled=True)
-    sent = call(
-        rows_forward, "rows_forward", sds((2048, LANES), F32), 5,
-        [pltpu.VMEM((2, SHORT, OCT, LANES), F32), pltpu.VMEM((256, 256), F32)], 1 << 29,
+    index = lax.axis_index("mask").astype(jnp.int32).reshape(1)
+    every = lax.all_gather(phases, "mask", axis=0, tiled=True)
+    codes = lax.dynamic_slice_in_dim(every, index[0] * OCT, OCT, axis=1)
+    octet = lambda m: (0, m, 0)
+    sent = pl.pallas_call(
+        rows_forward,
+        name="rows_forward",
+        out_shape=sds((2048, LANES), F32),
+        grid=(MASKS,),
+        in_specs=[
+            pl.BlockSpec((2, OCT, N), octet),
+            pl.BlockSpec((1, OCT, N), octet),
+            pl.BlockSpec((256, 256), lambda m: (0, 0)),
+            pl.BlockSpec((256, 256), lambda m: (0, 0)),
+            pl.BlockSpec((2, SHORT, LANES), lambda m: (0, 0, 0)),
+        ],
+        out_specs=pl.BlockSpec((2048, LANES), lambda m: (0, 0)),
+        scratch_shapes=[
+            pltpu.VMEM((2, SHORT, OCT, LANES), F32),
+            pltpu.VMEM((256, 256), F32),
+        ],
+        compiler_params=pltpu.CompilerParams(vmem_limit_bytes=60 << 20),
+        cost_estimate=pl.CostEstimate(flops=1 << 29, bytes_accessed=3 << 20, transcendentals=0),
     )(object_field, phases, t["lh"], t["ll"], t["row_tw"])
     inten = intensity.reshape(2, 16, 8, 4, LANES).transpose(3, 0, 4, 1, 2).reshape(4, 256, LANES)
     rec = lax.all_to_all(sent.reshape(LANES, 16, LANES), "rows", 0, 0, tiled=True)
@@ -329,9 +346,8 @@
     after = lax.ppermute(part, "mask", down)
     far_re = lax.ppermute(before[:1], "mask", up)
     far_im = lax.ppermute(after[1:], "mask", down)
-    index = lax.axis_index("mask").astype(jnp.int32).reshape(1)
     whole = sds((2, SHORT, N), F32)
-    return call(finish, "finish", (whole, whole), 7, [], 1 << 20, smem_first=True)(
+    return call(finish, "finish", (whole, whole), 7, [], 1 << 20, smem=(0,))(
         index, part, before, after, far_re, far_im, object_field
     )
 

time: 152 us -> 156 us (1.026)
  the two profiles are of different devices: /device:TPU:1 before, /device:TPU:2 now
where the time goes in v1:
time: 156 us
  waiting for transfers between devices  77.6 us (50%)
  starting transfers between devices  45.9 us (29%)
  between operations  14.3 us (9%)
  Pallas kernels  10.8 us (7%)
  local copies, waits for them, and re-layouts  7.08 us (5%)
    all_gather x1, waiting for transfers between devices, body(): every = lax.all_gather(phases, 'mask', axis=0, tiled=True)  36.4 us
    all_to_all x1, waiting for transfers between devices, body(): lax.all_to_all(sent.reshape(LANES, 16, LANES), 'rows', 0, 0, tiled=True)  21 us
    all_to_all x1, starting transfers between devices, body(): lax.all_to_all(back.reshape(512, 4, LANES), ('mask', 'rows'), 0, 0, tiled...  19.1 us
    all_to_all x1, starting transfers between devices, body(): lax.all_to_all(sent.reshape(LANES, 16, LANES), 'rows', 0, 0, tiled=True)  13.2 us
    ppermute x1, waiting for transfers between devices, body(): after = lax.ppermute(part, 'mask', down)  9.9 us
    ppermute x1, waiting for transfers between devices, body(): far_re = lax.ppermute(before[:1], 'mask', up)  6.42 us
    reshape x4, local copies, waits for them, and re-layouts, body(): intensity.reshape(2, 16, 8, 4, LANES).transpose(3, 0, 4, 1, 2)  5.03 us
    pallas_call x1, Pallas kernels, body(): pl.pallas_call(rows_forward, name='rows_forward', out_shape=sds((2048, LA...  4.59 us
  transfers between devices with their start and end apart: 7, of which 5 were waited for; matrix products, arithmetic and copies ran while one was open for 4% of the time, Pallas kernels for 2%

profile of v1, /device:TPU:2, one launch (start us, length us, event | category | flops | bytes accessed | tf_op | source)
XLA Modules:
  0.0 155.7 jit_solution(3066160892532563325)
XLA Ops:
  7.2 0.0 copy-start.9
  7.2 4.6 %rows_forward.1 = f32[2048,128]{1,0:T(8,128)} custom-call(f32[2,32,4096]{2,1,0:T(8,128)} %obj.3, s32[1,32,4096]{2,1,0:T(8,128)} %code.1, bf16[256,256]{1,0:T(8,128)(2,1)} %constant.28.clone.lh, bf16[256,256]{1,0:T(8,128)(2,1)} %constant.29.clone.ll, f32[2,32,128]{2,1,0:T(8,128)} %constant.34.clone.tw), custom_call_target="tpu_custom_call" | custom-call | flops 536870912 | bytes 3145728 | tf_op jit(solution)/shard_map/rows_forward/pallas_call | solution.py:312
  11.8 13.2 %all-to-all-start = ((f32[128,16,128]{2,1,0:T(8,128)}), f32[128,16,128]{2,1,0:T(8,128)S(1)}, u32[]{:S(2)}, u32[]{:S(2)}) async-start(f32[128,16,128]{2,1,0:T(8,128)} %bitcast.12), calls=%async_computation | async-start | bytes 2097152 | tf_op jit(solution)/shard_map/all_to_all | solution.py:333
  25.0 0.0 all-gather.2.cloned.1.call-start
  25.1 0.7 all-gather.2.cloned.1.call-update
  25.8 0.0 copy-done.9
  25.8 0.0 copy-start.1
  25.8 0.0 copy-start.2
  25.8 0.0 copy-start.4
  25.8 0.0 copy-start.5
  25.8 0.0 copy-start.6
  25.8 0.0 copy-start.7
  25.8 1.1 reshape.28
  27.0 1.4 copy.19
  28.4 1.2 reshape.29
  29.7 1.2 copy.17.inten
  30.9 21.0 %all-to-all-done = f32[128,16,128]{2,1,0:T(8,128)S(1)} async-done(((f32[128,16,128]{2,1,0:T(8,128)}), f32[128,16,128]{2,1,0:T(8,128)S(1)}, u32[]{:S(2)}, u32[]{:S(2)}) %all-to-all-start) | async-done | bytes 1048608 | tf_op jit(solution)/shard_map/all_to_all | solution.py:333
  51.9 0.0 copy-done.1
  51.9 0.0 copy-done.2
  51.9 0.0 copy-done.4
  51.9 0.0 copy-done.5
  51.9 0.0 copy-done.6
  52.0 0.0 copy-done.7
  52.0 0.0 copy-start.8
  52.0 0.9 copy-done.8
  52.9 3.8 %columns.1 = f32[2048,128]{1,0:T(8,128)} custom-call(f32[2048,128]{1,0:T(8,128)S(1)} %bitcast.11, f32[4,256,128]{2,1,0:T(8,128)S(1)} %copy.17.inten, bf16[256,256]{1,0:T(8,128)(2,1)S(1)} %copy-done.2, bf16[256,256]{1,0:T(8,128)(2,1)S(1)} %copy-done.1, bf16[256,256]{1,0:T(8,128)(2,1)S(1)} %copy-done.8, bf16[256,256]{1,0:T(8,128)(2,1)S(1)} %copy-done.7, ...), custom_call_target="tpu_custom_call" | custom-call | flops 1610612736 | bytes 3145728 | tf_op jit(solution)/shard_map/columns/pallas_call | solution.py:334
  56.6 0.0 copy-start.3
  56.6 19.1 %all-to-all-start.1 = ((f32[512,4,128]{2,1,0:T(4,128)}), f32[512,4,128]{2,1,0:T(4,128)S(1)}, u32[]{:S(2)}, u32[]{:S(2)}) async-start(f32[512,4,128]{2,1,0:T(4,128)} %bitcast.4), calls=%async_computation.1 | async-start | bytes 2097152 | tf_op jit(solution)/shard_map/all_to_all | solution.py:338
  75.8 0.0 copy-start
  75.8 36.4 %all-gather.2.cloned.1.call-done = s32[4,32,4096]{2,1,0:T(8,128)} async-done(((s32[1,32,4096]{2,1,0:T(8,128)}), s32[4,32,4096]{2,1,0:T(8,128)}) %all-gather.2.cloned.1.call-update) | async-done | bytes 2097168 | tf_op jit(solution)/shard_map/all_gather | solution.py:309
  112.2 1.1 constant_dynamic-slice_fusion.code
  113.3 0.0 all-to-all-done.1
  113.3 0.0 copy-done.3
  113.3 1.0 rows_back.1.own
  114.3 3.2 %collective-permute-start.1 = (f32[2,8,4096]{2,1,0:T(8,128)S(1)}, f32[2,8,4096]{2,1,0:T(8,128)S(1)}, u32[]{:S(2)}, u32[]{:S(2)}) collective-permute-start(f32[2,8,4096]{2,1,0:T(8,128)S(1)} %rows_back.1.own), channel_id=1, source_target_pairs={{128,0},{256,128},{384,256},{0,384},{129,1},{257,129},{385,257},{1... | collective-permute-start | bytes 786440 | tf_op jit(solution)/shard_map/ppermute | solution.py:346
  117.5 3.6 %collective-permute-start = (f32[2,8,4096]{2,1,0:T(8,128)S(1)}, f32[2,8,4096]{2,1,0:T(8,128)S(1)}, u32[]{:S(2)}, u32[]{:S(2)}) collective-permute-start(f32[2,8,4096]{2,1,0:T(8,128)S(1)} %rows_back.1.own), channel_id=1, source_target_pairs={{0,128},{128,256},{256,384},{384,0},{1,129},{129,257},{257,385},{3... | collective-permute-start | bytes 786440 | tf_op jit(solution)/shard_map/ppermute | solution.py:345
  121.1 9.9 %collective-permute-done.1.after = f32[2,8,4096]{2,1,0:T(8,128)S(1)} collective-permute-done((f32[2,8,4096]{2,1,0:T(8,128)S(1)}, f32[2,8,4096]{2,1,0:T(8,128)S(1)}, u32[]{:S(2)}, u32[]{:S(2)}) %collective-permute-start.1) | collective-permute-done | bytes 262176 | tf_op jit(solution)/shard_map/ppermute | solution.py:346
  131.0 4.4 %collective-permute-start.3 = (f32[1,8,4096]{2,1,0:T(8,128)S(1)}, f32[1,8,4096]{2,1,0:T(8,128)S(1)}, u32[]{:S(2)}, u32[]{:S(2)}) collective-permute-start(f32[1,8,4096]{2,1,0:T(8,128)S(1)} %slice.9), channel_id=1, source_target_pairs={{128,0},{256,128},{384,256},{0,384},{129,1},{257,129},{385,257},{1... | collective-permute-start | bytes 393224 | tf_op jit(solution)/shard_map/ppermute | solution.py:348
  135.4 0.0 collective-permute-done.before
  135.4 2.3 %collective-permute-start.2 = (f32[1,8,4096]{2,1,0:T(8,128)S(1)}, f32[1,8,4096]{2,1,0:T(8,128)S(1)}, u32[]{:S(2)}, u32[]{:S(2)}) collective-permute-start(f32[1,8,4096]{2,1,0:T(8,128)S(1)} %slice.8), channel_id=1, source_target_pairs={{0,128},{128,256},{256,384},{384,0},{1,129},{129,257},{257,385},{3... | collective-permute-start | bytes 393224 | tf_op jit(solution)/shard_map/ppermute | solution.py:347
  137.8 3.1 %collective-permute-done.3.far_im = f32[1,8,4096]{2,1,0:T(8,128)S(1)} collective-permute-done((f32[1,8,4096]{2,1,0:T(8,128)S(1)}, f32[1,8,4096]{2,1,0:T(8,128)S(1)}, u32[]{:S(2)}, u32[]{:S(2)}) %collective-permute-start.3) | collective-permute-done | bytes 131104 | tf_op jit(solution)/shard_map/ppermute | solution.py:348
  140.9 6.4 %collective-permute-done.2.far_re = f32[1,8,4096]{2,1,0:T(8,128)S(1)} collective-permute-done((f32[1,8,4096]{2,1,0:T(8,128)S(1)}, f32[1,8,4096]{2,1,0:T(8,128)S(1)}, u32[]{:S(2)}, u32[]{:S(2)}) %collective-permute-start.2) | collective-permute-done | bytes 131104 | tf_op jit(solution)/shard_map/ppermute | solution.py:347
  147.3 0.0 copy-done
  147.3 1.5 finish.1
  (2 shorter events, 0.0 us)
Async XLA Ops:
  7.2 18.6 %copy-start.9 = (f32[1,32,4096]{2,1,0:T(8,128)S(1)}, f32[1,32,4096]{2,1,0:T(8,128)}, u32[]{:S(2)}) copy-start(f32[1,32,4096]{2,1,0:T(8,128)} %param.13) | copy-start | bytes 1572868
  11.8 40.2 %all-to-all-start = ((f32[128,16,128]{2,1,0:T(8,128)}), f32[128,16,128]{2,1,0:T(8,128)S(1)}, u32[]{:S(2)}, u32[]{:S(2)}) async-start(f32[128,16,128]{2,1,0:T(8,128)} %bitcast.12), calls=%async_computation | async-start | bytes 2097152 | tf_op jit(solution)/shard_map/all_to_all | solution.py:333
  25.0 87.2 %all-gather.2.cloned.1.call-start = ((), (), s32[]{:S(2)}) async-start(), calls=%async_computation.2 | async-start | bytes 2621440 | tf_op jit(solution)/shard_map/all_gather | solution.py:309
  25.8 26.2 %copy-start.1 = (bf16[256,256]{1,0:T(8,128)(2,1)S(1)}, bf16[256,256]{1,0:T(8,128)(2,1)}, u32[]{:S(2)}) copy-start(bf16[256,256]{1,0:T(8,128)(2,1)} %constant.29.clone.ll) | copy-start | bytes 393220
  25.8 26.1 %copy-start.2 = (bf16[256,256]{1,0:T(8,128)(2,1)S(1)}, bf16[256,256]{1,0:T(8,128)(2,1)}, u32[]{:S(2)}) copy-start(bf16[256,256]{1,0:T(8,128)(2,1)} %constant.28.clone.lh) | copy-start | bytes 393220
  25.8 26.1 %copy-start.4 = (f32[2,4,128,128]{3,2,1,0:T(8,128)S(1)}, f32[2,4,128,128]{3,2,1,0:T(8,128)}, u32[]{:S(2)}) copy-start(f32[2,4,128,128]{3,2,1,0:T(8,128)} %constant.35.clone.tw) | copy-start | bytes 1572868
  25.8 26.1 %copy-start.5 = (bf16[4,256,256]{2,1,0:T(8,128)(2,1)S(1)}, bf16[4,256,256]{2,1,0:T(8,128)(2,1)}, u32[]{:S(2)}) copy-start(bf16[4,256,256]{2,1,0:T(8,128)(2,1)} %constant.33.clone.ml) | copy-start | bytes 1572868
  25.8 26.1 %copy-start.6 = (bf16[4,256,256]{2,1,0:T(8,128)(2,1)S(1)}, bf16[4,256,256]{2,1,0:T(8,128)(2,1)}, u32[]{:S(2)}) copy-start(bf16[4,256,256]{2,1,0:T(8,128)(2,1)} %constant.32.clone.mh) | copy-start | bytes 1572868
  25.8 26.1 %copy-start.7 = (bf16[256,256]{1,0:T(8,128)(2,1)S(1)}, bf16[256,256]{1,0:T(8,128)(2,1)}, u32[]{:S(2)}) copy-start(bf16[256,256]{1,0:T(8,128)(2,1)} %constant.31.clone.il) | copy-start | bytes 393220
  52.0 0.9 copy-start.8
  56.6 56.7 %copy-start.3 = (f32[2,32,128]{2,1,0:T(8,128)S(1)}, f32[2,32,128]{2,1,0:T(8,128)}, u32[]{:S(2)}) copy-start(f32[2,32,128]{2,1,0:T(8,128)} %constant.34.clone.tw) | copy-start | bytes 98308
  56.6 56.7 %all-to-all-start.1 = ((f32[512,4,128]{2,1,0:T(4,128)}), f32[512,4,128]{2,1,0:T(4,128)S(1)}, u32[]{:S(2)}, u32[]{:S(2)}) async-start(f32[512,4,128]{2,1,0:T(4,128)} %bitcast.4), calls=%async_computation.1 | async-start | bytes 2097152 | tf_op jit(solution)/shard_map/all_to_all | solution.py:338
  75.8 71.6 %copy-start = (f32[2,32,4096]{2,1,0:T(8,128)S(1)}, f32[2,32,4096]{2,1,0:T(8,128)}, u32[]{:S(2)}) copy-start(f32[2,32,4096]{2,1,0:T(8,128)} %obj.3) | copy-start | bytes 3145732
  114.3 16.7 %collective-permute-start.1 = (f32[2,8,4096]{2,1,0:T(8,128)S(1)}, f32[2,8,4096]{2,1,0:T(8,128)S(1)}, u32[]{:S(2)}, u32[]{:S(2)}) collective-permute-start(f32[2,8,4096]{2,1,0:T(8,128)S(1)} %rows_back.1.own), channel_id=1, source_target_pairs={{128,0},{256,128},{384,256},{0,384},{129,1},{257,129},{385,257},{1... | collective-permute-start | bytes 786440 | tf_op jit(solution)/shard_map/ppermute | solution.py:346
  117.5 17.9 %collective-permute-start = (f32[2,8,4096]{2,1,0:T(8,128)S(1)}, f32[2,8,4096]{2,1,0:T(8,128)S(1)}, u32[]{:S(2)}, u32[]{:S(2)}) collective-permute-start(f32[2,8,4096]{2,1,0:T(8,128)S(1)} %rows_back.1.own), channel_id=1, source_target_pairs={{0,128},{128,256},{256,384},{384,0},{1,129},{129,257},{257,385},{3... | collective-permute-start | bytes 786440 | tf_op jit(solution)/shard_map/ppermute | solution.py:345
  131.0 9.9 %collective-permute-start.3 = (f32[1,8,4096]{2,1,0:T(8,128)S(1)}, f32[1,8,4096]{2,1,0:T(8,128)S(1)}, u32[]{:S(2)}, u32[]{:S(2)}) collective-permute-start(f32[1,8,4096]{2,1,0:T(8,128)S(1)} %slice.9), channel_id=1, source_target_pairs={{128,0},{256,128},{384,256},{0,384},{129,1},{257,129},{385,257},{1... | collective-permute-start | bytes 393224 | tf_op jit(solution)/shard_map/ppermute | solution.py:348
  135.4 11.9 %collective-permute-start.2 = (f32[1,8,4096]{2,1,0:T(8,128)S(1)}, f32[1,8,4096]{2,1,0:T(8,128)S(1)}, u32[]{:S(2)}, u32[]{:S(2)}) collective-permute-start(f32[1,8,4096]{2,1,0:T(8,128)S(1)} %slice.8), channel_id=1, source_target_pairs={{0,128},{128,256},{256,384},{384,0},{1,129},{129,257},{257,385},{3... | collective-permute-start | bytes 393224 | tf_op jit(solution)/shard_map/ppermute | solution.py:347
Sparse Core Ops, SparseCore 0:
  28.0 84.1 all-gather.1

commit v2 on v1

--- a/solution.py
+++ b/solution.py
@@ -140,8 +140,14 @@
     return jnp.where(code >= 2, -a, a), jnp.where((code == 1) | (code == 2), -b, b)
 
 
-def rows_forward(obj, code, lh, ll, tw, out, mid, xs):
+def rows_forward(index, obj, code, lh, ll, tw, out, c0, c1, c2, c3, mid, xs):
     m = pl.program_id(0)
+    shift = lax.rem(m + MASKS - index[0], MASKS)
+    for s, c in enumerate((c0, c1, c2, c3)):
+
+        @pl.when(shift == s)
+        def _():
+            c[...] = code[0]
 
     def load(p):
         cols = slice(LANES * p, LANES * p + LANES)
@@ -230,8 +236,10 @@
                 ]
 
 
-def rows_back(rec, code, lh, ll, tw, out, mid, ys):
-    for l in range(MASKS):
+def rows_back(index, rec, c0, c1, c2, c3, lh, ll, tw, out_re, out_im, mid, ys):
+    out = (out_re, out_im)
+    for s, code in enumerate((c0, c1, c2, c3)):
+        l = lax.rem(index[0] + MASKS - s, MASKS)
         x = jnp.concatenate(
             [
                 jnp.concatenate(
@@ -253,19 +261,19 @@
 
         def store(p, v):
             cols = slice(LANES * p, LANES * p + LANES)
-            v = conj_code_times(code[l, :, cols], v)
+            v = conj_code_times(code[:, cols], v)
             for ri in range(2):
-                if l == 0:
-                    out[ri, :, cols] = v[ri]
-                elif l < MASKS - 1:
-                    out[ri, :, cols] += v[ri]
+                if s == 0:
+                    out[ri][:, cols] = v[ri]
+                elif s < MASKS - 1:
+                    out[ri][:, cols] += v[ri]
                 else:
-                    out[ri, :, cols] = (out[ri, :, cols] + v[ri]) * (1.0 / MASKS)
+                    out[ri][:, cols] = (out[ri][:, cols] + v[ri]) * (1.0 / MASKS)
 
         fft32(load, store, mid, 1)
 
 
-def finish(index, own, before, after, far_re, far_im, obj, updated, direction):
+def finish(index, own_re, own_im, b_re, b_im, a_re, a_im, far_re, far_im, obj, updated, direction):
     me = index[0]
 
     def put(shift, ri, value):
@@ -273,12 +281,14 @@
         direction[ri, rows, :] = value
         updated[ri, rows, :] = obj[ri, rows, :] - step_size * value
 
-    for ri in range(2):
-        put(0, ri, own[ri])
-        put(3, ri, before[ri])
-        put(1, ri, after[ri])
-    put(2, 0, far_re[0])
-    put(2, 1, far_im[0])
+    put(0, 0, own_re[...])
+    put(0, 1, own_im[...])
+    put(3, 0, b_re[...])
+    put(3, 1, b_im[...])
+    put(1, 0, a_re[...])
+    put(1, 1, a_im[...])
+    put(2, 0, far_re[...])
+    put(2, 1, far_im[...])
 
 
 VM = pl.BlockSpec(memory_space=pltpu.VMEM)
@@ -306,29 +316,30 @@
     t = {k: jnp.asarray(v) for k, v in tables().items()}
     sds = jax.ShapeDtypeStruct
     index = lax.axis_index("mask").astype(jnp.int32).reshape(1)
-    every = lax.all_gather(phases, "mask", axis=0, tiled=True)
-    codes = lax.dynamic_slice_in_dim(every, index[0] * OCT, OCT, axis=1)
     octet = lambda m: (0, m, 0)
-    sent = pl.pallas_call(
+    flat = lambda m: (0, 0)
+    rows8 = sds((OCT, N), jnp.int32)
+    sent, c0, c1, c2, c3 = pl.pallas_call(
         rows_forward,
         name="rows_forward",
-        out_shape=sds((2048, LANES), F32),
+        out_shape=(sds((2048, LANES), F32),) + (rows8,) * MASKS,
         grid=(MASKS,),
         in_specs=[
+            pl.BlockSpec(memory_space=pltpu.SMEM),
             pl.BlockSpec((2, OCT, N), octet),
             pl.BlockSpec((1, OCT, N), octet),
-            pl.BlockSpec((256, 256), lambda m: (0, 0)),
-            pl.BlockSpec((256, 256), lambda m: (0, 0)),
+            pl.BlockSpec((256, 256), flat),
+            pl.BlockSpec((256, 256), flat),
             pl.BlockSpec((2, SHORT, LANES), lambda m: (0, 0, 0)),
         ],
-        out_specs=pl.BlockSpec((2048, LANES), lambda m: (0, 0)),
+        out_specs=(pl.BlockSpec((2048, LANES), flat),) + (pl.BlockSpec((OCT, N), flat),) * MASKS,
         scratch_shapes=[
             pltpu.VMEM((2, SHORT, OCT, LANES), F32),
             pltpu.VMEM((256, 256), F32),
         ],
         compiler_params=pltpu.CompilerParams(vmem_limit_bytes=60 << 20),
         cost_estimate=pl.CostEstimate(flops=1 << 29, bytes_accessed=3 << 20, transcendentals=0),
-    )(object_field, phases, t["lh"], t["ll"], t["row_tw"])
+    )(index, object_field, phases, t["lh"], t["ll"], t["row_tw"])
     inten = intensity.reshape(2, 16, 8, 4, LANES).transpose(3, 0, 4, 1, 2).reshape(4, 256, LANES)
     rec = lax.all_to_all(sent.reshape(LANES, 16, LANES), "rows", 0, 0, tiled=True)
     back = call(
@@ -336,19 +347,25 @@
         [pltpu.VMEM((4, 2, 2, LANES, LANES), F32)], 3 << 29,
     )(rec.reshape(2048, LANES), inten, t["lh"], t["ll"], t["ih"], t["il"], t["mh"], t["ml"], t["col_tw"])
     rec = lax.all_to_all(back.reshape(512, 4, LANES), ("mask", "rows"), 0, 0, tiled=True)
-    part = call(
-        rows_back, "rows_back", sds((2, OCT, N), F32), 5,
-        [pltpu.VMEM((2, SHORT, OCT, LANES), F32), pltpu.VMEM((256, 256), F32)], 1 << 29,
-    )(rec.reshape(2048, LANES), codes, t["lh"], t["ll"], t["row_tw"])
     up = [(i, (i + 1) % MASKS) for i in range(MASKS)]
     down = [((i + 1) % MASKS, i) for i in range(MASKS)]
-    before = lax.ppermute(part, "mask", up)
-    after = lax.ppermute(part, "mask", down)
-    far_re = lax.ppermute(before[:1], "mask", up)
-    far_im = lax.ppermute(after[1:], "mask", down)
+    across = [(i, (i + 2) % MASKS) for i in range(MASKS)]
+    g1 = lax.ppermute(c1, "mask", up)
+    g2 = lax.ppermute(c2, "mask", across)
+    g3 = lax.ppermute(c3, "mask", down)
+    own_re, own_im = call(
+        rows_back, "rows_back", (sds((OCT, N), F32),) * 2, 9,
+        [pltpu.VMEM((2, SHORT, OCT, LANES), F32), pltpu.VMEM((256, 256), F32)], 1 << 29, smem=(0,),
+    )(index, rec.reshape(2048, LANES), c0, g1, g2, g3, t["lh"], t["ll"], t["row_tw"])
+    b_re = lax.ppermute(own_re, "mask", up)
+    a_im = lax.ppermute(own_im, "mask", down)
+    b_im = lax.ppermute(own_im, "mask", up)
+    a_re = lax.ppermute(own_re, "mask", down)
+    far_re = lax.ppermute(b_re, "mask", up)
+    far_im = lax.ppermute(a_im, "mask", down)
     whole = sds((2, SHORT, N), F32)
-    return call(finish, "finish", (whole, whole), 7, [], 1 << 20, smem=(0,))(
-        index, part, before, after, far_re, far_im, object_field
+    return call(finish, "finish", (whole, whole), 10, [], 1 << 20, smem=(0,))(
+        index, own_re, own_im, b_re, b_im, a_re, a_im, far_re, far_im, object_field
     )
 
 

time: 156 us -> 139 us (0.89)
  the two profiles are of different devices: /device:TPU:2 before, /device:TPU:1 now
where the time goes in v2:
time: 139 us; the launch traced here: 138 us
  starting transfers between devices  69.9 us (50%)
  waiting for transfers between devices  52.3 us (38%)
  Pallas kernels  10.9 us (8%)
  local copies, waits for them, and re-layouts  4.25 us (3%)
    all_to_all x1, waiting for transfers between devices, body(): lax.all_to_all(sent.reshape(LANES, 16, LANES), 'rows', 0, 0, tiled=True)  25.4 us
    all_to_all x1, starting transfers between devices, body(): lax.all_to_all(back.reshape(512, 4, LANES), ('mask', 'rows'), 0, 0, tiled...  16.6 us
    ppermute x1, waiting for transfers between devices, body(): g1 = lax.ppermute(c1, 'mask', up)  14.6 us
    all_to_all x1, starting transfers between devices, body(): lax.all_to_all(sent.reshape(LANES, 16, LANES), 'rows', 0, 0, tiled=True)  14.4 us
    ppermute x1, starting transfers between devices, body(): g2 = lax.ppermute(c2, 'mask', across)  7.36 us
    ppermute x1, waiting for transfers between devices, body(): g2 = lax.ppermute(c2, 'mask', across)  7.24 us
    ppermute x1, starting transfers between devices, body(): far_im = lax.ppermute(a_im, 'mask', down)  5.47 us
    ppermute x1, starting transfers between devices, body(): a_re = lax.ppermute(own_re, 'mask', down)  5.47 us
  transfers between devices with their start and end apart: 11, of which 5 were waited for; matrix products, arithmetic and copies ran while one was open for 2% of the time, Pallas kernels for 0%

profile of v2, /device:TPU:1, one launch (start us, length us, event | category | flops | bytes accessed | tf_op | source)
XLA Modules:
  0.0 138.2 jit_solution(5997270806606345851)
XLA Ops:
  0.6 4.6 %rows_forward.1 = (f32[2048,128]{1,0:T(8,128)}, s32[8,4096]{1,0:T(8,128)}, s32[8,4096]{1,0:T(8,128)}, s32[8,4096]{1,0:T(8,128)}, s32[8,4096]{1,0:T(8,128)}) custom-call(s32[1]{0:T(128)} %bitcast.index, f32[2,32,4096]{2,1,0:T(8,128)} %obj.3, s32[1,32,4096]{2,1,0:T(8,128)} %code.1, bf16[256,256]{1,0:T(8,128)(2,1)} %constant.22.clone.lh, ...), custom_call_target="tpu_custom_call" | custom-call | flops 536870912 | bytes 3145728 | tf_op jit(solution)/shard_map/rows_forward/pallas_call | solution.py:322
  5.3 0.0 copy-start.10
  5.3 14.4 %all-to-all-start = ((f32[128,16,128]{2,1,0:T(8,128)}), f32[128,16,128]{2,1,0:T(8,128)S(1)}, u32[]{:S(2)}, u32[]{:S(2)}) async-start(f32[128,16,128]{2,1,0:T(8,128)} %bitcast.13), calls=%async_computation | async-start | bytes 2097152 | tf_op jit(solution)/shard_map/all_to_all | solution.py:344
  19.6 0.0 copy-done.10
  19.6 0.4 reshape.28
  20.0 0.4 copy.17
  20.4 0.0 copy-start.3
  20.4 0.0 copy-start.4
  20.4 0.0 copy-start.5
  20.5 0.0 copy-start.6
  20.5 1.2 reshape.29
  21.7 1.3 copy.15.inten
  23.0 25.4 %all-to-all-done = f32[128,16,128]{2,1,0:T(8,128)S(1)} async-done(((f32[128,16,128]{2,1,0:T(8,128)}), f32[128,16,128]{2,1,0:T(8,128)S(1)}, u32[]{:S(2)}, u32[]{:S(2)}) %all-to-all-start) | async-done | bytes 1048608 | tf_op jit(solution)/shard_map/all_to_all | solution.py:344
  48.4 0.0 copy-done.3
  48.4 0.0 copy-done.4
  48.4 0.0 copy-done.5
  48.4 0.0 copy-done.6
  48.5 0.0 copy-done.1
  48.5 0.0 copy-done.2
  48.5 0.0 copy-start.7
  48.5 0.9 copy-done.7
  49.4 3.8 %columns.1 = f32[2048,128]{1,0:T(8,128)} custom-call(f32[2048,128]{1,0:T(8,128)S(1)} %bitcast.11, f32[4,256,128]{2,1,0:T(8,128)S(1)} %copy.15.inten, bf16[256,256]{1,0:T(8,128)(2,1)S(1)} %copy-done.4, bf16[256,256]{1,0:T(8,128)(2,1)S(1)} %copy-done.5, bf16[256,256]{1,0:T(8,128)(2,1)S(1)} %copy-done.6, bf16[256,256]{1,0:T(8,128)(2,1)S(1)} %copy-done.7, ...), custom_call_target="tpu_custom_call" | custom-call | flops 1610612736 | bytes 3145728 | tf_op jit(solution)/shard_map/columns/pallas_call | solution.py:345
  53.1 0.0 copy-start.9
  53.2 16.6 %all-to-all-start.1 = ((f32[512,4,128]{2,1,0:T(4,128)}), f32[512,4,128]{2,1,0:T(4,128)S(1)}, u32[]{:S(2)}, u32[]{:S(2)}) async-start(f32[512,4,128]{2,1,0:T(4,128)} %bitcast.4), calls=%async_computation.1 | async-start | bytes 2097152 | tf_op jit(solution)/shard_map/all_to_all | solution.py:349
  69.8 0.0 copy-start
  69.8 0.0 copy-done.13
  69.8 5.3 %collective-permute-start = (s32[8,4096]{1,0:T(8,128)S(1)}, s32[8,4096]{1,0:T(8,128)S(1)}, u32[]{:S(2)}, u32[]{:S(2)}) collective-permute-start(s32[8,4096]{1,0:T(8,128)S(1)} %copy-done.13), channel_id=1, source_target_pairs={{0,128},{128,256},{256,384},{384,0},{1,129},{129,257},{257,385},{3... | collective-permute-start | bytes 393224 | tf_op jit(solution)/shard_map/ppermute | solution.py:353
  75.1 7.4 %collective-permute-start.1 = (s32[8,4096]{1,0:T(8,128)S(1)}, s32[8,4096]{1,0:T(8,128)S(1)}, u32[]{:S(2)}, u32[]{:S(2)}) collective-permute-start(s32[8,4096]{1,0:T(8,128)S(1)} %copy-done.12), channel_id=1, source_target_pairs={{0,256},{128,384},{256,0},{384,128},{1,257},{129,385},{257,1},{385... | collective-permute-start | bytes 393224 | tf_op jit(solution)/shard_map/ppermute | solution.py:354
  82.4 4.1 %collective-permute-start.2 = (s32[8,4096]{1,0:T(8,128)S(1)}, s32[8,4096]{1,0:T(8,128)S(1)}, u32[]{:S(2)}, u32[]{:S(2)}) collective-permute-start(s32[8,4096]{1,0:T(8,128)S(1)} %copy-done.11), channel_id=1, source_target_pairs={{128,0},{256,128},{384,256},{0,384},{129,1},{257,129},{385,257},{1... | collective-permute-start | bytes 393224 | tf_op jit(solution)/shard_map/ppermute | solution.py:355
  86.6 14.6 %collective-permute-done.c1 = s32[8,4096]{1,0:T(8,128)S(1)} collective-permute-done((s32[8,4096]{1,0:T(8,128)S(1)}, s32[8,4096]{1,0:T(8,128)S(1)}, u32[]{:S(2)}, u32[]{:S(2)}) %collective-permute-start) | collective-permute-done | bytes 131104 | tf_op jit(solution)/shard_map/ppermute | solution.py:353
  101.2 7.2 %collective-permute-done.1.c2 = s32[8,4096]{1,0:T(8,128)S(1)} collective-permute-done((s32[8,4096]{1,0:T(8,128)S(1)}, s32[8,4096]{1,0:T(8,128)S(1)}, u32[]{:S(2)}, u32[]{:S(2)}) %collective-permute-start.1) | collective-permute-done | bytes 131104 | tf_op jit(solution)/shard_map/ppermute | solution.py:354
  108.4 0.0 collective-permute-done.2.c3
  108.5 0.0 all-to-all-done.1
  108.5 1.0 rows_back.1
  109.5 3.1 %collective-permute-start.3 = (f32[8,4096]{1,0:T(8,128)S(1)}, f32[8,4096]{1,0:T(8,128)S(1)}, u32[]{:S(2)}, u32[]{:S(2)}) collective-permute-start(f32[8,4096]{1,0:T(8,128)S(1)} %get-tuple-element.14.own_re), channel_id=1, source_target_pairs={{0,128},{128,256},{256,384},{384,0},{1,129},{129,257},{257,385},{3... | collective-permute-start | bytes 393224 | tf_op jit(solution)/shard_map/ppermute | solution.py:360
  112.6 4.3 %collective-permute-start.6 = (f32[8,4096]{1,0:T(8,128)S(1)}, f32[8,4096]{1,0:T(8,128)S(1)}, u32[]{:S(2)}, u32[]{:S(2)}) collective-permute-start(f32[8,4096]{1,0:T(8,128)S(1)} %get-tuple-element.15.own_im), channel_id=1, source_target_pairs={{128,0},{256,128},{384,256},{0,384},{129,1},{257,129},{385,257},{1... | collective-permute-start | bytes 393224 | tf_op jit(solution)/shard_map/ppermute | solution.py:361
  116.9 1.9 %collective-permute-start.4 = (f32[8,4096]{1,0:T(8,128)S(1)}, f32[8,4096]{1,0:T(8,128)S(1)}, u32[]{:S(2)}, u32[]{:S(2)}) collective-permute-start(f32[8,4096]{1,0:T(8,128)S(1)} %get-tuple-element.15.own_im), channel_id=1, source_target_pairs={{0,128},{128,256},{256,384},{384,0},{1,129},{129,257},{257,385},{3... | collective-permute-start | bytes 393224 | tf_op jit(solution)/shard_map/ppermute | solution.py:362
  118.8 5.5 %collective-permute-start.5 = (f32[8,4096]{1,0:T(8,128)S(1)}, f32[8,4096]{1,0:T(8,128)S(1)}, u32[]{:S(2)}, u32[]{:S(2)}) collective-permute-start(f32[8,4096]{1,0:T(8,128)S(1)} %get-tuple-element.14.own_re), channel_id=1, source_target_pairs={{128,0},{256,128},{384,256},{0,384},{129,1},{257,129},{385,257},{1... | collective-permute-start | bytes 393224 | tf_op jit(solution)/shard_map/ppermute | solution.py:363
  124.3 0.0 collective-permute-done.3.b_re
  124.3 1.9 %collective-permute-start.7 = (f32[8,4096]{1,0:T(8,128)S(1)}, f32[8,4096]{1,0:T(8,128)S(1)}, u32[]{:S(2)}, u32[]{:S(2)}) collective-permute-start(f32[8,4096]{1,0:T(8,128)S(1)} %collective-permute-done.3.b_re), channel_id=1, source_target_pairs={{0,128},{128,256},{256,384},{384,0},{1,129},{129,257},{257,385},{3... | collective-permute-start | bytes 393224 | tf_op jit(solution)/shard_map/ppermute | solution.py:364
  126.2 0.0 collective-permute-done.6.a_im
  126.3 5.5 %collective-permute-start.8 = (f32[8,4096]{1,0:T(8,128)S(1)}, f32[8,4096]{1,0:T(8,128)S(1)}, u32[]{:S(2)}, u32[]{:S(2)}) collective-permute-start(f32[8,4096]{1,0:T(8,128)S(1)} %collective-permute-done.6.a_im), channel_id=1, source_target_pairs={{128,0},{256,128},{384,256},{0,384},{129,1},{257,129},{385,257},{1... | collective-permute-start | bytes 393224 | tf_op jit(solution)/shard_map/ppermute | solution.py:365
  131.7 0.0 collective-permute-done.4.b_im
  131.7 0.0 collective-permute-done.5.a_re
  131.8 3.1 %collective-permute-done.7.far_re = f32[8,4096]{1,0:T(8,128)S(1)} collective-permute-done((f32[8,4096]{1,0:T(8,128)S(1)}, f32[8,4096]{1,0:T(8,128)S(1)}, u32[]{:S(2)}, u32[]{:S(2)}) %collective-permute-start.7) | collective-permute-done | bytes 131104 | tf_op jit(solution)/shard_map/ppermute | solution.py:364
  134.8 1.9 %collective-permute-done.8.far_im = f32[8,4096]{1,0:T(8,128)S(1)} collective-permute-done((f32[8,4096]{1,0:T(8,128)S(1)}, f32[8,4096]{1,0:T(8,128)S(1)}, u32[]{:S(2)}, u32[]{:S(2)}) %collective-permute-start.8) | collective-permute-done | bytes 131104 | tf_op jit(solution)/shard_map/ppermute | solution.py:365
  136.7 0.0 copy-done
  136.7 1.5 %finish.1 = (f32[2,32,4096]{2,1,0:T(8,128)}, f32[2,32,4096]{2,1,0:T(8,128)}) custom-call(s32[1]{0:T(128)} %bitcast.index, f32[8,4096]{1,0:T(8,128)S(1)} %get-tuple-element.14.own_re, f32[8,4096]{1,0:T(8,128)S(1)} %get-tuple-element.15.own_im, f32[8,4096]{1,0:T(8,128)S(1)} %collective-permute-done.3.b_re, f32[8,4096]{1,0:T(8,128)S(1)} %collective-permute-done.4.b_im, ...), custom_call_target="tpu_custom_call" | custom-call | flops 1048576 | bytes 3145728 | tf_op jit(solution)/shard_map/finish/pallas_call | solution.py:367
  (10 shorter events, 0.0 us)
Async XLA Ops:
  5.3 14.4 %copy-start.10 = (f32[1,32,4096]{2,1,0:T(8,128)S(1)}, f32[1,32,4096]{2,1,0:T(8,128)}, u32[]{:S(2)}) copy-start(f32[1,32,4096]{2,1,0:T(8,128)} %param.13) | copy-start | bytes 1572868
  5.3 43.2 %all-to-all-start = ((f32[128,16,128]{2,1,0:T(8,128)}), f32[128,16,128]{2,1,0:T(8,128)S(1)}, u32[]{:S(2)}, u32[]{:S(2)}) async-start(f32[128,16,128]{2,1,0:T(8,128)} %bitcast.13), calls=%async_computation | async-start | bytes 2097152 | tf_op jit(solution)/shard_map/all_to_all | solution.py:344
  20.4 28.0 %copy-start.3 = (f32[2,4,128,128]{3,2,1,0:T(8,128)S(1)}, f32[2,4,128,128]{3,2,1,0:T(8,128)}, u32[]{:S(2)}) copy-start(f32[2,4,128,128]{3,2,1,0:T(8,128)} %constant.29.clone.tw) | copy-start | bytes 1572868
  20.4 28.0 %copy-start.4 = (bf16[256,256]{1,0:T(8,128)(2,1)S(1)}, bf16[256,256]{1,0:T(8,128)(2,1)}, u32[]{:S(2)}) copy-start(bf16[256,256]{1,0:T(8,128)(2,1)} %constant.22.clone.lh) | copy-start | bytes 393220
  20.4 28.0 %copy-start.5 = (bf16[256,256]{1,0:T(8,128)(2,1)S(1)}, bf16[256,256]{1,0:T(8,128)(2,1)}, u32[]{:S(2)}) copy-start(bf16[256,256]{1,0:T(8,128)(2,1)} %constant.23.clone.ll) | copy-start | bytes 393220
  20.5 28.0 %copy-start.6 = (bf16[256,256]{1,0:T(8,128)(2,1)S(1)}, bf16[256,256]{1,0:T(8,128)(2,1)}, u32[]{:S(2)}) copy-start(bf16[256,256]{1,0:T(8,128)(2,1)} %constant.24.clone.ih) | copy-start | bytes 393220
  21.7 26.8 %copy-start.1 = (bf16[4,256,256]{2,1,0:T(8,128)(2,1)S(1)}, bf16[4,256,256]{2,1,0:T(8,128)(2,1)}, u32[]{:S(2)}) copy-start(bf16[4,256,256]{2,1,0:T(8,128)(2,1)} %constant.26.clone.mh) | copy-start | bytes 1572868
  21.7 26.8 %copy-start.2 = (bf16[4,256,256]{2,1,0:T(8,128)(2,1)S(1)}, bf16[4,256,256]{2,1,0:T(8,128)(2,1)}, u32[]{:S(2)}) copy-start(bf16[4,256,256]{2,1,0:T(8,128)(2,1)} %constant.27.clone.ml) | copy-start | bytes 1572868
  48.5 0.9 copy-start.7
  53.1 16.6 %copy-start.13 = (s32[8,4096]{1,0:T(8,128)S(1)}, s32[8,4096]{1,0:T(8,128)}, u32[]{:S(2)}) copy-start(s32[8,4096]{1,0:T(8,128)} %get-tuple-element.11) | copy-start | bytes 393220
  53.1 21.9 %copy-start.12 = (s32[8,4096]{1,0:T(8,128)S(1)}, s32[8,4096]{1,0:T(8,128)}, u32[]{:S(2)}) copy-start(s32[8,4096]{1,0:T(8,128)} %get-tuple-element.12) | copy-start | bytes 393220
  53.1 29.3 %copy-start.11 = (s32[8,4096]{1,0:T(8,128)S(1)}, s32[8,4096]{1,0:T(8,128)}, u32[]{:S(2)}) copy-start(s32[8,4096]{1,0:T(8,128)} %get-tuple-element.13) | copy-start | bytes 393220
  53.1 55.3 %copy-start.8 = (f32[2,32,128]{2,1,0:T(8,128)S(1)}, f32[2,32,128]{2,1,0:T(8,128)}, u32[]{:S(2)}) copy-start(f32[2,32,128]{2,1,0:T(8,128)} %constant.28.clone.tw) | copy-start | bytes 98308
  53.1 55.3 %copy-start.9 = (s32[8,4096]{1,0:T(8,128)S(1)}, s32[8,4096]{1,0:T(8,128)}, u32[]{:S(2)}) copy-start(s32[8,4096]{1,0:T(8,128)} %get-tuple-element.10.c0) | copy-start | bytes 393220
  53.2 55.3 %all-to-all-start.1 = ((f32[512,4,128]{2,1,0:T(4,128)}), f32[512,4,128]{2,1,0:T(4,128)S(1)}, u32[]{:S(2)}, u32[]{:S(2)}) async-start(f32[512,4,128]{2,1,0:T(4,128)} %bitcast.4), calls=%async_computation.1 | async-start | bytes 2097152 | tf_op jit(solution)/shard_map/all_to_all | solution.py:349
  69.8 67.0 %copy-start = (f32[2,32,4096]{2,1,0:T(8,128)S(1)}, f32[2,32,4096]{2,1,0:T(8,128)}, u32[]{:S(2)}) copy-start(f32[2,32,4096]{2,1,0:T(8,128)} %obj.3) | copy-start | bytes 3145732
  69.8 31.4 %collective-permute-start = (s32[8,4096]{1,0:T(8,128)S(1)}, s32[8,4096]{1,0:T(8,128)S(1)}, u32[]{:S(2)}, u32[]{:S(2)}) collective-permute-start(s32[8,4096]{1,0:T(8,128)S(1)} %copy-done.13), channel_id=1, source_target_pairs={{0,128},{128,256},{256,384},{384,0},{1,129},{129,257},{257,385},{3... | collective-permute-start | bytes 393224 | tf_op jit(solution)/shard_map/ppermute | solution.py:353
  75.1 33.4 %collective-permute-start.1 = (s32[8,4096]{1,0:T(8,128)S(1)}, s32[8,4096]{1,0:T(8,128)S(1)}, u32[]{:S(2)}, u32[]{:S(2)}) collective-permute-start(s32[8,4096]{1,0:T(8,128)S(1)} %copy-done.12), channel_id=1, source_target_pairs={{0,256},{128,384},{256,0},{384,128},{1,257},{129,385},{257,1},{385... | collective-permute-start | bytes 393224 | tf_op jit(solution)/shard_map/ppermute | solution.py:354
  82.4 26.0 %collective-permute-start.2 = (s32[8,4096]{1,0:T(8,128)S(1)}, s32[8,4096]{1,0:T(8,128)S(1)}, u32[]{:S(2)}, u32[]{:S(2)}) collective-permute-start(s32[8,4096]{1,0:T(8,128)S(1)} %copy-done.11), channel_id=1, source_target_pairs={{128,0},{256,128},{384,256},{0,384},{129,1},{257,129},{385,257},{1... | collective-permute-start | bytes 393224 | tf_op jit(solution)/shard_map/ppermute | solution.py:355
  109.5 14.8 %collective-permute-start.3 = (f32[8,4096]{1,0:T(8,128)S(1)}, f32[8,4096]{1,0:T(8,128)S(1)}, u32[]{:S(2)}, u32[]{:S(2)}) collective-permute-start(f32[8,4096]{1,0:T(8,128)S(1)} %get-tuple-element.14.own_re), channel_id=1, source_target_pairs={{0,128},{128,256},{256,384},{384,0},{1,129},{129,257},{257,385},{3... | collective-permute-start | bytes 393224 | tf_op jit(solution)/shard_map/ppermute | solution.py:360
  112.6 13.6 %collective-permute-start.6 = (f32[8,4096]{1,0:T(8,128)S(1)}, f32[8,4096]{1,0:T(8,128)S(1)}, u32[]{:S(2)}, u32[]{:S(2)}) collective-permute-start(f32[8,4096]{1,0:T(8,128)S(1)} %get-tuple-element.15.own_im), channel_id=1, source_target_pairs={{128,0},{256,128},{384,256},{0,384},{129,1},{257,129},{385,257},{1... | collective-permute-start | bytes 393224 | tf_op jit(solution)/shard_map/ppermute | solution.py:361
  116.9 14.8 %collective-permute-start.4 = (f32[8,4096]{1,0:T(8,128)S(1)}, f32[8,4096]{1,0:T(8,128)S(1)}, u32[]{:S(2)}, u32[]{:S(2)}) collective-permute-start(f32[8,4096]{1,0:T(8,128)S(1)} %get-tuple-element.15.own_im), channel_id=1, source_target_pairs={{0,128},{128,256},{256,384},{384,0},{1,129},{129,257},{257,385},{3... | collective-permute-start | bytes 393224 | tf_op jit(solution)/shard_map/ppermute | solution.py:362
  118.8 12.9 %collective-permute-start.5 = (f32[8,4096]{1,0:T(8,128)S(1)}, f32[8,4096]{1,0:T(8,128)S(1)}, u32[]{:S(2)}, u32[]{:S(2)}) collective-permute-start(f32[8,4096]{1,0:T(8,128)S(1)} %get-tuple-element.14.own_re), channel_id=1, source_target_pairs={{128,0},{256,128},{384,256},{0,384},{129,1},{257,129},{385,257},{1... | collective-permute-start | bytes 393224 | tf_op jit(solution)/shard_map/ppermute | solution.py:363
  124.3 10.5 %collective-permute-start.7 = (f32[8,4096]{1,0:T(8,128)S(1)}, f32[8,4096]{1,0:T(8,128)S(1)}, u32[]{:S(2)}, u32[]{:S(2)}) collective-permute-start(f32[8,4096]{1,0:T(8,128)S(1)} %collective-permute-done.3.b_re), channel_id=1, source_target_pairs={{0,128},{128,256},{256,384},{384,0},{1,129},{129,257},{257,385},{3... | collective-permute-start | bytes 393224 | tf_op jit(solution)/shard_map/ppermute | solution.py:364
  126.3 10.5 %collective-permute-start.8 = (f32[8,4096]{1,0:T(8,128)S(1)}, f32[8,4096]{1,0:T(8,128)S(1)}, u32[]{:S(2)}, u32[]{:S(2)}) collective-permute-start(f32[8,4096]{1,0:T(8,128)S(1)} %collective-permute-done.6.a_im), channel_id=1, source_target_pairs={{128,0},{256,128},{384,256},{0,384},{129,1},{257,129},{385,257},{1... | collective-permute-start | bytes 393224 | tf_op jit(solution)/shard_map/ppermute | solution.py:365

commit v3 on v2

--- a/solution.py
+++ b/solution.py
@@ -21,7 +21,7 @@
 def _split(table):
     high = table.astype(np.float32).astype(ml_dtypes.bfloat16)
     low = (table - high.astype(np.float64)).astype(np.float32).astype(ml_dtypes.bfloat16)
-    return high, low
+    return np.stack([high, low])
 
 
 @functools.lru_cache(maxsize=None)
@@ -41,10 +41,8 @@
         small = np.exp(-2j * math.pi * np.outer(r8, r8) / 8 - 2j * math.pi * r8[:, None] * e / 32)
         big = np.kron(np.eye(16), small)
         blocks.append(np.block([[big.real, big.imag], [-big.imag, big.real]]))
-    lh, ll = _split(left)
-    ih, il = _split(left.T)
-    mh, ml = _split(np.stack(blocks))
-    return dict(lh=lh, ll=ll, ih=ih, il=il, mh=mh, ml=ml, row_tw=row_tw, col_tw=col_tw)
+    both = np.concatenate([_split(left), _split(left.T)])
+    return dict(left=_split(left), both=both, block=_split(np.stack(blocks)), row_tw=row_tw, col_tw=col_tw)
 
 
 def split(x):
@@ -140,7 +138,7 @@
     return jnp.where(code >= 2, -a, a), jnp.where((code == 1) | (code == 2), -b, b)
 
 
-def rows_forward(index, obj, code, lh, ll, tw, out, c0, c1, c2, c3, mid, xs):
+def rows_forward(index, obj, code, left, tw, out, c0, c1, c2, c3, mid, xs):
     m = pl.program_id(0)
     shift = lax.rem(m + MASKS - index[0], MASKS)
     for s, c in enumerate((c0, c1, c2, c3)):
@@ -159,7 +157,7 @@
         xs[OCT * k : OCT * k + OCT, LANES:] = v[1]
 
     fft32(load, store, mid, -1)
-    y = dot3((lh[...], ll[...]), split(xs[...]), NT)
+    y = dot3((left[0], left[1]), split(xs[...]), NT)
     for ri in range(2):
         for h in range(2):
             out[pl.ds(ri * 8 + 2 * m + h, LANES, stride=16), :] = y[
@@ -167,7 +165,7 @@
             ]
 
 
-def columns(rec, inten, lh, ll, ih, il, mh, ml, tw, out, s):
+def columns(rec, inten, both, block, tw, out, s):
     for m in range(MASKS):
         x = jnp.concatenate(
             [
@@ -178,7 +176,7 @@
             ],
             axis=0,
         )
-        y = dot3((lh[...], ll[...]), split(x), NN)
+        y = dot3((both[0], both[1]), split(x), NN)
         t = (tw[0, m], tw[1, m])
         for h in range(2):
             cols = slice(LANES * h, LANES * h + LANES)
@@ -201,7 +199,7 @@
         x = jnp.concatenate(
             [jnp.concatenate([s[e, 0, h], s[e, 1, h]], axis=1) for h in range(2)], axis=0
         )
-        table = (mh[e], ml[e])
+        table = (block[0, e], block[1, e])
         y = dot3(split(x), table, NN)
         wr, wi = y[:, :LANES], y[:, LANES:]
         weight = wr * wr + wi * wi - inten[e]
@@ -228,7 +226,7 @@
         x = jnp.concatenate(
             [jnp.concatenate([s[m, ri, 0], s[m, ri, 1]], axis=1) for ri in range(2)], axis=0
         )
-        y = dot3((ih[...], il[...]), split(x), NN)
+        y = dot3((both[2], both[3]), split(x), NN)
         for ri in range(2):
             for h in range(2):
                 out[pl.ds(m * 512 + ri * 2 + h, LANES, stride=4), :] = y[
@@ -236,7 +234,7 @@
                 ]
 
 
-def rows_back(index, rec, c0, c1, c2, c3, lh, ll, tw, out_re, out_im, mid, ys):
+def rows_back(index, rec, c0, c1, c2, c3, left, tw, out_re, out_im, mid, ys):
     out = (out_re, out_im)
     for s, code in enumerate((c0, c1, c2, c3)):
         l = lax.rem(index[0] + MASKS - s, MASKS)
@@ -253,7 +251,7 @@
             ],
             axis=0,
         )
-        ys[...] = dot3(split(x), (lh[...], ll[...]), NN)
+        ys[...] = dot3(split(x), (left[0], left[1]), NN)
 
         def load(k):
             rows = slice(OCT * k, OCT * k + OCT)
@@ -328,8 +326,7 @@
             pl.BlockSpec(memory_space=pltpu.SMEM),
             pl.BlockSpec((2, OCT, N), octet),
             pl.BlockSpec((1, OCT, N), octet),
-            pl.BlockSpec((256, 256), flat),
-            pl.BlockSpec((256, 256), flat),
+            pl.BlockSpec((2, 256, 256), lambda m: (0, 0, 0)),
             pl.BlockSpec((2, SHORT, LANES), lambda m: (0, 0, 0)),
         ],
         out_specs=(pl.BlockSpec((2048, LANES), flat),) + (pl.BlockSpec((OCT, N), flat),) * MASKS,
@@ -339,24 +336,25 @@
         ],
         compiler_params=pltpu.CompilerParams(vmem_limit_bytes=60 << 20),
         cost_estimate=pl.CostEstimate(flops=1 << 29, bytes_accessed=3 << 20, transcendentals=0),
-    )(index, object_field, phases, t["lh"], t["ll"], t["row_tw"])
+    )(index, object_field, phases, t["left"], t["row_tw"])
     inten = intensity.reshape(2, 16, 8, 4, LANES).transpose(3, 0, 4, 1, 2).reshape(4, 256, LANES)
-    rec = lax.all_to_all(sent.reshape(LANES, 16, LANES), "rows", 0, 0, tiled=True)
-    back = call(
-        columns, "columns", sds((2048, LANES), F32), 9,
-        [pltpu.VMEM((4, 2, 2, LANES, LANES), F32)], 3 << 29,
-    )(rec.reshape(2048, LANES), inten, t["lh"], t["ll"], t["ih"], t["il"], t["mh"], t["ml"], t["col_tw"])
-    rec = lax.all_to_all(back.reshape(512, 4, LANES), ("mask", "rows"), 0, 0, tiled=True)
     up = [(i, (i + 1) % MASKS) for i in range(MASKS)]
     down = [((i + 1) % MASKS, i) for i in range(MASKS)]
     across = [(i, (i + 2) % MASKS) for i in range(MASKS)]
+    rec = lax.all_to_all(sent.reshape(LANES, 16, LANES), "rows", 0, 0, tiled=True)
     g1 = lax.ppermute(c1, "mask", up)
     g2 = lax.ppermute(c2, "mask", across)
     g3 = lax.ppermute(c3, "mask", down)
+    rec, g1, g2, g3 = lax.optimization_barrier((rec, g1, g2, g3))
+    back = call(
+        columns, "columns", sds((2048, LANES), F32), 5,
+        [pltpu.VMEM((4, 2, 2, LANES, LANES), F32)], 3 << 29,
+    )(rec.reshape(2048, LANES), inten, t["both"], t["block"], t["col_tw"])
+    rec = lax.all_to_all(back.reshape(512, 4, LANES), ("mask", "rows"), 0, 0, tiled=True)
     own_re, own_im = call(
-        rows_back, "rows_back", (sds((OCT, N), F32),) * 2, 9,
+        rows_back, "rows_back", (sds((OCT, N), F32),) * 2, 8,
         [pltpu.VMEM((2, SHORT, OCT, LANES), F32), pltpu.VMEM((256, 256), F32)], 1 << 29, smem=(0,),
-    )(index, rec.reshape(2048, LANES), c0, g1, g2, g3, t["lh"], t["ll"], t["row_tw"])
+    )(index, rec.reshape(2048, LANES), c0, g1, g2, g3, t["left"], t["row_tw"])
     b_re = lax.ppermute(own_re, "mask", up)
     a_im = lax.ppermute(own_im, "mask", down)
     b_im = lax.ppermute(own_im, "mask", up)

time: 139 us -> 135 us (0.971)
  blocking collectives: 0 us -> 53.5 us
  waiting for transfers between devices: 52.3 us -> 11.6 us
  starting transfers between devices: 69.9 us -> 53.7 us
    all_to_all x0 -> x1, blocking collectives: none -> 53.5 us  [body(): lax.all_to_all(back.reshape(512, 4, LANES), ('mask', 'rows'), 0, 0, tiled...]
    all_to_all x1, waiting for transfers between devices: 25.4 us -> 1.99 us  [body(): lax.all_to_all(sent.reshape(LANES, 16, LANES), 'rows', 0, 0, tiled=True)]
    all_to_all x1 -> x0, starting transfers between devices: 16.6 us -> none  [body(): lax.all_to_all(back.reshape(512, 4, LANES), ('mask', 'rows'), 0, 0, tiled...]
    ppermute x1, waiting for transfers between devices: 14.6 us -> 0.03 us  [body(): g1 = lax.ppermute(c1, 'mask', up)]
    ppermute x1, waiting for transfers between devices: 1.89 us -> 0.01 us  [body(): far_im = lax.ppermute(a_im, 'mask', down)]
  transfers between devices with their start and end apart: 11 -> 10, of which waited for: 5 -> 3; matrix products, arithmetic and copies ran while one was open for 2% -> 2% of each run, Pallas kernels for 0% -> 0%
where the time goes in v3:
time: 135 us; the launch traced here: 134 us
  starting transfers between devices  53.7 us (40%)
  blocking collectives  53.5 us (40%)
  waiting for transfers between devices  11.6 us (9%)
  Pallas kernels  9.91 us (7%)
  local copies, waits for them, and re-layouts  4.34 us (3%)
    all_to_all x1, blocking collectives, body(): lax.all_to_all(back.reshape(512, 4, LANES), ('mask', 'rows'), 0, 0, tiled...  53.5 us
    all_to_all x1, starting transfers between devices, body(): lax.all_to_all(sent.reshape(LANES, 16, LANES), 'rows', 0, 0, tiled=True)  14.4 us
    ppermute x1, starting transfers between devices, body(): g2 = lax.ppermute(c2, 'mask', across)  7.95 us
    ppermute x1, waiting for transfers between devices, body(): g2 = lax.ppermute(c2, 'mask', across)  6.33 us
    ppermute x1, starting transfers between devices, body(): g1 = lax.ppermute(c1, 'mask', up)  5.8 us
    ppermute x1, starting transfers between devices, body(): far_im = lax.ppermute(a_im, 'mask', down)  5.47 us
    ppermute x1, starting transfers between devices, body(): a_re = lax.ppermute(own_re, 'mask', down)  5.33 us
    pallas_call x1, Pallas kernels, body(): pl.pallas_call(rows_forward, name='rows_forward', out_shape=(sds((2048, L...  4.6 us
  transfers between devices with their start and end apart: 10, of which 3 were waited for; matrix products, arithmetic and copies ran while one was open for 2% of the time, Pallas kernels for 0%

profile of v3, /device:TPU:1, one launch (start us, length us, event | category | flops | bytes accessed | tf_op | source)
XLA Modules:
  0.0 133.8 jit_solution(11223031503501870145)
XLA Ops:
  0.6 4.6 %rows_forward.1 = (f32[2048,128]{1,0:T(8,128)}, s32[8,4096]{1,0:T(8,128)}, s32[8,4096]{1,0:T(8,128)}, s32[8,4096]{1,0:T(8,128)}, s32[8,4096]{1,0:T(8,128)}) custom-call(s32[1]{0:T(128)} %bitcast.index, f32[2,32,4096]{2,1,0:T(8,128)} %obj.3, s32[1,32,4096]{2,1,0:T(8,128)} %code.1, bf16[2,256,256]{2,1,0:T(8,128)(2,1)} %constant.16.clone.left, ...), custom_call_target="tpu_custom_call" | custom-call | flops 536870912 | bytes 3145728 | tf_op jit(solution)/shard_map/rows_forward/pallas_call | solution.py:320
  5.2 0.0 copy-start.7
  5.2 14.4 %all-to-all-start = ((f32[128,16,128]{2,1,0:T(8,128)}), f32[128,16,128]{2,1,0:T(8,128)S(1)}, u32[]{:S(2)}, u32[]{:S(2)}) async-start(f32[128,16,128]{2,1,0:T(8,128)} %bitcast.14), calls=%async_computation | async-start | bytes 2097152 | tf_op jit(solution)/shard_map/all_to_all | solution.py:344
  19.6 5.8 %collective-permute-start = (s32[8,4096]{1,0:T(8,128)}, s32[8,4096]{1,0:T(8,128)S(1)}, u32[]{:S(2)}, u32[]{:S(2)}) collective-permute-start(s32[8,4096]{1,0:T(8,128)} %get-tuple-element.14), channel_id=1, source_target_pairs={{0,128},{128,256},{256,384},{384,0},{1,129},{129,257},{257,385},{3... | collective-permute-start | bytes 393224 | tf_op jit(solution)/shard_map/ppermute | solution.py:345
  25.4 7.9 %collective-permute-start.1 = (s32[8,4096]{1,0:T(8,128)}, s32[8,4096]{1,0:T(8,128)S(1)}, u32[]{:S(2)}, u32[]{:S(2)}) collective-permute-start(s32[8,4096]{1,0:T(8,128)} %get-tuple-element.15), channel_id=1, source_target_pairs={{0,256},{128,384},{256,0},{384,128},{1,257},{129,385},{257,1},{385... | collective-permute-start | bytes 393224 | tf_op jit(solution)/shard_map/ppermute | solution.py:346
  33.4 3.4 %collective-permute-start.2 = (s32[8,4096]{1,0:T(8,128)}, s32[8,4096]{1,0:T(8,128)S(1)}, u32[]{:S(2)}, u32[]{:S(2)}) collective-permute-start(s32[8,4096]{1,0:T(8,128)} %get-tuple-element.16), channel_id=1, source_target_pairs={{128,0},{256,128},{384,256},{0,384},{129,1},{257,129},{385,257},{1... | collective-permute-start | bytes 393224 | tf_op jit(solution)/shard_map/ppermute | solution.py:347
  36.8 0.0 copy-done.7
  36.8 0.4 reshape.28
  37.1 0.4 copy.14
  37.5 0.0 copy-start.1
  37.6 1.2 reshape.29
  38.8 0.0 copy-start.2
  38.8 1.3 copy.12.inten
  40.1 0.0 collective-permute-done.c1
  40.1 6.3 %collective-permute-done.1.c2 = s32[8,4096]{1,0:T(8,128)S(1)} collective-permute-done((s32[8,4096]{1,0:T(8,128)}, s32[8,4096]{1,0:T(8,128)S(1)}, u32[]{:S(2)}, u32[]{:S(2)}) %collective-permute-start.1) | collective-permute-done | bytes 131104 | tf_op jit(solution)/shard_map/ppermute | solution.py:346
  46.4 0.0 collective-permute-done.2.c3
  46.4 2.0 %all-to-all-done = f32[128,16,128]{2,1,0:T(8,128)S(1)} async-done(((f32[128,16,128]{2,1,0:T(8,128)}), f32[128,16,128]{2,1,0:T(8,128)S(1)}, u32[]{:S(2)}, u32[]{:S(2)}) %all-to-all-start) | async-done | bytes 1048608 | tf_op jit(solution)/shard_map/all_to_all | solution.py:344
  48.4 0.0 copy-done.1
  48.4 0.0 copy-done.2
  48.4 0.0 copy-start.3
  48.4 1.0 copy-done.3
  49.5 2.8 %columns.1 = f32[2048,128]{1,0:T(8,128)S(1)} custom-call(f32[2048,128]{1,0:T(8,128)S(1)} %bitcast.10, f32[4,256,128]{2,1,0:T(8,128)S(1)} %copy.12.inten, bf16[4,256,256]{2,1,0:T(8,128)(2,1)S(1)} %copy-done.2, bf16[2,4,256,256]{3,2,1,0:T(8,128)(2,1)S(1)} %copy-done.1, f32[2,4,128,128]{3,2,1,0:T(8,128)S(1)} %copy-done.3), custom_call_target="tpu_custom_call" | custom-call | flops 1610612736 | bytes 3145728 | tf_op jit(solution)/shard_map/columns/pallas_call | solution.py:349
  52.3 0.0 copy-start.4
  52.3 0.0 copy-start.5
  52.3 0.0 copy-start.6
  52.3 53.5 %all_to_all.10 = f32[512,4,128]{2,1,0:T(4,128)S(1)} all-to-all(f32[512,4,128]{2,1,0:T(4,128)S(1)} %bitcast.12), channel_id=1, replica_groups=mesh['mask'=4,'rows'=128] {'mask','rows'}, dimensions={0} | all-to-all | bytes 2097152 | tf_op jit(solution)/shard_map/all_to_all | solution.py:353
  105.8 0.0 copy-start
  105.8 0.0 copy-done.4
  105.8 0.0 copy-done.5
  105.8 0.0 copy-done.6
  105.8 1.1 rows_back.1
  106.9 3.3 %collective-permute-start.3 = (f32[8,4096]{1,0:T(8,128)S(1)}, f32[8,4096]{1,0:T(8,128)S(1)}, u32[]{:S(2)}, u32[]{:S(2)}) collective-permute-start(f32[8,4096]{1,0:T(8,128)S(1)} %get-tuple-element.22.own_re), channel_id=1, source_target_pairs={{0,128},{128,256},{256,384},{384,0},{1,129},{129,257},{257,385},{3... | collective-permute-start | bytes 393224 | tf_op jit(solution)/shard_map/ppermute | solution.py:358
  110.2 4.1 %collective-permute-start.6 = (f32[8,4096]{1,0:T(8,128)S(1)}, f32[8,4096]{1,0:T(8,128)S(1)}, u32[]{:S(2)}, u32[]{:S(2)}) collective-permute-start(f32[8,4096]{1,0:T(8,128)S(1)} %get-tuple-element.23.own_im), channel_id=1, source_target_pairs={{128,0},{256,128},{384,256},{0,384},{129,1},{257,129},{385,257},{1... | collective-permute-start | bytes 393224 | tf_op jit(solution)/shard_map/ppermute | solution.py:359
  114.3 2.1 %collective-permute-start.4 = (f32[8,4096]{1,0:T(8,128)S(1)}, f32[8,4096]{1,0:T(8,128)S(1)}, u32[]{:S(2)}, u32[]{:S(2)}) collective-permute-start(f32[8,4096]{1,0:T(8,128)S(1)} %get-tuple-element.23.own_im), channel_id=1, source_target_pairs={{0,128},{128,256},{256,384},{384,0},{1,129},{129,257},{257,385},{3... | collective-permute-start | bytes 393224 | tf_op jit(solution)/shard_map/ppermute | solution.py:360
  116.4 5.3 %collective-permute-start.5 = (f32[8,4096]{1,0:T(8,128)S(1)}, f32[8,4096]{1,0:T(8,128)S(1)}, u32[]{:S(2)}, u32[]{:S(2)}) collective-permute-start(f32[8,4096]{1,0:T(8,128)S(1)} %get-tuple-element.22.own_re), channel_id=1, source_target_pairs={{128,0},{256,128},{384,256},{0,384},{129,1},{257,129},{385,257},{1... | collective-permute-start | bytes 393224 | tf_op jit(solution)/shard_map/ppermute | solution.py:361
  121.7 0.0 collective-permute-done.3.b_re
  121.7 1.9 %collective-permute-start.7 = (f32[8,4096]{1,0:T(8,128)S(1)}, f32[8,4096]{1,0:T(8,128)S(1)}, u32[]{:S(2)}, u32[]{:S(2)}) collective-permute-start(f32[8,4096]{1,0:T(8,128)S(1)} %collective-permute-done.3.b_re), channel_id=1, source_target_pairs={{0,128},{128,256},{256,384},{384,0},{1,129},{129,257},{257,385},{3... | collective-permute-start | bytes 393224 | tf_op jit(solution)/shard_map/ppermute | solution.py:362
  123.7 0.0 collective-permute-done.6.a_im
  123.7 5.5 %collective-permute-start.8 = (f32[8,4096]{1,0:T(8,128)S(1)}, f32[8,4096]{1,0:T(8,128)S(1)}, u32[]{:S(2)}, u32[]{:S(2)}) collective-permute-start(f32[8,4096]{1,0:T(8,128)S(1)} %collective-permute-done.6.a_im), channel_id=1, source_target_pairs={{128,0},{256,128},{384,256},{0,384},{129,1},{257,129},{385,257},{1... | collective-permute-start | bytes 393224 | tf_op jit(solution)/shard_map/ppermute | solution.py:363
  129.1 0.0 collective-permute-done.4.b_im
  129.2 0.0 collective-permute-done.5.a_re
  129.2 3.2 %collective-permute-done.7.far_re = f32[8,4096]{1,0:T(8,128)S(1)} collective-permute-done((f32[8,4096]{1,0:T(8,128)S(1)}, f32[8,4096]{1,0:T(8,128)S(1)}, u32[]{:S(2)}, u32[]{:S(2)}) %collective-permute-start.7) | collective-permute-done | bytes 131104 | tf_op jit(solution)/shard_map/ppermute | solution.py:362
  132.4 0.0 collective-permute-done.8.far_im
  132.4 0.0 copy-done
  132.4 1.5 %finish.1 = (f32[2,32,4096]{2,1,0:T(8,128)}, f32[2,32,4096]{2,1,0:T(8,128)}) custom-call(s32[1]{0:T(128)} %bitcast.index, f32[8,4096]{1,0:T(8,128)S(1)} %get-tuple-element.22.own_re, f32[8,4096]{1,0:T(8,128)S(1)} %get-tuple-element.23.own_im, f32[8,4096]{1,0:T(8,128)S(1)} %collective-permute-done.3.b_re, f32[8,4096]{1,0:T(8,128)S(1)} %collective-permute-done.4.b_im, ...), custom_call_target="tpu_custom_call" | custom-call | flops 1048576 | bytes 3145728 | tf_op jit(solution)/shard_map/finish/pallas_call | solution.py:365
Async XLA Ops:
  5.2 31.5 %copy-start.7 = (f32[1,32,4096]{2,1,0:T(8,128)S(1)}, f32[1,32,4096]{2,1,0:T(8,128)}, u32[]{:S(2)}) copy-start(f32[1,32,4096]{2,1,0:T(8,128)} %param.10) | copy-start | bytes 1572868
  5.2 43.2 %all-to-all-start = ((f32[128,16,128]{2,1,0:T(8,128)}), f32[128,16,128]{2,1,0:T(8,128)S(1)}, u32[]{:S(2)}, u32[]{:S(2)}) async-start(f32[128,16,128]{2,1,0:T(8,128)} %bitcast.14), calls=%async_computation | async-start | bytes 2097152 | tf_op jit(solution)/shard_map/all_to_all | solution.py:344
  19.6 20.5 %collective-permute-start = (s32[8,4096]{1,0:T(8,128)}, s32[8,4096]{1,0:T(8,128)S(1)}, u32[]{:S(2)}, u32[]{:S(2)}) collective-permute-start(s32[8,4096]{1,0:T(8,128)} %get-tuple-element.14), channel_id=1, source_target_pairs={{0,128},{128,256},{256,384},{384,0},{1,129},{129,257},{257,385},{3... | collective-permute-start | bytes 393224 | tf_op jit(solution)/shard_map/ppermute | solution.py:345
  25.4 21.0 %collective-permute-start.1 = (s32[8,4096]{1,0:T(8,128)}, s32[8,4096]{1,0:T(8,128)S(1)}, u32[]{:S(2)}, u32[]{:S(2)}) collective-permute-start(s32[8,4096]{1,0:T(8,128)} %get-tuple-element.15), channel_id=1, source_target_pairs={{0,256},{128,384},{256,0},{384,128},{1,257},{129,385},{257,1},{385... | collective-permute-start | bytes 393224 | tf_op jit(solution)/shard_map/ppermute | solution.py:346
  33.4 13.1 %collective-permute-start.2 = (s32[8,4096]{1,0:T(8,128)}, s32[8,4096]{1,0:T(8,128)S(1)}, u32[]{:S(2)}, u32[]{:S(2)}) collective-permute-start(s32[8,4096]{1,0:T(8,128)} %get-tuple-element.16), channel_id=1, source_target_pairs={{128,0},{256,128},{384,256},{0,384},{129,1},{257,129},{385,257},{1... | collective-permute-start | bytes 393224 | tf_op jit(solution)/shard_map/ppermute | solution.py:347
  37.5 10.9 %copy-start.1 = (bf16[2,4,256,256]{3,2,1,0:T(8,128)(2,1)S(1)}, bf16[2,4,256,256]{3,2,1,0:T(8,128)(2,1)}, u32[]{:S(2)}) copy-start(bf16[2,4,256,256]{3,2,1,0:T(8,128)(2,1)} %constant.18.clone.block) | copy-start | bytes 3145732
  38.8 9.7 %copy-start.2 = (bf16[4,256,256]{2,1,0:T(8,128)(2,1)S(1)}, bf16[4,256,256]{2,1,0:T(8,128)(2,1)}, u32[]{:S(2)}) copy-start(bf16[4,256,256]{2,1,0:T(8,128)(2,1)} %constant.17.clone.both) | copy-start | bytes 1572868
  48.4 1.0 copy-start.3
  52.3 53.6 %copy-start.4 = (bf16[2,256,256]{2,1,0:T(8,128)(2,1)S(1)}, bf16[2,256,256]{2,1,0:T(8,128)(2,1)}, u32[]{:S(2)}) copy-start(bf16[2,256,256]{2,1,0:T(8,128)(2,1)} %constant.16.clone.left) | copy-start | bytes 786436
  52.3 53.5 %copy-start.5 = (f32[2,32,128]{2,1,0:T(8,128)S(1)}, f32[2,32,128]{2,1,0:T(8,128)}, u32[]{:S(2)}) copy-start(f32[2,32,128]{2,1,0:T(8,128)} %constant.19.clone.tw) | copy-start | bytes 98308
  52.3 53.5 %copy-start.6 = (s32[8,4096]{1,0:T(8,128)S(1)}, s32[8,4096]{1,0:T(8,128)}, u32[]{:S(2)}) copy-start(s32[8,4096]{1,0:T(8,128)} %get-tuple-element.18.c0) | copy-start | bytes 393220
  105.8 26.5 %copy-start = (f32[2,32,4096]{2,1,0:T(8,128)S(1)}, f32[2,32,4096]{2,1,0:T(8,128)}, u32[]{:S(2)}) copy-start(f32[2,32,4096]{2,1,0:T(8,128)} %obj.3) | copy-start | bytes 3145732
  106.9 14.8 %collective-permute-start.3 = (f32[8,4096]{1,0:T(8,128)S(1)}, f32[8,4096]{1,0:T(8,128)S(1)}, u32[]{:S(2)}, u32[]{:S(2)}) collective-permute-start(f32[8,4096]{1,0:T(8,128)S(1)} %get-tuple-element.22.own_re), channel_id=1, source_target_pairs={{0,128},{128,256},{256,384},{384,0},{1,129},{129,257},{257,385},{3... | collective-permute-start | bytes 393224 | tf_op jit(solution)/shard_map/ppermute | solution.py:358
  110.2 13.5 %collective-permute-start.6 = (f32[8,4096]{1,0:T(8,128)S(1)}, f32[8,4096]{1,0:T(8,128)S(1)}, u32[]{:S(2)}, u32[]{:S(2)}) collective-permute-start(f32[8,4096]{1,0:T(8,128)S(1)} %get-tuple-element.23.own_im), channel_id=1, source_target_pairs={{128,0},{256,128},{384,256},{0,384},{129,1},{257,129},{385,257},{1... | collective-permute-start | bytes 393224 | tf_op jit(solution)/shard_map/ppermute | solution.py:359
  114.3 14.8 %collective-permute-start.4 = (f32[8,4096]{1,0:T(8,128)S(1)}, f32[8,4096]{1,0:T(8,128)S(1)}, u32[]{:S(2)}, u32[]{:S(2)}) collective-permute-start(f32[8,4096]{1,0:T(8,128)S(1)} %get-tuple-element.23.own_im), channel_id=1, source_target_pairs={{0,128},{128,256},{256,384},{384,0},{1,129},{129,257},{257,385},{3... | collective-permute-start | bytes 393224 | tf_op jit(solution)/shard_map/ppermute | solution.py:360
  116.4 12.8 %collective-permute-start.5 = (f32[8,4096]{1,0:T(8,128)S(1)}, f32[8,4096]{1,0:T(8,128)S(1)}, u32[]{:S(2)}, u32[]{:S(2)}) collective-permute-start(f32[8,4096]{1,0:T(8,128)S(1)} %get-tuple-element.22.own_re), channel_id=1, source_target_pairs={{128,0},{256,128},{384,256},{0,384},{129,1},{257,129},{385,257},{1... | collective-permute-start | bytes 393224 | tf_op jit(solution)/shard_map/ppermute | solution.py:361
  121.7 10.6 %collective-permute-start.7 = (f32[8,4096]{1,0:T(8,128)S(1)}, f32[8,4096]{1,0:T(8,128)S(1)}, u32[]{:S(2)}, u32[]{:S(2)}) collective-permute-start(f32[8,4096]{1,0:T(8,128)S(1)} %collective-permute-done.3.b_re), channel_id=1, source_target_pairs={{0,128},{128,256},{256,384},{384,0},{1,129},{129,257},{257,385},{3... | collective-permute-start | bytes 393224 | tf_op jit(solution)/shard_map/ppermute | solution.py:362
  123.7 8.7 %collective-permute-start.8 = (f32[8,4096]{1,0:T(8,128)S(1)}, f32[8,4096]{1,0:T(8,128)S(1)}, u32[]{:S(2)}, u32[]{:S(2)}) collective-permute-start(f32[8,4096]{1,0:T(8,128)S(1)} %collective-permute-done.6.a_im), channel_id=1, source_target_pairs={{128,0},{256,128},{384,256},{0,384},{129,1},{257,129},{385,257},{1... | collective-permute-start | bytes 393224 | tf_op jit(solution)/shard_map/ppermute | solution.py:363

commit v4 on v3

--- a/solution.py
+++ b/solution.py
@@ -24,11 +24,18 @@
     return np.stack([high, low])
 
 
+def exchange_order():
+    index = np.arange(LANES).reshape(2, 4, 8, 2)
+    return index.transpose(3, 0, 1, 2).reshape(LANES)
+
+
 @functools.lru_cache(maxsize=None)
 def tables():
     i128 = np.arange(LANES)
     w = np.exp(-2j * math.pi * (np.outer(i128, i128) % LANES) / LANES) / 64.0
+    w = w[exchange_order()]
     left = np.block([[w.real, -w.imag], [w.imag, w.real]])
+    inner = np.block([[w.real.T, -w.imag.T], [w.imag.T, w.real.T]])
     t = np.exp(-2j * math.pi * np.outer(np.arange(SHORT), i128) / N)
     row_tw = np.stack([t.real, t.imag]).astype(np.float32)
     rho = i128 % OCT
@@ -41,7 +48,7 @@
         small = np.exp(-2j * math.pi * np.outer(r8, r8) / 8 - 2j * math.pi * r8[:, None] * e / 32)
         big = np.kron(np.eye(16), small)
         blocks.append(np.block([[big.real, big.imag], [-big.imag, big.real]]))
-    both = np.concatenate([_split(left), _split(left.T)])
+    both = np.concatenate([_split(inner), _split(inner.T)])
     return dict(left=_split(left), both=both, block=_split(np.stack(blocks)), row_tw=row_tw, col_tw=col_tw)
 
 
@@ -229,20 +236,19 @@
         y = dot3((both[2], both[3]), split(x), NN)
         for ri in range(2):
             for h in range(2):
-                out[pl.ds(m * 512 + ri * 2 + h, LANES, stride=4), :] = y[
+                out[pl.ds(m * 4 + ri * 2 + h, LANES, stride=16), :] = y[
                     LANES * ri : LANES * ri + LANES, LANES * h : LANES * h + LANES
                 ]
 
 
-def rows_back(index, rec, c0, c1, c2, c3, left, tw, out_re, out_im, mid, ys):
-    out = (out_re, out_im)
+def rows_back(index, rec, c0, c1, c2, c3, left, tw, out, mid, ys):
     for s, code in enumerate((c0, c1, c2, c3)):
         l = lax.rem(index[0] + MASKS - s, MASKS)
         x = jnp.concatenate(
             [
                 jnp.concatenate(
                     [
-                        rec[pl.ds(l * 512 + ri * 2 + h, LANES, stride=4), :].T
+                        rec[pl.ds(l * 4 + ri * 2 + h, LANES, stride=16), :].T
                         for ri in range(2)
                     ],
                     axis=1,
@@ -262,31 +268,24 @@
             v = conj_code_times(code[:, cols], v)
             for ri in range(2):
                 if s == 0:
-                    out[ri][:, cols] = v[ri]
+                    out[0, ri, :, cols] = v[ri]
                 elif s < MASKS - 1:
-                    out[ri][:, cols] += v[ri]
+                    out[0, ri, :, cols] += v[ri]
                 else:
-                    out[ri][:, cols] = (out[ri][:, cols] + v[ri]) * (1.0 / MASKS)
+                    total = (out[0, ri, :, cols] + v[ri]) * (1.0 / MASKS)
+                    for copy in range(MASKS):
+                        out[copy, ri, :, cols] = total
 
         fft32(load, store, mid, 1)
 
 
-def finish(index, own_re, own_im, b_re, b_im, a_re, a_im, far_re, far_im, obj, updated, direction):
-    me = index[0]
-
-    def put(shift, ri, value):
-        rows = pl.ds(pl.multiple_of(lax.rem(me + shift, MASKS) * OCT, OCT), OCT)
-        direction[ri, rows, :] = value
-        updated[ri, rows, :] = obj[ri, rows, :] - step_size * value
-
-    put(0, 0, own_re[...])
-    put(0, 1, own_im[...])
-    put(3, 0, b_re[...])
-    put(3, 1, b_im[...])
-    put(1, 0, a_re[...])
-    put(1, 1, a_im[...])
-    put(2, 0, far_re[...])
-    put(2, 1, far_im[...])
+def finish(parts, obj, updated, direction):
+    for m in range(MASKS):
+        rows = slice(OCT * m, OCT * m + OCT)
+        for ri in range(2):
+            value = parts[m, ri]
+            direction[ri, rows, :] = value
+            updated[ri, rows, :] = obj[ri, rows, :] - step_size * value
 
 
 VM = pl.BlockSpec(memory_space=pltpu.VMEM)
@@ -341,30 +340,26 @@
     up = [(i, (i + 1) % MASKS) for i in range(MASKS)]
     down = [((i + 1) % MASKS, i) for i in range(MASKS)]
     across = [(i, (i + 2) % MASKS) for i in range(MASKS)]
-    rec = lax.all_to_all(sent.reshape(LANES, 16, LANES), "rows", 0, 0, tiled=True)
+    order = [int(i) for i in exchange_order()]
+    every = [m * LANES + i for i in order for m in range(MASKS)]
+    exchange = functools.partial(lax.all_to_all, split_axis=0, concat_axis=0, tiled=True)
+    rec = exchange(sent.reshape(LANES, 16, LANES), "rows", axis_index_groups=[order])
     g1 = lax.ppermute(c1, "mask", up)
     g2 = lax.ppermute(c2, "mask", across)
     g3 = lax.ppermute(c3, "mask", down)
-    rec, g1, g2, g3 = lax.optimization_barrier((rec, g1, g2, g3))
     back = call(
         columns, "columns", sds((2048, LANES), F32), 5,
         [pltpu.VMEM((4, 2, 2, LANES, LANES), F32)], 3 << 29,
     )(rec.reshape(2048, LANES), inten, t["both"], t["block"], t["col_tw"])
-    rec = lax.all_to_all(back.reshape(512, 4, LANES), ("mask", "rows"), 0, 0, tiled=True)
-    own_re, own_im = call(
-        rows_back, "rows_back", (sds((OCT, N), F32),) * 2, 8,
+    back, g1, g2, g3 = lax.optimization_barrier((back, g1, g2, g3))
+    rec = exchange(back.reshape(512, 4, LANES), ("mask", "rows"), axis_index_groups=[every])
+    part = call(
+        rows_back, "rows_back", sds((MASKS, 2, OCT, N), F32), 8,
         [pltpu.VMEM((2, SHORT, OCT, LANES), F32), pltpu.VMEM((256, 256), F32)], 1 << 29, smem=(0,),
     )(index, rec.reshape(2048, LANES), c0, g1, g2, g3, t["left"], t["row_tw"])
-    b_re = lax.ppermute(own_re, "mask", up)
-    a_im = lax.ppermute(own_im, "mask", down)
-    b_im = lax.ppermute(own_im, "mask", up)
-    a_re = lax.ppermute(own_re, "mask", down)
-    far_re = lax.ppermute(b_re, "mask", up)
-    far_im = lax.ppermute(a_im, "mask", down)
+    parts = exchange(part, "mask")
     whole = sds((2, SHORT, N), F32)
-    return call(finish, "finish", (whole, whole), 10, [], 1 << 20, smem=(0,))(
-        index, own_re, own_im, b_re, b_im, a_re, a_im, far_re, far_im, object_field
-    )
+    return call(finish, "finish", (whole, whole), 2, [], 1 << 20)(parts, object_field)
 
 
 def solution(mesh):

time: 135 us -> 135 us (level); the launches traced: 134 us -> 132 us
  starting transfers between devices: 53.7 us -> 31.8 us
  blocking collectives: 53.5 us -> 74.3 us
    ppermute x6 -> x0, starting transfers between devices: 22.2 us -> none  [the longest x1 5.47 us: body(): far_im = lax.ppermute(a_im, 'mask', down)]
    all_to_all x1 -> x2, blocking collectives: 53.5 us -> 74.3 us  [the longest x1 47.3 us: body(): exchange(back.reshape(512, 4, LANES), ('mask', 'rows'), axis_index_groups...]
    all_to_all x1, waiting for transfers between devices: 1.99 us -> 11 us  [body(): exchange(sent.reshape(LANES, 16, LANES), 'rows', axis_index_groups=[order])]
    ppermute x1, waiting for transfers between devices: 6.33 us -> 0.01 us  [body(): g2 = lax.ppermute(c2, 'mask', across)]
    ppermute x6 -> x0, waiting for transfers between devices: 3.21 us -> none  [the longest x1 3.19 us: body(): far_re = lax.ppermute(b_re, 'mask', up)]
  transfers between devices with their start and end apart: 10 -> 4, of which waited for: 3 -> 1; matrix products, arithmetic and copies ran while one was open for 2% -> 2% of each run, Pallas kernels for 0% -> 2%
where the time goes in v4:
time: 135 us; the launch traced here: 132 us
  blocking collectives  74.3 us (55%)
  starting transfers between devices  31.8 us (24%)
  waiting for transfers between devices  11 us (8%)
  Pallas kernels  10.1 us (7%)
  local copies, waits for them, and re-layouts  4.34 us (3%)
    all_to_all x1, blocking collectives, body(): exchange(back.reshape(512, 4, LANES), ('mask', 'rows'), axis_index_groups...  47.3 us
    all_to_all x1, blocking collectives, body(): parts = exchange(part, 'mask')  27 us
    all_to_all x1, starting transfers between devices, body(): exchange(sent.reshape(LANES, 16, LANES), 'rows', axis_index_groups=[order])  14.7 us
    all_to_all x1, waiting for transfers between devices, body(): exchange(sent.reshape(LANES, 16, LANES), 'rows', axis_index_groups=[order])  11 us
    ppermute x1, starting transfers between devices, body(): g2 = lax.ppermute(c2, 'mask', across)  7.95 us
    ppermute x1, starting transfers between devices, body(): g1 = lax.ppermute(c1, 'mask', up)  5.8 us
    pallas_call x1, Pallas kernels, body(): pl.pallas_call(rows_forward, name='rows_forward', out_shape=(sds((2048, L...  4.6 us
    ppermute x1, starting transfers between devices, body(): g3 = lax.ppermute(c3, 'mask', down)  3.37 us
  transfers between devices with their start and end apart: 4, of which 1 were waited for; matrix products, arithmetic and copies ran while one was open for 2% of the time, Pallas kernels for 2%

profile of v4, /device:TPU:1, one launch (start us, length us, event | category | flops | bytes accessed | tf_op | source)
XLA Modules:
  0.0 132.4 jit_solution(11360483564800184837)
XLA Ops:
  0.6 4.6 %rows_forward.1 = (f32[2048,128]{1,0:T(8,128)}, s32[8,4096]{1,0:T(8,128)}, s32[8,4096]{1,0:T(8,128)}, s32[8,4096]{1,0:T(8,128)}, s32[8,4096]{1,0:T(8,128)}) custom-call(s32[1]{0:T(128)} %bitcast.index, f32[2,32,4096]{2,1,0:T(8,128)} %obj.3, s32[1,32,4096]{2,1,0:T(8,128)} %code.1, bf16[2,256,256]{2,1,0:T(8,128)(2,1)} %constant.16.clone.left, ...), custom_call_target="tpu_custom_call" | custom-call | flops 536870912 | bytes 3145728 | tf_op jit(solution)/shard_map/rows_forward/pallas_call | solution.py:319
  5.2 0.0 copy-start.7
  5.2 14.7 %all-to-all-start = ((f32[128,16,128]{2,1,0:T(8,128)}), f32[128,16,128]{2,1,0:T(8,128)S(1)}, u32[]{:S(2)}, u32[]{:S(2)}) async-start(f32[128,16,128]{2,1,0:T(8,128)} %bitcast.14), calls=%async_computation | async-start | bytes 2097152 | tf_op jit(solution)/shard_map/all_to_all | solution.py:346
  19.9 5.8 %collective-permute-start = (s32[8,4096]{1,0:T(8,128)}, s32[8,4096]{1,0:T(8,128)S(1)}, u32[]{:S(2)}, u32[]{:S(2)}) collective-permute-start(s32[8,4096]{1,0:T(8,128)} %get-tuple-element.12), channel_id=1, source_target_pairs={{0,128},{128,256},{256,384},{384,0},{1,129},{129,257},{257,385},{3... | collective-permute-start | bytes 393224 | tf_op jit(solution)/shard_map/ppermute | solution.py:347
  25.7 7.9 %collective-permute-start.1 = (s32[8,4096]{1,0:T(8,128)}, s32[8,4096]{1,0:T(8,128)S(1)}, u32[]{:S(2)}, u32[]{:S(2)}) collective-permute-start(s32[8,4096]{1,0:T(8,128)} %get-tuple-element.13), channel_id=1, source_target_pairs={{0,256},{128,384},{256,0},{384,128},{1,257},{129,385},{257,1},{385... | collective-permute-start | bytes 393224 | tf_op jit(solution)/shard_map/ppermute | solution.py:348
  33.7 3.4 %collective-permute-start.2 = (s32[8,4096]{1,0:T(8,128)}, s32[8,4096]{1,0:T(8,128)S(1)}, u32[]{:S(2)}, u32[]{:S(2)}) collective-permute-start(s32[8,4096]{1,0:T(8,128)} %get-tuple-element.14), channel_id=1, source_target_pairs={{128,0},{256,128},{384,256},{0,384},{129,1},{257,129},{385,257},{1... | collective-permute-start | bytes 393224 | tf_op jit(solution)/shard_map/ppermute | solution.py:349
  37.1 0.0 copy-done.7
  37.1 0.4 reshape.28
  37.4 0.4 copy.14
  37.9 0.0 copy-start.4
  37.9 1.2 reshape.29
  39.1 0.0 copy-start.5
  39.1 1.3 copy.12.inten
  40.4 11.0 %all-to-all-done = f32[128,16,128]{2,1,0:T(8,128)S(1)} async-done(((f32[128,16,128]{2,1,0:T(8,128)}), f32[128,16,128]{2,1,0:T(8,128)S(1)}, u32[]{:S(2)}, u32[]{:S(2)}) %all-to-all-start) | async-done | bytes 1048608 | tf_op jit(solution)/shard_map/all_to_all | solution.py:346
  51.4 0.0 copy-done.4
  51.4 0.0 copy-done.5
  51.4 0.0 copy-start.6
  51.4 1.0 copy-done.6
  52.5 3.0 %columns.1 = f32[2048,128]{1,0:T(8,128)S(1)} custom-call(f32[2048,128]{1,0:T(8,128)S(1)} %bitcast.11, f32[4,256,128]{2,1,0:T(8,128)S(1)} %copy.12.inten, bf16[4,256,256]{2,1,0:T(8,128)(2,1)S(1)} %copy-done.5, bf16[2,4,256,256]{3,2,1,0:T(8,128)(2,1)S(1)} %copy-done.4, f32[2,4,128,128]{3,2,1,0:T(8,128)S(1)} %copy-done.6), custom_call_target="tpu_custom_call" | custom-call | flops 1610612736 | bytes 3145728 | tf_op jit(solution)/shard_map/columns/pallas_call | solution.py:350
  55.4 0.0 collective-permute-done.c1
  55.4 0.0 collective-permute-done.1.c2
  55.4 0.0 collective-permute-done.2.c3
  55.4 0.0 copy-start.1
  55.5 0.0 copy-start.2
  55.5 0.0 copy-start.3
  55.5 47.3 %all_to_all.15 = f32[512,4,128]{2,1,0:T(4,128)S(1)} all-to-all(f32[512,4,128]{2,1,0:T(4,128)S(1)} %bitcast.12), channel_id=1, replica_groups={{0,128,256,384,2,130,258,386,4,132,260,388,6,134,262,390,8,136,264,392,..., dimensions={0} | all-to-all | bytes 2097152 | tf_op jit(solution)/shard_map/all_to_all | solution.py:355
  102.8 0.0 copy-done.1
  102.8 0.0 copy-done.2
  102.8 0.0 copy-done.3
  102.8 1.1 rows_back.1
  103.9 0.0 copy-start
  103.9 27.0 %all_to_all.16.parts = f32[4,2,8,4096]{3,2,1,0:T(8,128)S(1)} all-to-all(f32[4,2,8,4096]{3,2,1,0:T(8,128)S(1)} %rows_back.1), channel_id=1, replica_groups=mesh['mask'=4,'rows'=128] {'mask'}, dimensions={0} | all-to-all | bytes 2097152 | tf_op jit(solution)/shard_map/all_to_all | solution.py:360
  130.9 0.0 copy-done
  130.9 1.5 %finish.1 = (f32[2,32,4096]{2,1,0:T(8,128)}, f32[2,32,4096]{2,1,0:T(8,128)}) custom-call(f32[4,2,8,4096]{3,2,1,0:T(8,128)S(1)} %all_to_all.16.parts, f32[2,32,4096]{2,1,0:T(8,128)S(1)} %copy-done), custom_call_target="tpu_custom_call" | custom-call | flops 1048576 | bytes 3145728 | tf_op jit(solution)/shard_map/finish/pallas_call | solution.py:362
Async XLA Ops:
  5.2 31.8 %copy-start.7 = (f32[1,32,4096]{2,1,0:T(8,128)S(1)}, f32[1,32,4096]{2,1,0:T(8,128)}, u32[]{:S(2)}) copy-start(f32[1,32,4096]{2,1,0:T(8,128)} %param.10) | copy-start | bytes 1572868
  5.2 46.2 %all-to-all-start = ((f32[128,16,128]{2,1,0:T(8,128)}), f32[128,16,128]{2,1,0:T(8,128)S(1)}, u32[]{:S(2)}, u32[]{:S(2)}) async-start(f32[128,16,128]{2,1,0:T(8,128)} %bitcast.14), calls=%async_computation | async-start | bytes 2097152 | tf_op jit(solution)/shard_map/all_to_all | solution.py:346
  19.9 35.5 %collective-permute-start = (s32[8,4096]{1,0:T(8,128)}, s32[8,4096]{1,0:T(8,128)S(1)}, u32[]{:S(2)}, u32[]{:S(2)}) collective-permute-start(s32[8,4096]{1,0:T(8,128)} %get-tuple-element.12), channel_id=1, source_target_pairs={{0,128},{128,256},{256,384},{384,0},{1,129},{129,257},{257,385},{3... | collective-permute-start | bytes 393224 | tf_op jit(solution)/shard_map/ppermute | solution.py:347
  25.7 29.7 %collective-permute-start.1 = (s32[8,4096]{1,0:T(8,128)}, s32[8,4096]{1,0:T(8,128)S(1)}, u32[]{:S(2)}, u32[]{:S(2)}) collective-permute-start(s32[8,4096]{1,0:T(8,128)} %get-tuple-element.13), channel_id=1, source_target_pairs={{0,256},{128,384},{256,0},{384,128},{1,257},{129,385},{257,1},{385... | collective-permute-start | bytes 393224 | tf_op jit(solution)/shard_map/ppermute | solution.py:348
  33.7 21.7 %collective-permute-start.2 = (s32[8,4096]{1,0:T(8,128)}, s32[8,4096]{1,0:T(8,128)S(1)}, u32[]{:S(2)}, u32[]{:S(2)}) collective-permute-start(s32[8,4096]{1,0:T(8,128)} %get-tuple-element.14), channel_id=1, source_target_pairs={{128,0},{256,128},{384,256},{0,384},{129,1},{257,129},{385,257},{1... | collective-permute-start | bytes 393224 | tf_op jit(solution)/shard_map/ppermute | solution.py:349
  37.9 13.6 %copy-start.4 = (bf16[2,4,256,256]{3,2,1,0:T(8,128)(2,1)S(1)}, bf16[2,4,256,256]{3,2,1,0:T(8,128)(2,1)}, u32[]{:S(2)}) copy-start(bf16[2,4,256,256]{3,2,1,0:T(8,128)(2,1)} %constant.18.clone.block) | copy-start | bytes 3145732
  39.1 12.3 %copy-start.5 = (bf16[4,256,256]{2,1,0:T(8,128)(2,1)S(1)}, bf16[4,256,256]{2,1,0:T(8,128)(2,1)}, u32[]{:S(2)}) copy-start(bf16[4,256,256]{2,1,0:T(8,128)(2,1)} %constant.17.clone.both) | copy-start | bytes 1572868
  51.4 1.0 copy-start.6
  55.4 47.3 %copy-start.1 = (bf16[2,256,256]{2,1,0:T(8,128)(2,1)S(1)}, bf16[2,256,256]{2,1,0:T(8,128)(2,1)}, u32[]{:S(2)}) copy-start(bf16[2,256,256]{2,1,0:T(8,128)(2,1)} %constant.16.clone.left) | copy-start | bytes 786436
  55.5 47.3 %copy-start.2 = (s32[8,4096]{1,0:T(8,128)S(1)}, s32[8,4096]{1,0:T(8,128)}, u32[]{:S(2)}) copy-start(s32[8,4096]{1,0:T(8,128)} %get-tuple-element.16.c0) | copy-start | bytes 393220
  55.5 47.3 %copy-start.3 = (f32[2,32,128]{2,1,0:T(8,128)S(1)}, f32[2,32,128]{2,1,0:T(8,128)}, u32[]{:S(2)}) copy-start(f32[2,32,128]{2,1,0:T(8,128)} %constant.19.clone.tw) | copy-start | bytes 98308
  103.9 27.0 %copy-start = (f32[2,32,4096]{2,1,0:T(8,128)S(1)}, f32[2,32,4096]{2,1,0:T(8,128)}, u32[]{:S(2)}) copy-start(f32[2,32,4096]{2,1,0:T(8,128)} %obj.3) | copy-start | bytes 3145732

commit v5 on v4

--- a/solution.py
+++ b/solution.py
@@ -41,15 +41,13 @@
     rho = i128 % OCT
     row = np.arange(MASKS)[:, None] * OCT + rho[None, :]
     t = np.exp(-2j * math.pi * (i128[None, :, None] * row[:, None, :]) / N)
-    col_tw = np.stack([t.real, t.imag]).astype(np.float32)
-    blocks = []
-    for e in range(4):
-        r8 = np.arange(OCT)
-        small = np.exp(-2j * math.pi * np.outer(r8, r8) / 8 - 2j * math.pi * r8[:, None] * e / 32)
-        big = np.kron(np.eye(16), small)
-        blocks.append(np.block([[big.real, big.imag], [-big.imag, big.real]]))
-    both = np.concatenate([_split(inner), _split(inner.T)])
-    return dict(left=_split(left), both=both, block=_split(np.stack(blocks)), row_tw=row_tw, col_tw=col_tw)
+    col_tw = np.stack([t.real, t.imag])
+    r8 = np.arange(OCT)
+    big = np.kron(np.eye(16), np.exp(-2j * math.pi * np.outer(r8, r8) / 8))
+    block = np.block([[big.real, big.imag], [-big.imag, big.real]])
+    t = np.exp(-2j * math.pi * np.outer(np.arange(OCT), rho) / SHORT)
+    col_tw = np.concatenate([col_tw.reshape(2, 4 * LANES, LANES), np.stack([t.real, t.imag])], axis=1)
+    return dict(left=_split(left), inner=_split(inner), block=_split(block), row_tw=row_tw, col_tw=col_tw.astype(np.float32))
 
 
 def split(x):
@@ -66,6 +64,7 @@
 
 NN = ((1,), (0,))
 NT = ((1,), (1,))
+TN = ((0,), (0,))
 
 
 def cmul(a, b):
@@ -145,7 +144,7 @@
     return jnp.where(code >= 2, -a, a), jnp.where((code == 1) | (code == 2), -b, b)
 
 
-def rows_forward(index, obj, code, left, tw, out, c0, c1, c2, c3, mid, xs):
+def rows_forward(index, obj, code, left, tw, out, c0, c2, c1, c3, mid, xs):
     m = pl.program_id(0)
     shift = lax.rem(m + MASKS - index[0], MASKS)
     for s, c in enumerate((c0, c1, c2, c3)):
@@ -172,7 +171,11 @@
             ]
 
 
-def columns(rec, inten, both, block, tw, out, s):
+def columns(rec, inten, inner, block, tw, out, s):
+    def turned(e, sign):
+        row = slice(4 * LANES + e, 4 * LANES + e + 1)
+        return tw[0, row, :], sign * tw[1, row, :]
+
     for m in range(MASKS):
         x = jnp.concatenate(
             [
@@ -183,8 +186,9 @@
             ],
             axis=0,
         )
-        y = dot3((both[0], both[1]), split(x), NN)
-        t = (tw[0, m], tw[1, m])
+        y = dot3((inner[0], inner[1]), split(x), NN)
+        rows = slice(LANES * m, LANES * m + LANES)
+        t = (tw[0, rows], tw[1, rows])
         for h in range(2):
             cols = slice(LANES * h, LANES * h + LANES)
             v = cmul((y[:LANES, cols], y[LANES:, cols]), t)
@@ -196,8 +200,9 @@
             rows = pl.ds(pl.multiple_of(i * OCT, OCT), OCT)
             y = fft4([(s[m, 0, h, rows, :], s[m, 1, h, rows, :]) for m in range(4)], -1)
             for e in range(4):
-                s[e, 0, h, rows, :] = y[e][0]
-                s[e, 1, h, rows, :] = y[e][1]
+                v = cmul(y[e], turned(e, 1)) if e else y[e]
+                s[e, 0, h, rows, :] = v[0]
+                s[e, 1, h, rows, :] = v[1]
             return 0
 
         lax.fori_loop(0, LANES // OCT, turn, 0, unroll=True)
@@ -206,12 +211,11 @@
         x = jnp.concatenate(
             [jnp.concatenate([s[e, 0, h], s[e, 1, h]], axis=1) for h in range(2)], axis=0
         )
-        table = (block[0, e], block[1, e])
-        y = dot3(split(x), table, NN)
+        y = dot3(split(x), (block[0], block[1]), NN)
         wr, wi = y[:, :LANES], y[:, LANES:]
         weight = wr * wr + wi * wi - inten[e]
         v = jnp.concatenate([wr * weight, wi * weight], axis=1)
-        y = dot3(split(v), table, NT)
+        y = dot3(split(v), (block[0], block[1]), NT)
         for h in range(2):
             rows = slice(LANES * h, LANES * h + LANES)
             s[e, 0, h] = y[rows, :LANES]
@@ -220,9 +224,11 @@
     for h in range(2):
         def turn_back(i, _):
             rows = pl.ds(pl.multiple_of(i * OCT, OCT), OCT)
-            y = fft4([(s[e, 0, h, rows, :], s[e, 1, h, rows, :]) for e in range(4)], 1)
+            x = [(s[e, 0, h, rows, :], s[e, 1, h, rows, :]) for e in range(4)]
+            y = fft4([cmul(v, turned(e, -1)) if e else v for e, v in enumerate(x)], 1)
             for m in range(4):
-                v = cmul(y[m], (tw[0, m, rows, :], -tw[1, m, rows, :]))
+                near = pl.ds(pl.multiple_of(LANES * m + i * OCT, OCT), OCT)
+                v = cmul(y[m], (tw[0, near, :], -tw[1, near, :]))
                 s[m, 0, h, rows, :] = v[0]
                 s[m, 1, h, rows, :] = v[1]
             return 0
@@ -233,7 +239,7 @@
         x = jnp.concatenate(
             [jnp.concatenate([s[m, ri, 0], s[m, ri, 1]], axis=1) for ri in range(2)], axis=0
         )
-        y = dot3((both[2], both[3]), split(x), NN)
+        y = dot3((inner[0], inner[1]), split(x), TN)
         for ri in range(2):
             for h in range(2):
                 out[pl.ds(m * 4 + ri * 2 + h, LANES, stride=16), :] = y[
@@ -316,7 +322,7 @@
     octet = lambda m: (0, m, 0)
     flat = lambda m: (0, 0)
     rows8 = sds((OCT, N), jnp.int32)
-    sent, c0, c1, c2, c3 = pl.pallas_call(
+    sent, c0, c2, c1, c3 = pl.pallas_call(
         rows_forward,
         name="rows_forward",
         out_shape=(sds((2048, LANES), F32),) + (rows8,) * MASKS,
@@ -350,8 +356,8 @@
     back = call(
         columns, "columns", sds((2048, LANES), F32), 5,
         [pltpu.VMEM((4, 2, 2, LANES, LANES), F32)], 3 << 29,
-    )(rec.reshape(2048, LANES), inten, t["both"], t["block"], t["col_tw"])
-    back, g1, g2, g3 = lax.optimization_barrier((back, g1, g2, g3))
+    )(rec.reshape(2048, LANES), inten, t["inner"], t["block"], t["col_tw"])
+    back, g2, g1, g3 = lax.optimization_barrier((back, g2, g1, g3))
     rec = exchange(back.reshape(512, 4, LANES), ("mask", "rows"), axis_index_groups=[every])
     part = call(
         rows_back, "rows_back", sds((MASKS, 2, OCT, N), F32), 8,

time: 135 us -> 134 us (level)
  local copies, waits for them, and re-layouts: 4.34 us -> 1.42 us
  waiting for transfers between devices: 11 us -> 12.9 us
    reshape x4, local copies, waits for them, and re-layouts: 3.26 us -> 1.37 us  [body(): intensity.reshape(2, 16, 8, 4, LANES).transpose(3, 0, 4, 1, 2)]
    all_to_all x1, waiting for transfers between devices: 11 us -> 12.9 us  [body(): exchange(sent.reshape(LANES, 16, LANES), 'rows', axis_index_groups=[order])]
    ppermute x1, starting transfers between devices: 5.8 us -> 4.02 us  [body(): g1 = lax.ppermute(c1, 'mask', up)]
    ppermute x1, starting transfers between devices: 7.95 us -> 9.73 us  [body(): g2 = lax.ppermute(c2, 'mask', across)]
  transfers between devices with their start and end apart: 4 -> 4, of which waited for: 1 -> 1; matrix products, arithmetic and copies ran while one was open for 2% -> 1% of each run, Pallas kernels for 2% -> 2%
where the time goes in v5:
time: 134 us; the launch traced here: 131 us
  blocking collectives  74.2 us (55%)
  starting transfers between devices  31.8 us (24%)
  waiting for transfers between devices  12.9 us (10%)
  Pallas kernels  10.3 us (8%)
  local copies, waits for them, and re-layouts  1.42 us (1%)
    all_to_all x1, blocking collectives, body(): exchange(back.reshape(512, 4, LANES), ('mask', 'rows'), axis_index_groups...  47.2 us
    all_to_all x1, blocking collectives, body(): parts = exchange(part, 'mask')  27 us
    all_to_all x1, starting transfers between devices, body(): exchange(sent.reshape(LANES, 16, LANES), 'rows', axis_index_groups=[order])  14.7 us
    all_to_all x1, waiting for transfers between devices, body(): exchange(sent.reshape(LANES, 16, LANES), 'rows', axis_index_groups=[order])  12.9 us
    ppermute x1, starting transfers between devices, body(): g2 = lax.ppermute(c2, 'mask', across)  9.73 us
    pallas_call x1, Pallas kernels, body(): pl.pallas_call(rows_forward, name='rows_forward', out_shape=(sds((2048, L...  4.6 us
    ppermute x1, starting transfers between devices, body(): g1 = lax.ppermute(c1, 'mask', up)  4.02 us
    ppermute x1, starting transfers between devices, body(): g3 = lax.ppermute(c3, 'mask', down)  3.37 us
  transfers between devices with their start and end apart: 4, of which 1 were waited for; matrix products, arithmetic and copies ran while one was open for 1% of the time, Pallas kernels for 2%

profile of v5, /device:TPU:1, one launch (start us, length us, event | category | flops | bytes accessed | tf_op | source)
XLA Modules:
  0.0 131.4 jit_solution(3756797993287032803)
XLA Ops:
  0.6 4.6 %rows_forward.1 = (f32[2048,128]{1,0:T(8,128)}, s32[8,4096]{1,0:T(8,128)}, s32[8,4096]{1,0:T(8,128)}, s32[8,4096]{1,0:T(8,128)}, s32[8,4096]{1,0:T(8,128)}) custom-call(s32[1]{0:T(128)} %bitcast.index, f32[2,32,4096]{2,1,0:T(8,128)} %obj.3, s32[1,32,4096]{2,1,0:T(8,128)} %code.1, bf16[2,256,256]{2,1,0:T(8,128)(2,1)} %constant.16.clone.left, ...), custom_call_target="tpu_custom_call" | custom-call | flops 536870912 | bytes 3145728 | tf_op jit(solution)/shard_map/rows_forward/pallas_call | solution.py:325
  5.2 0.0 copy-start.7
  5.2 14.7 %all-to-all-start = ((f32[128,16,128]{2,1,0:T(8,128)}), f32[128,16,128]{2,1,0:T(8,128)S(1)}, u32[]{:S(2)}, u32[]{:S(2)}) async-start(f32[128,16,128]{2,1,0:T(8,128)} %bitcast.14), calls=%async_computation | async-start | bytes 2097152 | tf_op jit(solution)/shard_map/all_to_all | solution.py:352
  19.9 9.7 %collective-permute-start = (s32[8,4096]{1,0:T(8,128)}, s32[8,4096]{1,0:T(8,128)S(1)}, u32[]{:S(2)}, u32[]{:S(2)}) collective-permute-start(s32[8,4096]{1,0:T(8,128)} %get-tuple-element.12), channel_id=1, source_target_pairs={{0,256},{128,384},{256,0},{384,128},{1,257},{129,385},{257,1},{385... | collective-permute-start | bytes 393224 | tf_op jit(solution)/shard_map/ppermute | solution.py:354
  29.7 4.0 %collective-permute-start.1 = (s32[8,4096]{1,0:T(8,128)}, s32[8,4096]{1,0:T(8,128)S(1)}, u32[]{:S(2)}, u32[]{:S(2)}) collective-permute-start(s32[8,4096]{1,0:T(8,128)} %get-tuple-element.13), channel_id=1, source_target_pairs={{0,128},{128,256},{256,384},{384,0},{1,129},{129,257},{257,385},{3... | collective-permute-start | bytes 393224 | tf_op jit(solution)/shard_map/ppermute | solution.py:353
  33.7 3.4 %collective-permute-start.2 = (s32[8,4096]{1,0:T(8,128)}, s32[8,4096]{1,0:T(8,128)S(1)}, u32[]{:S(2)}, u32[]{:S(2)}) collective-permute-start(s32[8,4096]{1,0:T(8,128)} %get-tuple-element.14), channel_id=1, source_target_pairs={{128,0},{256,128},{384,256},{0,384},{129,1},{257,129},{385,257},{1... | collective-permute-start | bytes 393224 | tf_op jit(solution)/shard_map/ppermute | solution.py:355
  37.1 0.0 copy-done.7
  37.1 0.4 reshape.28
  37.4 0.4 copy.14
  37.9 0.0 copy-start.6
  37.9 0.4 reshape.29
  38.3 0.0 copy-start.4
  38.3 0.0 copy-start.5
  38.3 0.2 copy.12.inten
  38.5 12.9 %all-to-all-done = f32[128,16,128]{2,1,0:T(8,128)S(1)} async-done(((f32[128,16,128]{2,1,0:T(8,128)}), f32[128,16,128]{2,1,0:T(8,128)S(1)}, u32[]{:S(2)}, u32[]{:S(2)}) %all-to-all-start) | async-done | bytes 1048608 | tf_op jit(solution)/shard_map/all_to_all | solution.py:352
  51.4 0.0 copy-done.6
  51.4 0.0 copy-done.4
  51.4 0.0 copy-done.5
  51.4 3.1 %columns.1 = f32[2048,128]{1,0:T(8,128)S(1)} custom-call(f32[2048,128]{1,0:T(8,128)S(1)} %bitcast.11, f32[4,256,128]{2,1,0:T(8,128)S(1)} %copy.12.inten, bf16[2,256,256]{2,1,0:T(8,128)(2,1)S(1)} %copy-done.5, bf16[2,256,256]{2,1,0:T(8,128)(2,1)S(1)} %copy-done.6, f32[2,520,128]{2,1,0:T(8,128)S(1)} %copy-done.4), custom_call_target="tpu_custom_call" | custom-call | flops 1610612736 | bytes 3145728 | tf_op jit(solution)/shard_map/columns/pallas_call | solution.py:356
  54.5 0.0 collective-permute-done.c2
  54.5 0.0 collective-permute-done.1.c1
  54.5 0.0 collective-permute-done.2.c3
  54.5 0.0 copy-start.1
  54.5 0.0 copy-start.2
  54.5 0.0 copy-start.3
  54.6 47.2 %all_to_all.15 = f32[512,4,128]{2,1,0:T(4,128)S(1)} all-to-all(f32[512,4,128]{2,1,0:T(4,128)S(1)} %bitcast.12), channel_id=1, replica_groups={{0,128,256,384,2,130,258,386,4,132,260,388,6,134,262,390,8,136,264,392,..., dimensions={0} | all-to-all | bytes 2097152 | tf_op jit(solution)/shard_map/all_to_all | solution.py:361
  101.8 0.0 copy-done.1
  101.8 0.0 copy-done.2
  101.8 0.0 copy-done.3
  101.8 1.1 rows_back.1
  102.9 0.0 copy-start
  103.0 27.0 %all_to_all.16.parts = f32[4,2,8,4096]{3,2,1,0:T(8,128)S(1)} all-to-all(f32[4,2,8,4096]{3,2,1,0:T(8,128)S(1)} %rows_back.1), channel_id=1, replica_groups=mesh['mask'=4,'rows'=128] {'mask'}, dimensions={0} | all-to-all | bytes 2097152 | tf_op jit(solution)/shard_map/all_to_all | solution.py:366
  129.9 0.0 copy-done
  129.9 1.5 %finish.1 = (f32[2,32,4096]{2,1,0:T(8,128)}, f32[2,32,4096]{2,1,0:T(8,128)}) custom-call(f32[4,2,8,4096]{3,2,1,0:T(8,128)S(1)} %all_to_all.16.parts, f32[2,32,4096]{2,1,0:T(8,128)S(1)} %copy-done), custom_call_target="tpu_custom_call" | custom-call | flops 1048576 | bytes 3145728 | tf_op jit(solution)/shard_map/finish/pallas_call | solution.py:368
Async XLA Ops:
  5.2 31.8 %copy-start.7 = (f32[1,32,4096]{2,1,0:T(8,128)S(1)}, f32[1,32,4096]{2,1,0:T(8,128)}, u32[]{:S(2)}) copy-start(f32[1,32,4096]{2,1,0:T(8,128)} %param.10) | copy-start | bytes 1572868
  5.2 46.1 %all-to-all-start = ((f32[128,16,128]{2,1,0:T(8,128)}), f32[128,16,128]{2,1,0:T(8,128)S(1)}, u32[]{:S(2)}, u32[]{:S(2)}) async-start(f32[128,16,128]{2,1,0:T(8,128)} %bitcast.14), calls=%async_computation | async-start | bytes 2097152 | tf_op jit(solution)/shard_map/all_to_all | solution.py:352
  19.9 34.6 %collective-permute-start = (s32[8,4096]{1,0:T(8,128)}, s32[8,4096]{1,0:T(8,128)S(1)}, u32[]{:S(2)}, u32[]{:S(2)}) collective-permute-start(s32[8,4096]{1,0:T(8,128)} %get-tuple-element.12), channel_id=1, source_target_pairs={{0,256},{128,384},{256,0},{384,128},{1,257},{129,385},{257,1},{385... | collective-permute-start | bytes 393224 | tf_op jit(solution)/shard_map/ppermute | solution.py:354
  29.7 24.8 %collective-permute-start.1 = (s32[8,4096]{1,0:T(8,128)}, s32[8,4096]{1,0:T(8,128)S(1)}, u32[]{:S(2)}, u32[]{:S(2)}) collective-permute-start(s32[8,4096]{1,0:T(8,128)} %get-tuple-element.13), channel_id=1, source_target_pairs={{0,128},{128,256},{256,384},{384,0},{1,129},{129,257},{257,385},{3... | collective-permute-start | bytes 393224 | tf_op jit(solution)/shard_map/ppermute | solution.py:353
  33.7 20.8 %collective-permute-start.2 = (s32[8,4096]{1,0:T(8,128)}, s32[8,4096]{1,0:T(8,128)S(1)}, u32[]{:S(2)}, u32[]{:S(2)}) collective-permute-start(s32[8,4096]{1,0:T(8,128)} %get-tuple-element.14), channel_id=1, source_target_pairs={{128,0},{256,128},{384,256},{0,384},{129,1},{257,129},{385,257},{1... | collective-permute-start | bytes 393224 | tf_op jit(solution)/shard_map/ppermute | solution.py:355
  37.9 13.5 %copy-start.6 = (bf16[2,256,256]{2,1,0:T(8,128)(2,1)S(1)}, bf16[2,256,256]{2,1,0:T(8,128)(2,1)}, u32[]{:S(2)}) copy-start(bf16[2,256,256]{2,1,0:T(8,128)(2,1)} %constant.18.clone.block) | copy-start | bytes 786436
  38.3 13.1 %copy-start.4 = (f32[2,520,128]{2,1,0:T(8,128)S(1)}, f32[2,520,128]{2,1,0:T(8,128)}, u32[]{:S(2)}) copy-start(f32[2,520,128]{2,1,0:T(8,128)} %constant.20.clone.tw) | copy-start | bytes 1597444
  38.3 13.1 %copy-start.5 = (bf16[2,256,256]{2,1,0:T(8,128)(2,1)S(1)}, bf16[2,256,256]{2,1,0:T(8,128)(2,1)}, u32[]{:S(2)}) copy-start(bf16[2,256,256]{2,1,0:T(8,128)(2,1)} %constant.17.clone.inner) | copy-start | bytes 786436
  54.5 47.3 %copy-start.1 = (bf16[2,256,256]{2,1,0:T(8,128)(2,1)S(1)}, bf16[2,256,256]{2,1,0:T(8,128)(2,1)}, u32[]{:S(2)}) copy-start(bf16[2,256,256]{2,1,0:T(8,128)(2,1)} %constant.16.clone.left) | copy-start | bytes 786436
  54.5 47.3 %copy-start.2 = (s32[8,4096]{1,0:T(8,128)S(1)}, s32[8,4096]{1,0:T(8,128)}, u32[]{:S(2)}) copy-start(s32[8,4096]{1,0:T(8,128)} %get-tuple-element.16.c0) | copy-start | bytes 393220
  54.5 47.3 %copy-start.3 = (f32[2,32,128]{2,1,0:T(8,128)S(1)}, f32[2,32,128]{2,1,0:T(8,128)}, u32[]{:S(2)}) copy-start(f32[2,32,128]{2,1,0:T(8,128)} %constant.19.clone.tw) | copy-start | bytes 98308
  102.9 27.0 %copy-start = (f32[2,32,4096]{2,1,0:T(8,128)S(1)}, f32[2,32,4096]{2,1,0:T(8,128)}, u32[]{:S(2)}) copy-start(f32[2,32,4096]{2,1,0:T(8,128)} %obj.3) | copy-start | bytes 3145732

commit v6 on v5

--- a/solution.py
+++ b/solution.py
@@ -26,7 +26,7 @@
 
 def exchange_order():
     index = np.arange(LANES).reshape(2, 4, 8, 2)
-    return index.transpose(3, 0, 1, 2).reshape(LANES)
+    return index.transpose(0, 1, 3, 2).reshape(LANES)
 
 
 @functools.lru_cache(maxsize=None)
@@ -274,22 +274,20 @@
             v = conj_code_times(code[:, cols], v)
             for ri in range(2):
                 if s == 0:
-                    out[0, ri, :, cols] = v[ri]
+                    out[ri, :, cols] = v[ri]
                 elif s < MASKS - 1:
-                    out[0, ri, :, cols] += v[ri]
+                    out[ri, :, cols] += v[ri]
                 else:
-                    total = (out[0, ri, :, cols] + v[ri]) * (1.0 / MASKS)
-                    for copy in range(MASKS):
-                        out[copy, ri, :, cols] = total
+                    out[ri, :, cols] = (out[ri, :, cols] + v[ri]) * (1.0 / MASKS)
 
         fft32(load, store, mid, 1)
 
 
-def finish(parts, obj, updated, direction):
-    for m in range(MASKS):
-        rows = slice(OCT * m, OCT * m + OCT)
+def finish(masks, own, near, far, other, obj, updated, direction):
+    for i, part in enumerate((own, near, far, other)):
+        rows = pl.ds(pl.multiple_of(masks[i] * OCT, OCT), OCT)
         for ri in range(2):
-            value = parts[m, ri]
+            value = part[ri]
             direction[ri, rows, :] = value
             updated[ri, rows, :] = obj[ri, rows, :] - step_size * value
 
@@ -360,12 +358,27 @@
     back, g2, g1, g3 = lax.optimization_barrier((back, g2, g1, g3))
     rec = exchange(back.reshape(512, 4, LANES), ("mask", "rows"), axis_index_groups=[every])
     part = call(
-        rows_back, "rows_back", sds((MASKS, 2, OCT, N), F32), 8,
+        rows_back, "rows_back", sds((2, OCT, N), F32), 8,
         [pltpu.VMEM((2, SHORT, OCT, LANES), F32), pltpu.VMEM((256, 256), F32)], 1 << 29, smem=(0,),
     )(index, rec.reshape(2048, LANES), c0, g1, g2, g3, t["left"], t["row_tw"])
-    parts = exchange(part, "mask")
+    ring = [
+        (m * LANES + r, (m + 1 - 2 * (r % 2)) % MASKS * LANES + r)
+        for m in range(MASKS)
+        for r in range(LANES)
+    ]
+    swap = [(r, r ^ 1) for r in range(LANES)]
+    near = lax.ppermute(part, ("mask", "rows"), ring)
+    partner = lax.ppermute(part, "rows", swap)
+    passed = lax.ppermute(partner, ("mask", "rows"), ring)
+    far = lax.ppermute(near, ("mask", "rows"), ring)
+    other = lax.ppermute(passed, "rows", swap)
+    side = 2 * (lax.axis_index("rows").astype(jnp.int32) % 2) - 1
+    me = index[0] + MASKS
+    masks = jnp.stack([me, me + side, me + 2, me - side]) % MASKS
     whole = sds((2, SHORT, N), F32)
-    return call(finish, "finish", (whole, whole), 2, [], 1 << 20)(parts, object_field)
+    return call(finish, "finish", (whole, whole), 6, [], 1 << 20, smem=(0,))(
+        masks, part, near, far, other, object_field
+    )
 
 
 def solution(mesh):

time: 134 us -> 132 us (0.985)
  blocking collectives: 74.2 us -> 48.2 us
  starting transfers between devices: 31.8 us -> 45.9 us
  waiting for transfers between devices: 12.9 us -> 21.9 us
    all_to_all x1 -> x0, blocking collectives: 27 us -> none  [body(): parts = exchange(part, 'mask')]
    ppermute x0 -> x5, starting transfers between devices: none -> 14.4 us  [the longest x1 3.89 us: body(): passed = lax.ppermute(partner, ('mask', 'rows'), ring)]
    ppermute x0 -> x5, waiting for transfers between devices: none -> 11.9 us  [the longest x1 6.96 us: body(): near = lax.ppermute(part, ('mask', 'rows'), ring)]
    all_to_all x1, waiting for transfers between devices: 12.9 us -> 10 us  [body(): exchange(sent.reshape(LANES, 16, LANES), 'rows', axis_index_groups=[order])]
  transfers between devices with their start and end apart: 4 -> 9, of which waited for: 1 -> 4; matrix products, arithmetic and copies ran while one was open for 1% -> 1% of each run, Pallas kernels for 2% -> 2%
where the time goes in v6:
time: 132 us; the launch traced here: 129 us
  blocking collectives  48.2 us (37%)
  starting transfers between devices  45.9 us (35%)
  waiting for transfers between devices  21.9 us (17%)
  Pallas kernels  10.8 us (8%)
  local copies, waits for them, and re-layouts  1.42 us (1%)
    all_to_all x1, blocking collectives, body(): exchange(back.reshape(512, 4, LANES), ('mask', 'rows'), axis_index_groups...  48.2 us
    all_to_all x1, starting transfers between devices, body(): exchange(sent.reshape(LANES, 16, LANES), 'rows', axis_index_groups=[order])  14.4 us
    all_to_all x1, waiting for transfers between devices, body(): exchange(sent.reshape(LANES, 16, LANES), 'rows', axis_index_groups=[order])  10 us
    ppermute x1, starting transfers between devices, body(): g2 = lax.ppermute(c2, 'mask', across)  9.73 us
    ppermute x1, waiting for transfers between devices, body(): near = lax.ppermute(part, ('mask', 'rows'), ring)  6.96 us
    pallas_call x1, Pallas kernels, body(): pl.pallas_call(rows_forward, name='rows_forward', out_shape=(sds((2048, L...  4.6 us
    ppermute x1, starting transfers between devices, body(): g1 = lax.ppermute(c1, 'mask', up)  4.02 us
    ppermute x1, starting transfers between devices, body(): passed = lax.ppermute(partner, ('mask', 'rows'), ring)  3.89 us
  transfers between devices with their start and end apart: 9, of which 4 were waited for; matrix products, arithmetic and copies ran while one was open for 1% of the time, Pallas kernels for 2%

profile of v6, /device:TPU:1, one launch (start us, length us, event | category | flops | bytes accessed | tf_op | source)
XLA Modules:
  0.0 129.2 jit_solution(12165526967062610145)
XLA Ops:
  0.6 4.6 %rows_forward.1 = (f32[2048,128]{1,0:T(8,128)}, s32[8,4096]{1,0:T(8,128)}, s32[8,4096]{1,0:T(8,128)}, s32[8,4096]{1,0:T(8,128)}, s32[8,4096]{1,0:T(8,128)}) custom-call(s32[1]{0:T(128)} %bitcast.4.index, f32[2,32,4096]{2,1,0:T(8,128)} %obj.3, s32[1,32,4096]{2,1,0:T(8,128)} %code.1, bf16[2,256,256]{2,1,0:T(8,128)(2,1)} %constant.51.clone.left, ...), custom_call_target="tpu_custom_call" | custom-call | flops 536870912 | bytes 3145728 | tf_op jit(solution)/shard_map/rows_forward/pallas_call | solution.py:323
  5.2 0.0 copy-start.7
  5.3 14.4 %all-to-all-start = ((f32[128,16,128]{2,1,0:T(8,128)}), f32[128,16,128]{2,1,0:T(8,128)S(1)}, u32[]{:S(2)}, u32[]{:S(2)}) async-start(f32[128,16,128]{2,1,0:T(8,128)} %bitcast.18), calls=%async_computation | async-start | bytes 2097152 | tf_op jit(solution)/shard_map/all_to_all | solution.py:350
  19.6 9.7 %collective-permute-start = (s32[8,4096]{1,0:T(8,128)}, s32[8,4096]{1,0:T(8,128)S(1)}, u32[]{:S(2)}, u32[]{:S(2)}) collective-permute-start(s32[8,4096]{1,0:T(8,128)} %get-tuple-element.12), channel_id=1, source_target_pairs={{0,256},{128,384},{256,0},{384,128},{1,257},{129,385},{257,1},{385... | collective-permute-start | bytes 393224 | tf_op jit(solution)/shard_map/ppermute | solution.py:352
  29.4 4.0 %collective-permute-start.1 = (s32[8,4096]{1,0:T(8,128)}, s32[8,4096]{1,0:T(8,128)S(1)}, u32[]{:S(2)}, u32[]{:S(2)}) collective-permute-start(s32[8,4096]{1,0:T(8,128)} %get-tuple-element.13), channel_id=1, source_target_pairs={{0,128},{128,256},{256,384},{384,0},{1,129},{129,257},{257,385},{3... | collective-permute-start | bytes 393224 | tf_op jit(solution)/shard_map/ppermute | solution.py:351
  33.4 3.4 %collective-permute-start.2 = (s32[8,4096]{1,0:T(8,128)}, s32[8,4096]{1,0:T(8,128)S(1)}, u32[]{:S(2)}, u32[]{:S(2)}) collective-permute-start(s32[8,4096]{1,0:T(8,128)} %get-tuple-element.14), channel_id=1, source_target_pairs={{128,0},{256,128},{384,256},{0,384},{129,1},{257,129},{385,257},{1... | collective-permute-start | bytes 393224 | tf_op jit(solution)/shard_map/ppermute | solution.py:353
  36.8 0.0 copy-done.7
  36.8 0.4 reshape.28
  37.1 0.4 copy.14
  37.5 0.0 copy-start.6
  37.6 0.4 reshape.29
  38.0 0.0 copy-start.4
  38.0 0.0 copy-start.5
  38.0 0.2 copy.12.inten
  38.2 10.0 %all-to-all-done = f32[128,16,128]{2,1,0:T(8,128)S(1)} async-done(((f32[128,16,128]{2,1,0:T(8,128)}), f32[128,16,128]{2,1,0:T(8,128)S(1)}, u32[]{:S(2)}, u32[]{:S(2)}) %all-to-all-start) | async-done | bytes 1048608 | tf_op jit(solution)/shard_map/all_to_all | solution.py:350
  48.2 0.0 copy-done.6
  48.2 0.0 copy-done.4
  48.2 0.0 copy-done.5
  48.3 3.1 %columns.1 = f32[2048,128]{1,0:T(8,128)S(1)} custom-call(f32[2048,128]{1,0:T(8,128)S(1)} %bitcast.15, f32[4,256,128]{2,1,0:T(8,128)S(1)} %copy.12.inten, bf16[2,256,256]{2,1,0:T(8,128)(2,1)S(1)} %copy-done.5, bf16[2,256,256]{2,1,0:T(8,128)(2,1)S(1)} %copy-done.6, f32[2,520,128]{2,1,0:T(8,128)S(1)} %copy-done.4), custom_call_target="tpu_custom_call" | custom-call | flops 1610612736 | bytes 3145728 | tf_op jit(solution)/shard_map/columns/pallas_call | solution.py:354
  51.4 0.0 collective-permute-done.c2
  51.4 0.0 collective-permute-done.1.c1
  51.4 0.0 collective-permute-done.2.c3
  51.4 0.0 copy-start.1
  51.4 0.0 copy-start.2
  51.4 0.0 copy-start.3
  51.4 48.2 %all_to_all.10 = f32[512,4,128]{2,1,0:T(4,128)S(1)} all-to-all(f32[512,4,128]{2,1,0:T(4,128)S(1)} %bitcast.16), channel_id=1, replica_groups={{0,128,256,384,2,130,258,386,4,132,260,388,6,134,262,390,8,136,264,392,..., dimensions={0} | all-to-all | bytes 2097152 | tf_op jit(solution)/shard_map/all_to_all | solution.py:359
  99.6 0.0 copy-done.1
  99.6 0.0 copy-done.2
  99.6 0.0 copy-done.3
  99.6 0.0 copy-start
  99.6 1.1 rows_back.1.own
  100.7 3.1 %collective-permute-start.5 = (f32[2,8,4096]{2,1,0:T(8,128)S(1)}, f32[2,8,4096]{2,1,0:T(8,128)S(1)}, u32[]{:S(2)}, u32[]{:S(2)}) collective-permute-start(f32[2,8,4096]{2,1,0:T(8,128)S(1)} %rows_back.1.own), channel_id=1, source_target_pairs={{0,1},{1,0},{2,3},{3,2},{4,5},{5,4},{6,7},{7,6},{8,9},{9,8},{10,11... | collective-permute-start | bytes 786440 | tf_op jit(solution)/shard_map/ppermute | solution.py:371
  103.8 2.1 %collective-permute-start.3 = (f32[2,8,4096]{2,1,0:T(8,128)S(1)}, f32[2,8,4096]{2,1,0:T(8,128)S(1)}, u32[]{:S(2)}, u32[]{:S(2)}) collective-permute-start(f32[2,8,4096]{2,1,0:T(8,128)S(1)} %rows_back.1.own), channel_id=1, source_target_pairs={{0,128},{1,385},{2,130},{3,387},{4,132},{5,389},{6,134},{7,391},{8... | collective-permute-start | bytes 786440 | tf_op jit(solution)/shard_map/ppermute | solution.py:370
  105.8 0.0 collective-permute-done.5
  105.8 3.9 %collective-permute-start.6 = (f32[2,8,4096]{2,1,0:T(8,128)S(1)}, f32[2,8,4096]{2,1,0:T(8,128)S(1)}, u32[]{:S(2)}, u32[]{:S(2)}) collective-permute-start(f32[2,8,4096]{2,1,0:T(8,128)S(1)} %collective-permute-done.5), channel_id=1, source_target_pairs={{0,128},{1,385},{2,130},{3,387},{4,132},{5,389},{6,134},{7,391},{8... | collective-permute-start | bytes 786440 | tf_op jit(solution)/shard_map/ppermute | solution.py:372
  109.7 7.0 %collective-permute-done.3.near = f32[2,8,4096]{2,1,0:T(8,128)S(1)} collective-permute-done((f32[2,8,4096]{2,1,0:T(8,128)S(1)}, f32[2,8,4096]{2,1,0:T(8,128)S(1)}, u32[]{:S(2)}, u32[]{:S(2)}) %collective-permute-start.3) | collective-permute-done | bytes 262176 | tf_op jit(solution)/shard_map/ppermute | solution.py:370
  116.7 1.9 %collective-permute-start.4 = (f32[2,8,4096]{2,1,0:T(8,128)S(1)}, f32[2,8,4096]{2,1,0:T(8,128)S(1)}, u32[]{:S(2)}, u32[]{:S(2)}) collective-permute-start(f32[2,8,4096]{2,1,0:T(8,128)S(1)} %collective-permute-done.3.near), channel_id=1, source_target_pairs={{0,128},{1,385},{2,130},{3,387},{4,132},{5,389},{6,134},{7,391},{8... | collective-permute-start | bytes 786440 | tf_op jit(solution)/shard_map/ppermute | solution.py:373
  118.6 2.1 %collective-permute-done.6 = f32[2,8,4096]{2,1,0:T(8,128)S(1)} collective-permute-done((f32[2,8,4096]{2,1,0:T(8,128)S(1)}, f32[2,8,4096]{2,1,0:T(8,128)S(1)}, u32[]{:S(2)}, u32[]{:S(2)}) %collective-permute-start.6) | collective-permute-done | bytes 262176 | tf_op jit(solution)/shard_map/ppermute | solution.py:372
  120.7 3.5 %collective-permute-start.7 = (f32[2,8,4096]{2,1,0:T(8,128)S(1)}, f32[2,8,4096]{2,1,0:T(8,128)S(1)}, u32[]{:S(2)}, u32[]{:S(2)}) collective-permute-start(f32[2,8,4096]{2,1,0:T(8,128)S(1)} %collective-permute-done.6), channel_id=1, source_target_pairs={{0,1},{1,0},{2,3},{3,2},{4,5},{5,4},{6,7},{7,6},{8,9},{9,8},{10,11... | collective-permute-start | bytes 786440 | tf_op jit(solution)/shard_map/ppermute | solution.py:374
  124.2 0.1 and_select_fusion.masks
  124.3 2.8 %collective-permute-done.4.far = f32[2,8,4096]{2,1,0:T(8,128)S(1)} collective-permute-done((f32[2,8,4096]{2,1,0:T(8,128)S(1)}, f32[2,8,4096]{2,1,0:T(8,128)S(1)}, u32[]{:S(2)}, u32[]{:S(2)}) %collective-permute-start.4) | collective-permute-done | bytes 262176 | tf_op jit(solution)/shard_map/ppermute | solution.py:373
  127.2 0.0 collective-permute-done.7.other
  127.2 0.0 copy-done
  127.2 2.0 %finish.1 = (f32[2,32,4096]{2,1,0:T(8,128)}, f32[2,32,4096]{2,1,0:T(8,128)}) custom-call(s32[4]{0:T(128)S(1)} %and_select_fusion.masks, f32[2,8,4096]{2,1,0:T(8,128)S(1)} %rows_back.1.own, f32[2,8,4096]{2,1,0:T(8,128)S(1)} %collective-permute-done.3.near, f32[2,8,4096]{2,1,0:T(8,128)S(1)} %collective-permute-done.4.far, ...), custom_call_target="tpu_custom_call" | custom-call | flops 1048576 | bytes 3145728 | tf_op jit(solution)/shard_map/finish/pallas_call | solution.py:379
Async XLA Ops:
  5.2 31.5 %copy-start.7 = (f32[1,32,4096]{2,1,0:T(8,128)S(1)}, f32[1,32,4096]{2,1,0:T(8,128)}, u32[]{:S(2)}) copy-start(f32[1,32,4096]{2,1,0:T(8,128)} %param.10) | copy-start | bytes 1572868
  5.3 43.0 %all-to-all-start = ((f32[128,16,128]{2,1,0:T(8,128)}), f32[128,16,128]{2,1,0:T(8,128)S(1)}, u32[]{:S(2)}, u32[]{:S(2)}) async-start(f32[128,16,128]{2,1,0:T(8,128)} %bitcast.18), calls=%async_computation | async-start | bytes 2097152 | tf_op jit(solution)/shard_map/all_to_all | solution.py:350
  19.6 31.7 %collective-permute-start = (s32[8,4096]{1,0:T(8,128)}, s32[8,4096]{1,0:T(8,128)S(1)}, u32[]{:S(2)}, u32[]{:S(2)}) collective-permute-start(s32[8,4096]{1,0:T(8,128)} %get-tuple-element.12), channel_id=1, source_target_pairs={{0,256},{128,384},{256,0},{384,128},{1,257},{129,385},{257,1},{385... | collective-permute-start | bytes 393224 | tf_op jit(solution)/shard_map/ppermute | solution.py:352
  29.4 22.0 %collective-permute-start.1 = (s32[8,4096]{1,0:T(8,128)}, s32[8,4096]{1,0:T(8,128)S(1)}, u32[]{:S(2)}, u32[]{:S(2)}) collective-permute-start(s32[8,4096]{1,0:T(8,128)} %get-tuple-element.13), channel_id=1, source_target_pairs={{0,128},{128,256},{256,384},{384,0},{1,129},{129,257},{257,385},{3... | collective-permute-start | bytes 393224 | tf_op jit(solution)/shard_map/ppermute | solution.py:351
  33.4 18.0 %collective-permute-start.2 = (s32[8,4096]{1,0:T(8,128)}, s32[8,4096]{1,0:T(8,128)S(1)}, u32[]{:S(2)}, u32[]{:S(2)}) collective-permute-start(s32[8,4096]{1,0:T(8,128)} %get-tuple-element.14), channel_id=1, source_target_pairs={{128,0},{256,128},{384,256},{0,384},{129,1},{257,129},{385,257},{1... | collective-permute-start | bytes 393224 | tf_op jit(solution)/shard_map/ppermute | solution.py:353
  37.5 10.7 %copy-start.6 = (bf16[2,256,256]{2,1,0:T(8,128)(2,1)S(1)}, bf16[2,256,256]{2,1,0:T(8,128)(2,1)}, u32[]{:S(2)}) copy-start(bf16[2,256,256]{2,1,0:T(8,128)(2,1)} %constant.53.clone.block) | copy-start | bytes 786436
  38.0 10.3 %copy-start.4 = (f32[2,520,128]{2,1,0:T(8,128)S(1)}, f32[2,520,128]{2,1,0:T(8,128)}, u32[]{:S(2)}) copy-start(f32[2,520,128]{2,1,0:T(8,128)} %constant.55.clone.tw) | copy-start | bytes 1597444
  38.0 10.3 %copy-start.5 = (bf16[2,256,256]{2,1,0:T(8,128)(2,1)S(1)}, bf16[2,256,256]{2,1,0:T(8,128)(2,1)}, u32[]{:S(2)}) copy-start(bf16[2,256,256]{2,1,0:T(8,128)(2,1)} %constant.52.clone.inner) | copy-start | bytes 786436
  51.4 48.2 %copy-start.1 = (bf16[2,256,256]{2,1,0:T(8,128)(2,1)S(1)}, bf16[2,256,256]{2,1,0:T(8,128)(2,1)}, u32[]{:S(2)}) copy-start(bf16[2,256,256]{2,1,0:T(8,128)(2,1)} %constant.51.clone.left) | copy-start | bytes 786436
  51.4 48.2 %copy-start.2 = (s32[8,4096]{1,0:T(8,128)S(1)}, s32[8,4096]{1,0:T(8,128)}, u32[]{:S(2)}) copy-start(s32[8,4096]{1,0:T(8,128)} %get-tuple-element.16.c0) | copy-start | bytes 393220
  51.4 48.2 %copy-start.3 = (f32[2,32,128]{2,1,0:T(8,128)S(1)}, f32[2,32,128]{2,1,0:T(8,128)}, u32[]{:S(2)}) copy-start(f32[2,32,128]{2,1,0:T(8,128)} %constant.54.clone.tw) | copy-start | bytes 98308
  99.6 27.6 %copy-start = (f32[2,32,4096]{2,1,0:T(8,128)S(1)}, f32[2,32,4096]{2,1,0:T(8,128)}, u32[]{:S(2)}) copy-start(f32[2,32,4096]{2,1,0:T(8,128)} %obj.3) | copy-start | bytes 3145732
  100.7 5.1 %collective-permute-start.5 = (f32[2,8,4096]{2,1,0:T(8,128)S(1)}, f32[2,8,4096]{2,1,0:T(8,128)S(1)}, u32[]{:S(2)}, u32[]{:S(2)}) collective-permute-start(f32[2,8,4096]{2,1,0:T(8,128)S(1)} %rows_back.1.own), channel_id=1, source_target_pairs={{0,1},{1,0},{2,3},{3,2},{4,5},{5,4},{6,7},{7,6},{8,9},{9,8},{10,11... | collective-permute-start | bytes 786440 | tf_op jit(solution)/shard_map/ppermute | solution.py:371
  103.8 12.9 %collective-permute-start.3 = (f32[2,8,4096]{2,1,0:T(8,128)S(1)}, f32[2,8,4096]{2,1,0:T(8,128)S(1)}, u32[]{:S(2)}, u32[]{:S(2)}) collective-permute-start(f32[2,8,4096]{2,1,0:T(8,128)S(1)} %rows_back.1.own), channel_id=1, source_target_pairs={{0,128},{1,385},{2,130},{3,387},{4,132},{5,389},{6,134},{7,391},{8... | collective-permute-start | bytes 786440 | tf_op jit(solution)/shard_map/ppermute | solution.py:370
  105.8 14.9 %collective-permute-start.6 = (f32[2,8,4096]{2,1,0:T(8,128)S(1)}, f32[2,8,4096]{2,1,0:T(8,128)S(1)}, u32[]{:S(2)}, u32[]{:S(2)}) collective-permute-start(f32[2,8,4096]{2,1,0:T(8,128)S(1)} %collective-permute-done.5), channel_id=1, source_target_pairs={{0,128},{1,385},{2,130},{3,387},{4,132},{5,389},{6,134},{7,391},{8... | collective-permute-start | bytes 786440 | tf_op jit(solution)/shard_map/ppermute | solution.py:372
  116.7 10.5 %collective-permute-start.4 = (f32[2,8,4096]{2,1,0:T(8,128)S(1)}, f32[2,8,4096]{2,1,0:T(8,128)S(1)}, u32[]{:S(2)}, u32[]{:S(2)}) collective-permute-start(f32[2,8,4096]{2,1,0:T(8,128)S(1)} %collective-permute-done.3.near), channel_id=1, source_target_pairs={{0,128},{1,385},{2,130},{3,387},{4,132},{5,389},{6,134},{7,391},{8... | collective-permute-start | bytes 786440 | tf_op jit(solution)/shard_map/ppermute | solution.py:373
  120.7 6.5 %collective-permute-start.7 = (f32[2,8,4096]{2,1,0:T(8,128)S(1)}, f32[2,8,4096]{2,1,0:T(8,128)S(1)}, u32[]{:S(2)}, u32[]{:S(2)}) collective-permute-start(f32[2,8,4096]{2,1,0:T(8,128)S(1)} %collective-permute-done.6), channel_id=1, source_target_pairs={{0,1},{1,0},{2,3},{3,2},{4,5},{5,4},{6,7},{7,6},{8,9},{9,8},{10,11... | collective-permute-start | bytes 786440 | tf_op jit(solution)/shard_map/ppermute | solution.py:374

commit v7 on v6

--- a/solution.py
+++ b/solution.py
@@ -247,7 +247,7 @@
                 ]
 
 
-def rows_back(index, rec, c0, c1, c2, c3, left, tw, out, mid, ys):
+def rows_back(index, rec, c0, c1, c2, c3, left, tw, out, out_re, out_im, mid, ys):
     for s, code in enumerate((c0, c1, c2, c3)):
         l = lax.rem(index[0] + MASKS - s, MASKS)
         x = jnp.concatenate(
@@ -278,16 +278,19 @@
                 elif s < MASKS - 1:
                     out[ri, :, cols] += v[ri]
                 else:
-                    out[ri, :, cols] = (out[ri, :, cols] + v[ri]) * (1.0 / MASKS)
+                    total = (out[ri, :, cols] + v[ri]) * (1.0 / MASKS)
+                    out[ri, :, cols] = total
+                    (out_re, out_im)[ri][:, cols] = total
 
         fft32(load, store, mid, 1)
 
 
-def finish(masks, own, near, far, other, obj, updated, direction):
-    for i, part in enumerate((own, near, far, other)):
+def finish(masks, own_re, own_im, near_re, near_im, far_re, far_im, other, obj, updated, direction):
+    parts = ((own_re, own_im), (near_re, near_im), (far_re, far_im), (other.at[0], other.at[1]))
+    for i, part in enumerate(parts):
         rows = pl.ds(pl.multiple_of(masks[i] * OCT, OCT), OCT)
         for ri in range(2):
-            value = part[ri]
+            value = part[ri][...]
             direction[ri, rows, :] = value
             updated[ri, rows, :] = obj[ri, rows, :] - step_size * value
 
@@ -357,8 +360,9 @@
     )(rec.reshape(2048, LANES), inten, t["inner"], t["block"], t["col_tw"])
     back, g2, g1, g3 = lax.optimization_barrier((back, g2, g1, g3))
     rec = exchange(back.reshape(512, 4, LANES), ("mask", "rows"), axis_index_groups=[every])
-    part = call(
-        rows_back, "rows_back", sds((2, OCT, N), F32), 8,
+    half = sds((OCT, N), F32)
+    part, own_re, own_im = call(
+        rows_back, "rows_back", (sds((2, OCT, N), F32), half, half), 8,
         [pltpu.VMEM((2, SHORT, OCT, LANES), F32), pltpu.VMEM((256, 256), F32)], 1 << 29, smem=(0,),
     )(index, rec.reshape(2048, LANES), c0, g1, g2, g3, t["left"], t["row_tw"])
     ring = [
@@ -366,18 +370,18 @@
         for m in range(MASKS)
         for r in range(LANES)
     ]
-    swap = [(r, r ^ 1) for r in range(LANES)]
-    near = lax.ppermute(part, ("mask", "rows"), ring)
-    partner = lax.ppermute(part, "rows", swap)
-    passed = lax.ppermute(partner, ("mask", "rows"), ring)
-    far = lax.ppermute(near, ("mask", "rows"), ring)
-    other = lax.ppermute(passed, "rows", swap)
+    both = ("mask", "rows")
+    near_re = lax.ppermute(own_re, both, ring)
+    near_im = lax.ppermute(own_im, both, ring)
+    other = lax.ppermute(part, both, [(b, a) for a, b in ring])
+    far_re = lax.ppermute(near_re, both, ring)
+    far_im = lax.ppermute(near_im, both, ring)
     side = 2 * (lax.axis_index("rows").astype(jnp.int32) % 2) - 1
     me = index[0] + MASKS
     masks = jnp.stack([me, me + side, me + 2, me - side]) % MASKS
     whole = sds((2, SHORT, N), F32)
-    return call(finish, "finish", (whole, whole), 6, [], 1 << 20, smem=(0,))(
-        masks, part, near, far, other, object_field
+    return call(finish, "finish", (whole, whole), 9, [], 1 << 20, smem=(0,))(
+        masks, own_re, own_im, near_re, near_im, far_re, far_im, other, object_field
     )
 
 

time: 132 us -> 128 us (0.970); the launches traced: 129 us -> 127 us
  waiting for transfers between devices: 21.9 us -> 17.5 us
  starting transfers between devices: 45.9 us -> 48.5 us
    ppermute x5, waiting for transfers between devices: 11.9 us -> 7.41 us  [the longest x1 5.36 us: body(): far_re = lax.ppermute(near_re, both, ring)]
    ppermute x5, starting transfers between devices: 14.4 us -> 17 us  [the longest x1 4.23 us: body(): far_re = lax.ppermute(near_re, both, ring)]
  transfers between devices with their start and end apart: 9 -> 9, of which waited for: 4 -> 3; matrix products, arithmetic and copies ran while one was open for 1% -> 1% of each run, Pallas kernels for 2% -> 2%
where the time goes in v7:
time: 128 us; the launch traced here: 127 us
  starting transfers between devices  48.5 us (38%)
  blocking collectives  48.2 us (38%)
  waiting for transfers between devices  17.5 us (14%)
  Pallas kernels  10.7 us (8%)
  local copies, waits for them, and re-layouts  1.42 us (1%)
    all_to_all x1, blocking collectives, body(): exchange(back.reshape(512, 4, LANES), ('mask', 'rows'), axis_index_groups...  48.2 us
    all_to_all x1, starting transfers between devices, body(): exchange(sent.reshape(LANES, 16, LANES), 'rows', axis_index_groups=[order])  14.4 us
    all_to_all x1, waiting for transfers between devices, body(): exchange(sent.reshape(LANES, 16, LANES), 'rows', axis_index_groups=[order])  10 us
    ppermute x1, starting transfers between devices, body(): g2 = lax.ppermute(c2, 'mask', across)  9.73 us
    ppermute x1, waiting for transfers between devices, body(): far_re = lax.ppermute(near_re, both, ring)  5.36 us
    pallas_call x1, Pallas kernels, body(): pl.pallas_call(rows_forward, name='rows_forward', out_shape=(sds((2048, L...  4.6 us
    ppermute x1, starting transfers between devices, body(): far_re = lax.ppermute(near_re, both, ring)  4.23 us
    ppermute x1, starting transfers between devices, body(): g1 = lax.ppermute(c1, 'mask', up)  4.02 us
  transfers between devices with their start and end apart: 9, of which 3 were waited for; matrix products, arithmetic and copies ran while one was open for 1% of the time, Pallas kernels for 2%

profile of v7, /device:TPU:1, one launch (start us, length us, event | category | flops | bytes accessed | tf_op | source)
XLA Modules:
  0.0 127.3 jit_solution(11043494955688156893)
XLA Ops:
  0.6 4.6 %rows_forward.1 = (f32[2048,128]{1,0:T(8,128)}, s32[8,4096]{1,0:T(8,128)}, s32[8,4096]{1,0:T(8,128)}, s32[8,4096]{1,0:T(8,128)}, s32[8,4096]{1,0:T(8,128)}) custom-call(s32[1]{0:T(128)} %bitcast.4.index, f32[2,32,4096]{2,1,0:T(8,128)} %obj.3, s32[1,32,4096]{2,1,0:T(8,128)} %code.1, bf16[2,256,256]{2,1,0:T(8,128)(2,1)} %constant.51.clone.left, ...), custom_call_target="tpu_custom_call" | custom-call | flops 536870912 | bytes 3145728 | tf_op jit(solution)/shard_map/rows_forward/pallas_call | solution.py:326
  5.2 0.0 copy-start.7
  5.3 14.4 %all-to-all-start = ((f32[128,16,128]{2,1,0:T(8,128)}), f32[128,16,128]{2,1,0:T(8,128)S(1)}, u32[]{:S(2)}, u32[]{:S(2)}) async-start(f32[128,16,128]{2,1,0:T(8,128)} %bitcast.18), calls=%async_computation | async-start | bytes 2097152 | tf_op jit(solution)/shard_map/all_to_all | solution.py:353
  19.6 9.7 %collective-permute-start = (s32[8,4096]{1,0:T(8,128)}, s32[8,4096]{1,0:T(8,128)S(1)}, u32[]{:S(2)}, u32[]{:S(2)}) collective-permute-start(s32[8,4096]{1,0:T(8,128)} %get-tuple-element.15), channel_id=1, source_target_pairs={{0,256},{128,384},{256,0},{384,128},{1,257},{129,385},{257,1},{385... | collective-permute-start | bytes 393224 | tf_op jit(solution)/shard_map/ppermute | solution.py:355
  29.4 4.0 %collective-permute-start.1 = (s32[8,4096]{1,0:T(8,128)}, s32[8,4096]{1,0:T(8,128)S(1)}, u32[]{:S(2)}, u32[]{:S(2)}) collective-permute-start(s32[8,4096]{1,0:T(8,128)} %get-tuple-element.16), channel_id=1, source_target_pairs={{0,128},{128,256},{256,384},{384,0},{1,129},{129,257},{257,385},{3... | collective-permute-start | bytes 393224 | tf_op jit(solution)/shard_map/ppermute | solution.py:354
  33.4 3.4 %collective-permute-start.2 = (s32[8,4096]{1,0:T(8,128)}, s32[8,4096]{1,0:T(8,128)S(1)}, u32[]{:S(2)}, u32[]{:S(2)}) collective-permute-start(s32[8,4096]{1,0:T(8,128)} %get-tuple-element.17), channel_id=1, source_target_pairs={{128,0},{256,128},{384,256},{0,384},{129,1},{257,129},{385,257},{1... | collective-permute-start | bytes 393224 | tf_op jit(solution)/shard_map/ppermute | solution.py:356
  36.8 0.0 copy-done.7
  36.8 0.4 reshape.28
  37.1 0.4 copy.14
  37.5 0.0 copy-start.4
  37.6 0.4 reshape.29
  38.0 0.0 copy-start.1
  38.0 0.0 copy-start.3
  38.0 0.2 copy.12.inten
  38.2 10.0 %all-to-all-done = f32[128,16,128]{2,1,0:T(8,128)S(1)} async-done(((f32[128,16,128]{2,1,0:T(8,128)}), f32[128,16,128]{2,1,0:T(8,128)S(1)}, u32[]{:S(2)}, u32[]{:S(2)}) %all-to-all-start) | async-done | bytes 1048608 | tf_op jit(solution)/shard_map/all_to_all | solution.py:353
  48.2 0.0 copy-done.4
  48.2 0.0 copy-done.1
  48.2 0.0 copy-done.3
  48.3 3.1 %columns.1 = f32[2048,128]{1,0:T(8,128)S(1)} custom-call(f32[2048,128]{1,0:T(8,128)S(1)} %bitcast.14, f32[4,256,128]{2,1,0:T(8,128)S(1)} %copy.12.inten, bf16[2,256,256]{2,1,0:T(8,128)(2,1)S(1)} %copy-done.3, bf16[2,256,256]{2,1,0:T(8,128)(2,1)S(1)} %copy-done.4, f32[2,520,128]{2,1,0:T(8,128)S(1)} %copy-done.1), custom_call_target="tpu_custom_call" | custom-call | flops 1610612736 | bytes 3145728 | tf_op jit(solution)/shard_map/columns/pallas_call | solution.py:357
  51.3 0.0 collective-permute-done.c2
  51.3 0.0 collective-permute-done.1.c1
  51.3 0.0 collective-permute-done.2.c3
  51.4 0.0 copy-start.2
  51.4 0.0 copy-start.5
  51.4 0.0 copy-start.6
  51.4 48.2 %all_to_all.10 = f32[512,4,128]{2,1,0:T(4,128)S(1)} all-to-all(f32[512,4,128]{2,1,0:T(4,128)S(1)} %bitcast.15), channel_id=1, replica_groups={{0,128,256,384,2,130,258,386,4,132,260,388,6,134,262,390,8,136,264,392,..., dimensions={0} | all-to-all | bytes 2097152 | tf_op jit(solution)/shard_map/all_to_all | solution.py:362
  99.6 0.0 copy-start
  99.6 0.0 copy-done.2
  99.6 0.0 copy-done.5
  99.6 0.0 copy-done.6
  99.6 1.1 rows_back.1
  100.7 2.9 %collective-permute-start.3 = (f32[8,4096]{1,0:T(8,128)S(1)}, f32[8,4096]{1,0:T(8,128)S(1)}, u32[]{:S(2)}, u32[]{:S(2)}) collective-permute-start(f32[8,4096]{1,0:T(8,128)S(1)} %get-tuple-element.23.own_re), channel_id=1, source_target_pairs={{0,128},{1,385},{2,130},{3,387},{4,132},{5,389},{6,134},{7,391},{8... | collective-permute-start | bytes 393224 | tf_op jit(solution)/shard_map/ppermute | solution.py:374
  103.6 3.0 %collective-permute-start.4 = (f32[8,4096]{1,0:T(8,128)S(1)}, f32[8,4096]{1,0:T(8,128)S(1)}, u32[]{:S(2)}, u32[]{:S(2)}) collective-permute-start(f32[8,4096]{1,0:T(8,128)S(1)} %get-tuple-element.24.own_im), channel_id=1, source_target_pairs={{0,128},{1,385},{2,130},{3,387},{4,132},{5,389},{6,134},{7,391},{8... | collective-permute-start | bytes 393224 | tf_op jit(solution)/shard_map/ppermute | solution.py:375
  106.6 3.2 %collective-permute-start.7 = (f32[2,8,4096]{2,1,0:T(8,128)S(1)}, f32[2,8,4096]{2,1,0:T(8,128)S(1)}, u32[]{:S(2)}, u32[]{:S(2)}) collective-permute-start(f32[2,8,4096]{2,1,0:T(8,128)S(1)} %get-tuple-element.25), channel_id=1, source_target_pairs={{128,0},{385,1},{130,2},{387,3},{132,4},{389,5},{134,6},{391,7},{1... | collective-permute-start | bytes 786440 | tf_op jit(solution)/shard_map/ppermute | solution.py:376
  109.8 0.0 collective-permute-done.3.near_re
  109.8 4.2 %collective-permute-start.5 = (f32[8,4096]{1,0:T(8,128)S(1)}, f32[8,4096]{1,0:T(8,128)S(1)}, u32[]{:S(2)}, u32[]{:S(2)}) collective-permute-start(f32[8,4096]{1,0:T(8,128)S(1)} %collective-permute-done.3.near_re), channel_id=1, source_target_pairs={{0,128},{1,385},{2,130},{3,387},{4,132},{5,389},{6,134},{7,391},{8... | collective-permute-start | bytes 393224 | tf_op jit(solution)/shard_map/ppermute | solution.py:377
  114.0 0.0 collective-permute-done.4.near_im
  114.0 3.7 %collective-permute-start.6 = (f32[8,4096]{1,0:T(8,128)S(1)}, f32[8,4096]{1,0:T(8,128)S(1)}, u32[]{:S(2)}, u32[]{:S(2)}) collective-permute-start(f32[8,4096]{1,0:T(8,128)S(1)} %collective-permute-done.4.near_im), channel_id=1, source_target_pairs={{0,128},{1,385},{2,130},{3,387},{4,132},{5,389},{6,134},{7,391},{8... | collective-permute-start | bytes 393224 | tf_op jit(solution)/shard_map/ppermute | solution.py:378
  117.8 0.1 and_select_fusion.masks
  117.8 5.4 %collective-permute-done.5.far_re = f32[8,4096]{1,0:T(8,128)S(1)} collective-permute-done((f32[8,4096]{1,0:T(8,128)S(1)}, f32[8,4096]{1,0:T(8,128)S(1)}, u32[]{:S(2)}, u32[]{:S(2)}) %collective-permute-start.5) | collective-permute-done | bytes 131104 | tf_op jit(solution)/shard_map/ppermute | solution.py:377
  123.2 2.0 %collective-permute-done.6.far_im = f32[8,4096]{1,0:T(8,128)S(1)} collective-permute-done((f32[8,4096]{1,0:T(8,128)S(1)}, f32[8,4096]{1,0:T(8,128)S(1)}, u32[]{:S(2)}, u32[]{:S(2)}) %collective-permute-start.6) | collective-permute-done | bytes 131104 | tf_op jit(solution)/shard_map/ppermute | solution.py:378
  125.3 0.0 collective-permute-done.7.other
  125.3 0.0 copy-done
  125.3 2.0 %finish.1 = (f32[2,32,4096]{2,1,0:T(8,128)}, f32[2,32,4096]{2,1,0:T(8,128)}) custom-call(s32[4]{0:T(128)S(1)} %and_select_fusion.masks, f32[8,4096]{1,0:T(8,128)S(1)} %get-tuple-element.23.own_re, f32[8,4096]{1,0:T(8,128)S(1)} %get-tuple-element.24.own_im, f32[8,4096]{1,0:T(8,128)S(1)} %collective-permute-done.3.near_re, ...), custom_call_target="tpu_custom_call" | custom-call | flops 1048576 | bytes 3145728 | tf_op jit(solution)/shard_map/finish/pallas_call | solution.py:383
Async XLA Ops:
  5.2 31.5 %copy-start.7 = (f32[1,32,4096]{2,1,0:T(8,128)S(1)}, f32[1,32,4096]{2,1,0:T(8,128)}, u32[]{:S(2)}) copy-start(f32[1,32,4096]{2,1,0:T(8,128)} %param.10) | copy-start | bytes 1572868
  5.3 43.0 %all-to-all-start = ((f32[128,16,128]{2,1,0:T(8,128)}), f32[128,16,128]{2,1,0:T(8,128)S(1)}, u32[]{:S(2)}, u32[]{:S(2)}) async-start(f32[128,16,128]{2,1,0:T(8,128)} %bitcast.18), calls=%async_computation | async-start | bytes 2097152 | tf_op jit(solution)/shard_map/all_to_all | solution.py:353
  19.6 31.7 %collective-permute-start = (s32[8,4096]{1,0:T(8,128)}, s32[8,4096]{1,0:T(8,128)S(1)}, u32[]{:S(2)}, u32[]{:S(2)}) collective-permute-start(s32[8,4096]{1,0:T(8,128)} %get-tuple-element.15), channel_id=1, source_target_pairs={{0,256},{128,384},{256,0},{384,128},{1,257},{129,385},{257,1},{385... | collective-permute-start | bytes 393224 | tf_op jit(solution)/shard_map/ppermute | solution.py:355
  29.4 22.0 %collective-permute-start.1 = (s32[8,4096]{1,0:T(8,128)}, s32[8,4096]{1,0:T(8,128)S(1)}, u32[]{:S(2)}, u32[]{:S(2)}) collective-permute-start(s32[8,4096]{1,0:T(8,128)} %get-tuple-element.16), channel_id=1, source_target_pairs={{0,128},{128,256},{256,384},{384,0},{1,129},{129,257},{257,385},{3... | collective-permute-start | bytes 393224 | tf_op jit(solution)/shard_map/ppermute | solution.py:354
  33.4 18.0 %collective-permute-start.2 = (s32[8,4096]{1,0:T(8,128)}, s32[8,4096]{1,0:T(8,128)S(1)}, u32[]{:S(2)}, u32[]{:S(2)}) collective-permute-start(s32[8,4096]{1,0:T(8,128)} %get-tuple-element.17), channel_id=1, source_target_pairs={{128,0},{256,128},{384,256},{0,384},{129,1},{257,129},{385,257},{1... | collective-permute-start | bytes 393224 | tf_op jit(solution)/shard_map/ppermute | solution.py:356
  37.5 10.7 %copy-start.4 = (bf16[2,256,256]{2,1,0:T(8,128)(2,1)S(1)}, bf16[2,256,256]{2,1,0:T(8,128)(2,1)}, u32[]{:S(2)}) copy-start(bf16[2,256,256]{2,1,0:T(8,128)(2,1)} %constant.53.clone.block) | copy-start | bytes 786436
  38.0 10.3 %copy-start.1 = (f32[2,520,128]{2,1,0:T(8,128)S(1)}, f32[2,520,128]{2,1,0:T(8,128)}, u32[]{:S(2)}) copy-start(f32[2,520,128]{2,1,0:T(8,128)} %constant.55.clone.tw) | copy-start | bytes 1597444
  38.0 10.3 %copy-start.3 = (bf16[2,256,256]{2,1,0:T(8,128)(2,1)S(1)}, bf16[2,256,256]{2,1,0:T(8,128)(2,1)}, u32[]{:S(2)}) copy-start(bf16[2,256,256]{2,1,0:T(8,128)(2,1)} %constant.52.clone.inner) | copy-start | bytes 786436
  51.4 48.2 %copy-start.2 = (bf16[2,256,256]{2,1,0:T(8,128)(2,1)S(1)}, bf16[2,256,256]{2,1,0:T(8,128)(2,1)}, u32[]{:S(2)}) copy-start(bf16[2,256,256]{2,1,0:T(8,128)(2,1)} %constant.51.clone.left) | copy-start | bytes 786436
  51.4 48.2 %copy-start.5 = (f32[2,32,128]{2,1,0:T(8,128)S(1)}, f32[2,32,128]{2,1,0:T(8,128)}, u32[]{:S(2)}) copy-start(f32[2,32,128]{2,1,0:T(8,128)} %constant.54.clone.tw) | copy-start | bytes 98308
  51.4 48.2 %copy-start.6 = (s32[8,4096]{1,0:T(8,128)S(1)}, s32[8,4096]{1,0:T(8,128)}, u32[]{:S(2)}) copy-start(s32[8,4096]{1,0:T(8,128)} %get-tuple-element.19.c0) | copy-start | bytes 393220
  99.6 25.7 %copy-start = (f32[2,32,4096]{2,1,0:T(8,128)S(1)}, f32[2,32,4096]{2,1,0:T(8,128)}, u32[]{:S(2)}) copy-start(f32[2,32,4096]{2,1,0:T(8,128)} %obj.3) | copy-start | bytes 3145732
  100.7 9.1 %collective-permute-start.3 = (f32[8,4096]{1,0:T(8,128)S(1)}, f32[8,4096]{1,0:T(8,128)S(1)}, u32[]{:S(2)}, u32[]{:S(2)}) collective-permute-start(f32[8,4096]{1,0:T(8,128)S(1)} %get-tuple-element.23.own_re), channel_id=1, source_target_pairs={{0,128},{1,385},{2,130},{3,387},{4,132},{5,389},{6,134},{7,391},{8... | collective-permute-start | bytes 393224 | tf_op jit(solution)/shard_map/ppermute | solution.py:374
  103.6 10.4 %collective-permute-start.4 = (f32[8,4096]{1,0:T(8,128)S(1)}, f32[8,4096]{1,0:T(8,128)S(1)}, u32[]{:S(2)}, u32[]{:S(2)}) collective-permute-start(f32[8,4096]{1,0:T(8,128)S(1)} %get-tuple-element.24.own_im), channel_id=1, source_target_pairs={{0,128},{1,385},{2,130},{3,387},{4,132},{5,389},{6,134},{7,391},{8... | collective-permute-start | bytes 393224 | tf_op jit(solution)/shard_map/ppermute | solution.py:375
  106.6 18.6 %collective-permute-start.7 = (f32[2,8,4096]{2,1,0:T(8,128)S(1)}, f32[2,8,4096]{2,1,0:T(8,128)S(1)}, u32[]{:S(2)}, u32[]{:S(2)}) collective-permute-start(f32[2,8,4096]{2,1,0:T(8,128)S(1)} %get-tuple-element.25), channel_id=1, source_target_pairs={{128,0},{385,1},{130,2},{387,3},{132,4},{389,5},{134,6},{391,7},{1... | collective-permute-start | bytes 786440 | tf_op jit(solution)/shard_map/ppermute | solution.py:376
  109.8 13.4 %collective-permute-start.5 = (f32[8,4096]{1,0:T(8,128)S(1)}, f32[8,4096]{1,0:T(8,128)S(1)}, u32[]{:S(2)}, u32[]{:S(2)}) collective-permute-start(f32[8,4096]{1,0:T(8,128)S(1)} %collective-permute-done.3.near_re), channel_id=1, source_target_pairs={{0,128},{1,385},{2,130},{3,387},{4,132},{5,389},{6,134},{7,391},{8... | collective-permute-start | bytes 393224 | tf_op jit(solution)/shard_map/ppermute | solution.py:377
  114.0 11.2 %collective-permute-start.6 = (f32[8,4096]{1,0:T(8,128)S(1)}, f32[8,4096]{1,0:T(8,128)S(1)}, u32[]{:S(2)}, u32[]{:S(2)}) collective-permute-start(f32[8,4096]{1,0:T(8,128)S(1)} %collective-permute-done.4.near_im), channel_id=1, source_target_pairs={{0,128},{1,385},{2,130},{3,387},{4,132},{5,389},{6,134},{7,391},{8... | collective-permute-start | bytes 393224 | tf_op jit(solution)/shard_map/ppermute | solution.py:378

commit v8 on v7

--- a/solution.py
+++ b/solution.py
@@ -285,10 +285,12 @@
         fft32(load, store, mid, 1)
 
 
-def finish(masks, own_re, own_im, near_re, near_im, far_re, far_im, other, obj, updated, direction):
+def finish(index, core, own_re, own_im, near_re, near_im, far_re, far_im, other, obj, updated, direction):
     parts = ((own_re, own_im), (near_re, near_im), (far_re, far_im), (other.at[0], other.at[1]))
-    for i, part in enumerate(parts):
-        rows = pl.ds(pl.multiple_of(masks[i] * OCT, OCT), OCT)
+    side = 2 * lax.rem(core[0], 2) - 1
+    for shift, part in zip((0, side, 2, -side), parts):
+        mask = lax.rem(index[0] + MASKS + shift, MASKS)
+        rows = pl.ds(pl.multiple_of(mask * OCT, OCT), OCT)
         for ri in range(2):
             value = part[ri][...]
             direction[ri, rows, :] = value
@@ -346,13 +348,18 @@
     inten = intensity.reshape(2, 16, 8, 4, LANES).transpose(3, 0, 4, 1, 2).reshape(4, 256, LANES)
     up = [(i, (i + 1) % MASKS) for i in range(MASKS)]
     down = [((i + 1) % MASKS, i) for i in range(MASKS)]
-    across = [(i, (i + 2) % MASKS) for i in range(MASKS)]
+    ring = [
+        (m * LANES + r, (m + 1 - 2 * (r % 2)) % MASKS * LANES + r)
+        for m in range(MASKS)
+        for r in range(LANES)
+    ]
+    both = ("mask", "rows")
     order = [int(i) for i in exchange_order()]
     every = [m * LANES + i for i in order for m in range(MASKS)]
     exchange = functools.partial(lax.all_to_all, split_axis=0, concat_axis=0, tiled=True)
     rec = exchange(sent.reshape(LANES, 16, LANES), "rows", axis_index_groups=[order])
     g1 = lax.ppermute(c1, "mask", up)
-    g2 = lax.ppermute(c2, "mask", across)
+    g2 = lax.ppermute(lax.ppermute(c2, both, ring), both, ring)
     g3 = lax.ppermute(c3, "mask", down)
     back = call(
         columns, "columns", sds((2048, LANES), F32), 5,
@@ -365,23 +372,15 @@
         rows_back, "rows_back", (sds((2, OCT, N), F32), half, half), 8,
         [pltpu.VMEM((2, SHORT, OCT, LANES), F32), pltpu.VMEM((256, 256), F32)], 1 << 29, smem=(0,),
     )(index, rec.reshape(2048, LANES), c0, g1, g2, g3, t["left"], t["row_tw"])
-    ring = [
-        (m * LANES + r, (m + 1 - 2 * (r % 2)) % MASKS * LANES + r)
-        for m in range(MASKS)
-        for r in range(LANES)
-    ]
-    both = ("mask", "rows")
     near_re = lax.ppermute(own_re, both, ring)
     near_im = lax.ppermute(own_im, both, ring)
     other = lax.ppermute(part, both, [(b, a) for a, b in ring])
     far_re = lax.ppermute(near_re, both, ring)
     far_im = lax.ppermute(near_im, both, ring)
-    side = 2 * (lax.axis_index("rows").astype(jnp.int32) % 2) - 1
-    me = index[0] + MASKS
-    masks = jnp.stack([me, me + side, me + 2, me - side]) % MASKS
+    core = lax.axis_index("rows").astype(jnp.int32).reshape(1)
     whole = sds((2, SHORT, N), F32)
-    return call(finish, "finish", (whole, whole), 9, [], 1 << 20, smem=(0,))(
-        masks, own_re, own_im, near_re, near_im, far_re, far_im, other, object_field
+    return call(finish, "finish", (whole, whole), 10, [], 1 << 20, smem=(0, 1))(
+        index, core, own_re, own_im, near_re, near_im, far_re, far_im, other, object_field
     )
 
 

time: 128 us -> 128 us (level)
  starting transfers between devices: 48.5 us -> 50.5 us
  waiting for transfers between devices: 17.5 us -> 15.9 us
    ppermute x1, starting transfers between devices: 3.37 us -> 5.47 us  [body(): g3 = lax.ppermute(c3, 'mask', down)]
    ppermute x1, starting transfers between devices: 4.02 us -> 1.92 us  [body(): g1 = lax.ppermute(c1, 'mask', up)]
    ppermute x1 -> x2, starting transfers between devices: 9.73 us -> 11.7 us  [body(): g2 = lax.ppermute(lax.ppermute(c2, both, ring), both, ring)]
    all_to_all x1, waiting for transfers between devices: 10 us -> 8.34 us  [body(): exchange(sent.reshape(LANES, 16, LANES), 'rows', axis_index_groups=[order])]
  transfers between devices with their start and end apart: 9 -> 10, of which waited for: 3 -> 3; matrix products, arithmetic and copies ran while one was open for 1% -> 1% of each run, Pallas kernels for 2% -> 2%
where the time goes in v8:
time: 128 us; the launch traced here: 127 us
  starting transfers between devices  50.5 us (39%)
  blocking collectives  47.9 us (37%)
  waiting for transfers between devices  15.9 us (12%)
  Pallas kernels  10.2 us (8%)
  local copies, waits for them, and re-layouts  1.42 us (1%)
    all_to_all x1, blocking collectives, body(): exchange(back.reshape(512, 4, LANES), ('mask', 'rows'), axis_index_groups...  47.9 us
    all_to_all x1, starting transfers between devices, body(): exchange(sent.reshape(LANES, 16, LANES), 'rows', axis_index_groups=[order])  14.4 us
    ppermute x2, starting transfers between devices, body(): g2 = lax.ppermute(lax.ppermute(c2, both, ring), both, ring)  11.7 us
    all_to_all x1, waiting for transfers between devices, body(): exchange(sent.reshape(LANES, 16, LANES), 'rows', axis_index_groups=[order])  8.34 us
    ppermute x1, starting transfers between devices, body(): g3 = lax.ppermute(c3, 'mask', down)  5.47 us
    ppermute x1, waiting for transfers between devices, body(): far_re = lax.ppermute(near_re, both, ring)  5.47 us
    pallas_call x1, Pallas kernels, body(): pl.pallas_call(rows_forward, name='rows_forward', out_shape=(sds((2048, L...  4.6 us
    ppermute x1, starting transfers between devices, body(): far_re = lax.ppermute(near_re, both, ring)  4.23 us
  transfers between devices with their start and end apart: 10, of which 3 were waited for; matrix products, arithmetic and copies ran while one was open for 1% of the time, Pallas kernels for 2%

profile of v8, /device:TPU:1, one launch (start us, length us, event | category | flops | bytes accessed | tf_op | source)
XLA Modules:
  0.0 126.7 jit_solution(3878267654464059072)
XLA Ops:
  0.6 4.6 %rows_forward.1 = (f32[2048,128]{1,0:T(8,128)}, s32[8,4096]{1,0:T(8,128)}, s32[8,4096]{1,0:T(8,128)}, s32[8,4096]{1,0:T(8,128)}, s32[8,4096]{1,0:T(8,128)}) custom-call(s32[1]{0:T(128)} %bitcast.index, f32[2,32,4096]{2,1,0:T(8,128)} %obj.3, s32[1,32,4096]{2,1,0:T(8,128)} %code.1, bf16[2,256,256]{2,1,0:T(8,128)(2,1)} %constant.19.clone.left, ...), custom_call_target="tpu_custom_call" | custom-call | flops 536870912 | bytes 3145728 | tf_op jit(solution)/shard_map/rows_forward/pallas_call | solution.py:328
  5.2 0.0 copy-start.7
  5.2 14.4 %all-to-all-start = ((f32[128,16,128]{2,1,0:T(8,128)}), f32[128,16,128]{2,1,0:T(8,128)S(1)}, u32[]{:S(2)}, u32[]{:S(2)}) async-start(f32[128,16,128]{2,1,0:T(8,128)} %bitcast.15), calls=%async_computation | async-start | bytes 2097152 | tf_op jit(solution)/shard_map/all_to_all | solution.py:360
  19.6 9.8 %collective-permute-start = (s32[8,4096]{1,0:T(8,128)}, s32[8,4096]{1,0:T(8,128)}, u32[]{:S(2)}, u32[]{:S(2)}) collective-permute-start(s32[8,4096]{1,0:T(8,128)} %get-tuple-element.15), channel_id=1, source_target_pairs={{0,128},{1,385},{2,130},{3,387},{4,132},{5,389},{6,134},{7,391},{8... | collective-permute-start | bytes 393224 | tf_op jit(solution)/shard_map/ppermute | solution.py:362
  29.4 1.9 %collective-permute-start.2 = (s32[8,4096]{1,0:T(8,128)}, s32[8,4096]{1,0:T(8,128)S(1)}, u32[]{:S(2)}, u32[]{:S(2)}) collective-permute-start(s32[8,4096]{1,0:T(8,128)} %get-tuple-element.16), channel_id=1, source_target_pairs={{0,128},{128,256},{256,384},{384,0},{1,129},{129,257},{257,385},{3... | collective-permute-start | bytes 393224 | tf_op jit(solution)/shard_map/ppermute | solution.py:361
  31.3 5.5 %collective-permute-start.3 = (s32[8,4096]{1,0:T(8,128)}, s32[8,4096]{1,0:T(8,128)S(1)}, u32[]{:S(2)}, u32[]{:S(2)}) collective-permute-start(s32[8,4096]{1,0:T(8,128)} %get-tuple-element.17), channel_id=1, source_target_pairs={{128,0},{256,128},{384,256},{0,384},{129,1},{257,129},{385,257},{1... | collective-permute-start | bytes 393224 | tf_op jit(solution)/shard_map/ppermute | solution.py:363
  36.8 0.0 copy-done.7
  36.8 0.4 reshape.32
  37.2 0.4 copy.14
  37.6 0.0 copy-start.4
  37.6 0.4 reshape.33
  38.0 0.0 copy-start.1
  38.0 0.0 copy-start.3
  38.0 0.2 copy.12.inten
  38.2 0.0 collective-permute-done
  38.2 1.9 %collective-permute-start.1 = (s32[8,4096]{1,0:T(8,128)}, s32[8,4096]{1,0:T(8,128)S(1)}, u32[]{:S(2)}, u32[]{:S(2)}) collective-permute-start(s32[8,4096]{1,0:T(8,128)} %collective-permute-done), channel_id=1, source_target_pairs={{0,128},{1,385},{2,130},{3,387},{4,132},{5,389},{6,134},{7,391},{8... | collective-permute-start | bytes 393224 | tf_op jit(solution)/shard_map/ppermute | solution.py:362
  40.2 8.3 %all-to-all-done = f32[128,16,128]{2,1,0:T(8,128)S(1)} async-done(((f32[128,16,128]{2,1,0:T(8,128)}), f32[128,16,128]{2,1,0:T(8,128)S(1)}, u32[]{:S(2)}, u32[]{:S(2)}) %all-to-all-start) | async-done | bytes 1048608 | tf_op jit(solution)/shard_map/all_to_all | solution.py:360
  48.5 0.0 copy-done.4
  48.5 0.0 copy-done.1
  48.5 0.0 copy-done.3
  48.5 3.1 %columns.1 = f32[2048,128]{1,0:T(8,128)S(1)} custom-call(f32[2048,128]{1,0:T(8,128)S(1)} %bitcast.11, f32[4,256,128]{2,1,0:T(8,128)S(1)} %copy.12.inten, bf16[2,256,256]{2,1,0:T(8,128)(2,1)S(1)} %copy-done.3, bf16[2,256,256]{2,1,0:T(8,128)(2,1)S(1)} %copy-done.4, f32[2,520,128]{2,1,0:T(8,128)S(1)} %copy-done.1), custom_call_target="tpu_custom_call" | custom-call | flops 1610612736 | bytes 3145728 | tf_op jit(solution)/shard_map/columns/pallas_call | solution.py:364
  51.6 0.0 collective-permute-done.2.c1
  51.6 0.0 collective-permute-done.3.c3
  51.6 0.0 collective-permute-done.1.c2
  51.6 0.0 copy-start.2
  51.6 0.0 copy-start.5
  51.7 0.0 copy-start.6
  51.7 47.9 %all_to_all.10 = f32[512,4,128]{2,1,0:T(4,128)S(1)} all-to-all(f32[512,4,128]{2,1,0:T(4,128)S(1)} %bitcast.12), channel_id=1, replica_groups={{0,128,256,384,2,130,258,386,4,132,260,388,6,134,262,390,8,136,264,392,..., dimensions={0} | all-to-all | bytes 2097152 | tf_op jit(solution)/shard_map/all_to_all | solution.py:369
  99.6 0.0 copy-start
  99.6 0.0 copy-done.2
  99.6 0.0 copy-done.5
  99.6 0.0 copy-done.6
  99.6 1.1 rows_back.1
  100.7 2.9 %collective-permute-start.4 = (f32[8,4096]{1,0:T(8,128)S(1)}, f32[8,4096]{1,0:T(8,128)S(1)}, u32[]{:S(2)}, u32[]{:S(2)}) collective-permute-start(f32[8,4096]{1,0:T(8,128)S(1)} %get-tuple-element.23.own_re), channel_id=1, source_target_pairs={{0,128},{1,385},{2,130},{3,387},{4,132},{5,389},{6,134},{7,391},{8... | collective-permute-start | bytes 393224 | tf_op jit(solution)/shard_map/ppermute | solution.py:375
  103.6 3.0 %collective-permute-start.5 = (f32[8,4096]{1,0:T(8,128)S(1)}, f32[8,4096]{1,0:T(8,128)S(1)}, u32[]{:S(2)}, u32[]{:S(2)}) collective-permute-start(f32[8,4096]{1,0:T(8,128)S(1)} %get-tuple-element.24.own_im), channel_id=1, source_target_pairs={{0,128},{1,385},{2,130},{3,387},{4,132},{5,389},{6,134},{7,391},{8... | collective-permute-start | bytes 393224 | tf_op jit(solution)/shard_map/ppermute | solution.py:376
  106.6 3.2 %collective-permute-start.8 = (f32[2,8,4096]{2,1,0:T(8,128)S(1)}, f32[2,8,4096]{2,1,0:T(8,128)S(1)}, u32[]{:S(2)}, u32[]{:S(2)}) collective-permute-start(f32[2,8,4096]{2,1,0:T(8,128)S(1)} %get-tuple-element.25), channel_id=1, source_target_pairs={{128,0},{385,1},{130,2},{387,3},{132,4},{389,5},{134,6},{391,7},{1... | collective-permute-start | bytes 786440 | tf_op jit(solution)/shard_map/ppermute | solution.py:377
  109.8 0.0 collective-permute-done.4.near_re
  109.8 4.2 %collective-permute-start.6 = (f32[8,4096]{1,0:T(8,128)S(1)}, f32[8,4096]{1,0:T(8,128)S(1)}, u32[]{:S(2)}, u32[]{:S(2)}) collective-permute-start(f32[8,4096]{1,0:T(8,128)S(1)} %collective-permute-done.4.near_re), channel_id=1, source_target_pairs={{0,128},{1,385},{2,130},{3,387},{4,132},{5,389},{6,134},{7,391},{8... | collective-permute-start | bytes 393224 | tf_op jit(solution)/shard_map/ppermute | solution.py:378
  114.0 0.0 collective-permute-done.5.near_im
  114.1 3.7 %collective-permute-start.7 = (f32[8,4096]{1,0:T(8,128)S(1)}, f32[8,4096]{1,0:T(8,128)S(1)}, u32[]{:S(2)}, u32[]{:S(2)}) collective-permute-start(f32[8,4096]{1,0:T(8,128)S(1)} %collective-permute-done.5.near_im), channel_id=1, source_target_pairs={{0,128},{1,385},{2,130},{3,387},{4,132},{5,389},{6,134},{7,391},{8... | collective-permute-start | bytes 393224 | tf_op jit(solution)/shard_map/ppermute | solution.py:379
  117.8 5.5 %collective-permute-done.6.far_re = f32[8,4096]{1,0:T(8,128)S(1)} collective-permute-done((f32[8,4096]{1,0:T(8,128)S(1)}, f32[8,4096]{1,0:T(8,128)S(1)}, u32[]{:S(2)}, u32[]{:S(2)}) %collective-permute-start.6) | collective-permute-done | bytes 131104 | tf_op jit(solution)/shard_map/ppermute | solution.py:378
  123.2 2.0 %collective-permute-done.7.far_im = f32[8,4096]{1,0:T(8,128)S(1)} collective-permute-done((f32[8,4096]{1,0:T(8,128)S(1)}, f32[8,4096]{1,0:T(8,128)S(1)}, u32[]{:S(2)}, u32[]{:S(2)}) %collective-permute-start.7) | collective-permute-done | bytes 131104 | tf_op jit(solution)/shard_map/ppermute | solution.py:379
  125.3 0.0 collective-permute-done.8.other
  125.3 0.0 copy-done
  125.3 1.5 %finish.1 = (f32[2,32,4096]{2,1,0:T(8,128)}, f32[2,32,4096]{2,1,0:T(8,128)}) custom-call(s32[1]{0:T(128)} %bitcast.index, s32[1]{0:T(128)} %bitcast.1.core, f32[8,4096]{1,0:T(8,128)S(1)} %get-tuple-element.23.own_re, f32[8,4096]{1,0:T(8,128)S(1)} %get-tuple-element.24.own_im, f32[8,4096]{1,0:T(8,128)S(1)} %collective-permute-done.4.near_re, ...), custom_call_target="tpu_custom_call" | custom-call | flops 1048576 | bytes 3145728 | tf_op jit(solution)/shard_map/finish/pallas_call | solution.py:382
Async XLA Ops:
  5.2 31.6 %copy-start.7 = (f32[1,32,4096]{2,1,0:T(8,128)S(1)}, f32[1,32,4096]{2,1,0:T(8,128)}, u32[]{:S(2)}) copy-start(f32[1,32,4096]{2,1,0:T(8,128)} %param.10) | copy-start | bytes 1572868
  5.2 43.3 %all-to-all-start = ((f32[128,16,128]{2,1,0:T(8,128)}), f32[128,16,128]{2,1,0:T(8,128)S(1)}, u32[]{:S(2)}, u32[]{:S(2)}) async-start(f32[128,16,128]{2,1,0:T(8,128)} %bitcast.15), calls=%async_computation | async-start | bytes 2097152 | tf_op jit(solution)/shard_map/all_to_all | solution.py:360
  19.6 18.6 %collective-permute-start = (s32[8,4096]{1,0:T(8,128)}, s32[8,4096]{1,0:T(8,128)}, u32[]{:S(2)}, u32[]{:S(2)}) collective-permute-start(s32[8,4096]{1,0:T(8,128)} %get-tuple-element.15), channel_id=1, source_target_pairs={{0,128},{1,385},{2,130},{3,387},{4,132},{5,389},{6,134},{7,391},{8... | collective-permute-start | bytes 393224 | tf_op jit(solution)/shard_map/ppermute | solution.py:362
  29.4 22.2 %collective-permute-start.2 = (s32[8,4096]{1,0:T(8,128)}, s32[8,4096]{1,0:T(8,128)S(1)}, u32[]{:S(2)}, u32[]{:S(2)}) collective-permute-start(s32[8,4096]{1,0:T(8,128)} %get-tuple-element.16), channel_id=1, source_target_pairs={{0,128},{128,256},{256,384},{384,0},{1,129},{129,257},{257,385},{3... | collective-permute-start | bytes 393224 | tf_op jit(solution)/shard_map/ppermute | solution.py:361
  31.3 20.3 %collective-permute-start.3 = (s32[8,4096]{1,0:T(8,128)}, s32[8,4096]{1,0:T(8,128)S(1)}, u32[]{:S(2)}, u32[]{:S(2)}) collective-permute-start(s32[8,4096]{1,0:T(8,128)} %get-tuple-element.17), channel_id=1, source_target_pairs={{128,0},{256,128},{384,256},{0,384},{129,1},{257,129},{385,257},{1... | collective-permute-start | bytes 393224 | tf_op jit(solution)/shard_map/ppermute | solution.py:363
  37.6 10.9 %copy-start.4 = (bf16[2,256,256]{2,1,0:T(8,128)(2,1)S(1)}, bf16[2,256,256]{2,1,0:T(8,128)(2,1)}, u32[]{:S(2)}) copy-start(bf16[2,256,256]{2,1,0:T(8,128)(2,1)} %constant.21.clone.block) | copy-start | bytes 786436
  38.0 10.5 %copy-start.1 = (f32[2,520,128]{2,1,0:T(8,128)S(1)}, f32[2,520,128]{2,1,0:T(8,128)}, u32[]{:S(2)}) copy-start(f32[2,520,128]{2,1,0:T(8,128)} %constant.23.clone.tw) | copy-start | bytes 1597444
  38.0 10.5 %copy-start.3 = (bf16[2,256,256]{2,1,0:T(8,128)(2,1)S(1)}, bf16[2,256,256]{2,1,0:T(8,128)(2,1)}, u32[]{:S(2)}) copy-start(bf16[2,256,256]{2,1,0:T(8,128)(2,1)} %constant.20.clone.inner) | copy-start | bytes 786436
  38.2 13.4 %collective-permute-start.1 = (s32[8,4096]{1,0:T(8,128)}, s32[8,4096]{1,0:T(8,128)S(1)}, u32[]{:S(2)}, u32[]{:S(2)}) collective-permute-start(s32[8,4096]{1,0:T(8,128)} %collective-permute-done), channel_id=1, source_target_pairs={{0,128},{1,385},{2,130},{3,387},{4,132},{5,389},{6,134},{7,391},{8... | collective-permute-start | bytes 393224 | tf_op jit(solution)/shard_map/ppermute | solution.py:362
  51.6 48.0 %copy-start.2 = (bf16[2,256,256]{2,1,0:T(8,128)(2,1)S(1)}, bf16[2,256,256]{2,1,0:T(8,128)(2,1)}, u32[]{:S(2)}) copy-start(bf16[2,256,256]{2,1,0:T(8,128)(2,1)} %constant.19.clone.left) | copy-start | bytes 786436
  51.6 47.9 %copy-start.5 = (f32[2,32,128]{2,1,0:T(8,128)S(1)}, f32[2,32,128]{2,1,0:T(8,128)}, u32[]{:S(2)}) copy-start(f32[2,32,128]{2,1,0:T(8,128)} %constant.22.clone.tw) | copy-start | bytes 98308
  51.7 47.9 %copy-start.6 = (s32[8,4096]{1,0:T(8,128)S(1)}, s32[8,4096]{1,0:T(8,128)}, u32[]{:S(2)}) copy-start(s32[8,4096]{1,0:T(8,128)} %get-tuple-element.19.c0) | copy-start | bytes 393220
  99.6 25.7 %copy-start = (f32[2,32,4096]{2,1,0:T(8,128)S(1)}, f32[2,32,4096]{2,1,0:T(8,128)}, u32[]{:S(2)}) copy-start(f32[2,32,4096]{2,1,0:T(8,128)} %obj.3) | copy-start | bytes 3145732
  100.7 9.1 %collective-permute-start.4 = (f32[8,4096]{1,0:T(8,128)S(1)}, f32[8,4096]{1,0:T(8,128)S(1)}, u32[]{:S(2)}, u32[]{:S(2)}) collective-permute-start(f32[8,4096]{1,0:T(8,128)S(1)} %get-tuple-element.23.own_re), channel_id=1, source_target_pairs={{0,128},{1,385},{2,130},{3,387},{4,132},{5,389},{6,134},{7,391},{8... | collective-permute-start | bytes 393224 | tf_op jit(solution)/shard_map/ppermute | solution.py:375
  103.6 10.5 %collective-permute-start.5 = (f32[8,4096]{1,0:T(8,128)S(1)}, f32[8,4096]{1,0:T(8,128)S(1)}, u32[]{:S(2)}, u32[]{:S(2)}) collective-permute-start(f32[8,4096]{1,0:T(8,128)S(1)} %get-tuple-element.24.own_im), channel_id=1, source_target_pairs={{0,128},{1,385},{2,130},{3,387},{4,132},{5,389},{6,134},{7,391},{8... | collective-permute-start | bytes 393224 | tf_op jit(solution)/shard_map/ppermute | solution.py:376
  106.6 18.6 %collective-permute-start.8 = (f32[2,8,4096]{2,1,0:T(8,128)S(1)}, f32[2,8,4096]{2,1,0:T(8,128)S(1)}, u32[]{:S(2)}, u32[]{:S(2)}) collective-permute-start(f32[2,8,4096]{2,1,0:T(8,128)S(1)} %get-tuple-element.25), channel_id=1, source_target_pairs={{128,0},{385,1},{130,2},{387,3},{132,4},{389,5},{134,6},{391,7},{1... | collective-permute-start | bytes 786440 | tf_op jit(solution)/shard_map/ppermute | solution.py:377
  109.8 13.4 %collective-permute-start.6 = (f32[8,4096]{1,0:T(8,128)S(1)}, f32[8,4096]{1,0:T(8,128)S(1)}, u32[]{:S(2)}, u32[]{:S(2)}) collective-permute-start(f32[8,4096]{1,0:T(8,128)S(1)} %collective-permute-done.4.near_re), channel_id=1, source_target_pairs={{0,128},{1,385},{2,130},{3,387},{4,132},{5,389},{6,134},{7,391},{8... | collective-permute-start | bytes 393224 | tf_op jit(solution)/shard_map/ppermute | solution.py:378
  114.1 11.2 %collective-permute-start.7 = (f32[8,4096]{1,0:T(8,128)S(1)}, f32[8,4096]{1,0:T(8,128)S(1)}, u32[]{:S(2)}, u32[]{:S(2)}) collective-permute-start(f32[8,4096]{1,0:T(8,128)S(1)} %collective-permute-done.5.near_im), channel_id=1, source_target_pairs={{0,128},{1,385},{2,130},{3,387},{4,132},{5,389},{6,134},{7,391},{8... | collective-permute-start | bytes 393224 | tf_op jit(solution)/shard_map/ppermute | solution.py:379

commit v9 on v8

--- a/solution.py
+++ b/solution.py
@@ -144,14 +144,20 @@
     return jnp.where(code >= 2, -a, a), jnp.where((code == 1) | (code == 2), -b, b)
 
 
-def rows_forward(index, obj, code, left, tw, out, c0, c2, c1, c3, mid, xs):
+def rows_forward(index, obj, code, every, left, tw, out, c0, c2, c1, c3, mid, xs, buf, sems, code_sems):
     m = pl.program_id(0)
-    shift = lax.rem(m + MASKS - index[0], MASKS)
-    for s, c in enumerate((c0, c1, c2, c3)):
-
-        @pl.when(shift == s)
-        def _():
-            c[...] = code[0]
+
+    def code_copy(s, c):
+        row = pl.multiple_of(lax.rem(index[0] + s, MASKS) * OCT, OCT)
+        return pltpu.make_async_copy(every.at[0, pl.ds(row, OCT), :], c, code_sems.at[s])
+
+    def out_copy(step):
+        return pltpu.make_async_copy(buf.at[step], out.at[:, step], sems.at[step])
+
+    @pl.when(m == 0)
+    def _():
+        for s, c in enumerate((c0, c1, c2, c3)):
+            code_copy(s, c).start()
 
     def load(p):
         cols = slice(LANES * p, LANES * p + LANES)
@@ -166,9 +172,17 @@
     y = dot3((left[0], left[1]), split(xs[...]), NT)
     for ri in range(2):
         for h in range(2):
-            out[pl.ds(ri * 8 + 2 * m + h, LANES, stride=16), :] = y[
+            buf[m, :, ri * 2 + h, :] = y[
                 LANES * ri : LANES * ri + LANES, LANES * h : LANES * h + LANES
             ]
+    out_copy(m).start()
+
+    @pl.when(m == MASKS - 1)
+    def _():
+        for s, c in enumerate((c0, c1, c2, c3)):
+            code_copy(s, c).wait()
+        for step in range(MASKS):
+            out_copy(step).wait()
 
 
 def columns(rec, inten, inner, block, tw, out, s):
@@ -180,7 +194,7 @@
         x = jnp.concatenate(
             [
                 jnp.concatenate(
-                    [rec[pl.ds(ri * 8 + 2 * m + h, LANES, stride=16), :] for h in range(2)], axis=1
+                    [rec[pl.ds(m * 4 + ri * 2 + h, LANES, stride=16), :] for h in range(2)], axis=1
                 )
                 for ri in range(2)
             ],
@@ -285,16 +299,36 @@
         fft32(load, store, mid, 1)
 
 
-def finish(index, core, own_re, own_im, near_re, near_im, far_re, far_im, other, obj, updated, direction):
-    parts = ((own_re, own_im), (near_re, near_im), (far_re, far_im), (other.at[0], other.at[1]))
-    side = 2 * lax.rem(core[0], 2) - 1
-    for shift, part in zip((0, side, 2, -side), parts):
-        mask = lax.rem(index[0] + MASKS + shift, MASKS)
+def write_rows(masks, parts, obj, updated, direction, bufs, sems):
+    copies = []
+    for i, (mask, part) in enumerate(zip(masks, parts)):
         rows = pl.ds(pl.multiple_of(mask * OCT, OCT), OCT)
         for ri in range(2):
             value = part[ri][...]
-            direction[ri, rows, :] = value
-            updated[ri, rows, :] = obj[ri, rows, :] - step_size * value
+            bufs[i, 0, ri] = obj[ri, rows, :] - step_size * value
+            bufs[i, 1, ri] = value
+        for j, out in enumerate((updated, direction)):
+            copy = pltpu.make_async_copy(bufs.at[i, j], out.at[:, rows, :], sems.at[i, j])
+            copy.start()
+            copies.append(copy)
+    for copy in copies:
+        copy.wait()
+
+
+def side_of(core):
+    return 2 * lax.rem(core[0], 2) - 1
+
+
+def finish_first(index, core, own_re, own_im, near_re, near_im, obj, updated, direction, bufs, sems):
+    masks = [lax.rem(index[0] + MASKS + shift, MASKS) for shift in (0, side_of(core))]
+    parts = ((own_re, own_im), (near_re, near_im))
+    write_rows(masks, parts, obj, updated, direction, bufs, sems)
+
+
+def finish_last(index, core, far_re, far_im, other, obj, _u, _d, updated, direction, bufs, sems):
+    masks = [lax.rem(index[0] + MASKS + shift, MASKS) for shift in (-side_of(core), 2)]
+    parts = ((other.at[0], other.at[1]), (far_re, far_im))
+    write_rows(masks, parts, obj, updated, direction, bufs, sems)
 
 
 VM = pl.BlockSpec(memory_space=pltpu.VMEM)
@@ -328,23 +362,27 @@
     sent, c0, c2, c1, c3 = pl.pallas_call(
         rows_forward,
         name="rows_forward",
-        out_shape=(sds((2048, LANES), F32),) + (rows8,) * MASKS,
+        out_shape=(sds((LANES, MASKS, 4, LANES), F32),) + (rows8,) * MASKS,
         grid=(MASKS,),
         in_specs=[
             pl.BlockSpec(memory_space=pltpu.SMEM),
             pl.BlockSpec((2, OCT, N), octet),
             pl.BlockSpec((1, OCT, N), octet),
+            pl.BlockSpec(memory_space=pl.ANY),
             pl.BlockSpec((2, 256, 256), lambda m: (0, 0, 0)),
             pl.BlockSpec((2, SHORT, LANES), lambda m: (0, 0, 0)),
         ],
-        out_specs=(pl.BlockSpec((2048, LANES), flat),) + (pl.BlockSpec((OCT, N), flat),) * MASKS,
+        out_specs=(pl.BlockSpec(memory_space=pl.ANY),) * (1 + MASKS),
         scratch_shapes=[
             pltpu.VMEM((2, SHORT, OCT, LANES), F32),
             pltpu.VMEM((256, 256), F32),
+            pltpu.VMEM((MASKS, LANES, 4, LANES), F32),
+            pltpu.SemaphoreType.DMA((MASKS,)),
+            pltpu.SemaphoreType.DMA((MASKS,)),
         ],
         compiler_params=pltpu.CompilerParams(vmem_limit_bytes=60 << 20),
         cost_estimate=pl.CostEstimate(flops=1 << 29, bytes_accessed=3 << 20, transcendentals=0),
-    )(index, object_field, phases, t["left"], t["row_tw"])
+    )(index, object_field, phases, phases, t["left"], t["row_tw"])
     inten = intensity.reshape(2, 16, 8, 4, LANES).transpose(3, 0, 4, 1, 2).reshape(4, 256, LANES)
     up = [(i, (i + 1) % MASKS) for i in range(MASKS)]
     down = [((i + 1) % MASKS, i) for i in range(MASKS)]
@@ -379,9 +417,27 @@
     far_im = lax.ppermute(near_im, both, ring)
     core = lax.axis_index("rows").astype(jnp.int32).reshape(1)
     whole = sds((2, SHORT, N), F32)
-    return call(finish, "finish", (whole, whole), 10, [], 1 << 20, smem=(0, 1))(
-        index, core, own_re, own_im, near_re, near_im, far_re, far_im, other, object_field
+    scalars = [pl.BlockSpec(memory_space=pltpu.SMEM)] * 2
+    anywhere = [pl.BlockSpec(memory_space=pl.ANY)] * 2
+    scratch = [pltpu.VMEM((2, 2, 2, OCT, N), F32), pltpu.SemaphoreType.DMA((2, 2))]
+    cost = pl.CostEstimate(flops=1 << 19, bytes_accessed=2 << 20, transcendentals=0)
+    options = dict(
+        out_shape=(whole, whole),
+        out_specs=anywhere,
+        scratch_shapes=scratch,
+        compiler_params=pltpu.CompilerParams(vmem_limit_bytes=24 << 20),
+        cost_estimate=cost,
     )
+    first = pl.pallas_call(
+        finish_first, name="finish_first", in_specs=scalars + [VM] * 5, **options
+    )(index, core, own_re, own_im, near_re, near_im, object_field)
+    return pl.pallas_call(
+        finish_last,
+        name="finish_last",
+        in_specs=scalars + [VM] * 4 + anywhere,
+        input_output_aliases={6: 0, 7: 1},
+        **options,
+    )(index, core, far_re, far_im, other, object_field, *first)
 
 
 def solution(mesh):

time: 128 us -> 141 us (1.10)
  Pallas kernels: 10.2 us -> 24.4 us
    pallas_call x2 -> x3, Pallas kernels: 6.06 us -> 20.3 us  [the longest x1 18.2 us: body(): pl.pallas_call(rows_forward, name='rows_forward', out_shape=(sds((LANES,...]
  transfers between devices with their start and end apart: 10 -> 10, of which waited for: 3 -> 3; matrix products, arithmetic and copies ran while one was open for 1% -> 1% of each run, Pallas kernels for 2% -> 3%
where the time goes in v9:
time: 141 us; the launch traced here: 140 us
  starting transfers between devices  50.5 us (36%)
  blocking collectives  47.9 us (34%)
  Pallas kernels  24.4 us (17%)
  waiting for transfers between devices  14.8 us (10%)
  local copies, waits for them, and re-layouts  1.42 us (1%)
    all_to_all x1, blocking collectives, body(): exchange(back.reshape(512, 4, LANES), ('mask', 'rows'), axis_index_groups...  47.9 us
    pallas_call x1, Pallas kernels, body(): pl.pallas_call(rows_forward, name='rows_forward', out_shape=(sds((LANES,...  18.2 us
    all_to_all x1, starting transfers between devices, body(): exchange(sent.reshape(LANES, 16, LANES), 'rows', axis_index_groups=[order])  14.4 us
    ppermute x2, starting transfers between devices, body(): g2 = lax.ppermute(lax.ppermute(c2, both, ring), both, ring)  11.7 us
    all_to_all x1, waiting for transfers between devices, body(): exchange(sent.reshape(LANES, 16, LANES), 'rows', axis_index_groups=[order])  8.34 us
    ppermute x1, starting transfers between devices, body(): g3 = lax.ppermute(c3, 'mask', down)  5.47 us
    ppermute x1, waiting for transfers between devices, body(): far_re = lax.ppermute(near_re, both, ring)  4.41 us
    ppermute x1, starting transfers between devices, body(): far_re = lax.ppermute(near_re, both, ring)  4.23 us
  transfers between devices with their start and end apart: 10, of which 3 were waited for; matrix products, arithmetic and copies ran while one was open for 1% of the time, Pallas kernels for 3%

profile of v9, /device:TPU:1, one launch (start us, length us, event | category | flops | bytes accessed | tf_op | source)
XLA Modules:
  0.0 139.9 jit_solution(12855857846385882951)
XLA Ops:
  0.6 18.2 %rows_forward.1 = (f32[128,4,4,128]{3,2,1,0:T(4,128)}, s32[8,4096]{1,0:T(8,128)}, s32[8,4096]{1,0:T(8,128)}, s32[8,4096]{1,0:T(8,128)}, s32[8,4096]{1,0:T(8,128)}) custom-call(s32[1]{0:T(128)} %bitcast.index, f32[2,32,4096]{2,1,0:T(8,128)} %obj.5, s32[1,32,4096]{2,1,0:T(8,128)} %every.1, s32[1,32,4096]{2,1,0:T(8,128)} %every.1, ...), custom_call_target="tpu_custom_call" | custom-call | flops 536870912 | bytes 3145728 | tf_op jit(solution)/shard_map/rows_forward/pallas_call | solution.py:362
  18.8 0.0 copy-start.7
  18.9 14.4 %all-to-all-start = ((f32[128,16,128]{2,1,0:T(8,128)}), f32[128,16,128]{2,1,0:T(8,128)S(1)}, u32[]{:S(2)}, u32[]{:S(2)}) async-start(f32[128,16,128]{2,1,0:T(8,128)} %bitcast.15), calls=%async_computation | async-start | bytes 2097152 | tf_op jit(solution)/shard_map/all_to_all | solution.py:398
  33.2 9.8 %collective-permute-start = (s32[8,4096]{1,0:T(8,128)}, s32[8,4096]{1,0:T(8,128)}, u32[]{:S(2)}, u32[]{:S(2)}) collective-permute-start(s32[8,4096]{1,0:T(8,128)} %get-tuple-element.17), channel_id=1, source_target_pairs={{0,128},{1,385},{2,130},{3,387},{4,132},{5,389},{6,134},{7,391},{8... | collective-permute-start | bytes 393224 | tf_op jit(solution)/shard_map/ppermute | solution.py:400
  43.0 1.9 %collective-permute-start.2 = (s32[8,4096]{1,0:T(8,128)}, s32[8,4096]{1,0:T(8,128)S(1)}, u32[]{:S(2)}, u32[]{:S(2)}) collective-permute-start(s32[8,4096]{1,0:T(8,128)} %get-tuple-element.18), channel_id=1, source_target_pairs={{0,128},{128,256},{256,384},{384,0},{1,129},{129,257},{257,385},{3... | collective-permute-start | bytes 393224 | tf_op jit(solution)/shard_map/ppermute | solution.py:399
  44.9 5.5 %collective-permute-start.3 = (s32[8,4096]{1,0:T(8,128)}, s32[8,4096]{1,0:T(8,128)S(1)}, u32[]{:S(2)}, u32[]{:S(2)}) collective-permute-start(s32[8,4096]{1,0:T(8,128)} %get-tuple-element.19), channel_id=1, source_target_pairs={{128,0},{256,128},{384,256},{0,384},{129,1},{257,129},{385,257},{1... | collective-permute-start | bytes 393224 | tf_op jit(solution)/shard_map/ppermute | solution.py:401
  50.4 0.0 copy-done.7
  50.4 0.4 reshape.32
  50.8 0.4 copy.16
  51.2 0.0 copy-start.6
  51.2 0.4 reshape.33
  51.6 0.0 copy-start.4
  51.6 0.0 copy-start.5
  51.6 0.2 copy.14.inten
  51.8 0.0 collective-permute-done
  51.9 1.9 %collective-permute-start.1 = (s32[8,4096]{1,0:T(8,128)}, s32[8,4096]{1,0:T(8,128)S(1)}, u32[]{:S(2)}, u32[]{:S(2)}) collective-permute-start(s32[8,4096]{1,0:T(8,128)} %collective-permute-done), channel_id=1, source_target_pairs={{0,128},{1,385},{2,130},{3,387},{4,132},{5,389},{6,134},{7,391},{8... | collective-permute-start | bytes 393224 | tf_op jit(solution)/shard_map/ppermute | solution.py:400
  53.8 8.3 %all-to-all-done = f32[128,16,128]{2,1,0:T(8,128)S(1)} async-done(((f32[128,16,128]{2,1,0:T(8,128)}), f32[128,16,128]{2,1,0:T(8,128)S(1)}, u32[]{:S(2)}, u32[]{:S(2)}) %all-to-all-start) | async-done | bytes 1048608 | tf_op jit(solution)/shard_map/all_to_all | solution.py:398
  62.1 0.0 copy-done.6
  62.1 0.0 copy-done.4
  62.1 0.0 copy-done.5
  62.1 3.1 %columns.1 = f32[2048,128]{1,0:T(8,128)S(1)} custom-call(f32[2048,128]{1,0:T(8,128)S(1)} %bitcast.11, f32[4,256,128]{2,1,0:T(8,128)S(1)} %copy.14.inten, bf16[2,256,256]{2,1,0:T(8,128)(2,1)S(1)} %copy-done.6, bf16[2,256,256]{2,1,0:T(8,128)(2,1)S(1)} %copy-done.5, f32[2,520,128]{2,1,0:T(8,128)S(1)} %copy-done.4), custom_call_target="tpu_custom_call" | custom-call | flops 1610612736 | bytes 3145728 | tf_op jit(solution)/shard_map/columns/pallas_call | solution.py:402
  65.2 0.0 collective-permute-done.2.c1
  65.2 0.0 collective-permute-done.3.c3
  65.2 0.0 collective-permute-done.1.c2
  65.2 0.0 copy-start.1
  65.3 0.0 copy-start.2
  65.3 0.0 copy-start.3
  65.3 47.9 %all_to_all.10 = f32[512,4,128]{2,1,0:T(4,128)S(1)} all-to-all(f32[512,4,128]{2,1,0:T(4,128)S(1)} %bitcast.12), channel_id=1, replica_groups={{0,128,256,384,2,130,258,386,4,132,260,388,6,134,262,390,8,136,264,392,..., dimensions={0} | all-to-all | bytes 2097152 | tf_op jit(solution)/shard_map/all_to_all | solution.py:407
  113.2 0.0 copy-start
  113.2 0.0 copy-done.1
  113.2 0.0 copy-done.2
  113.2 0.0 copy-done.3
  113.2 1.1 rows_back.1
  114.3 2.9 %collective-permute-start.4 = (f32[8,4096]{1,0:T(8,128)S(1)}, f32[8,4096]{1,0:T(8,128)S(1)}, u32[]{:S(2)}, u32[]{:S(2)}) collective-permute-start(f32[8,4096]{1,0:T(8,128)S(1)} %get-tuple-element.25.own_re), channel_id=1, source_target_pairs={{0,128},{1,385},{2,130},{3,387},{4,132},{5,389},{6,134},{7,391},{8... | collective-permute-start | bytes 393224 | tf_op jit(solution)/shard_map/ppermute | solution.py:413
  117.2 3.0 %collective-permute-start.6 = (f32[8,4096]{1,0:T(8,128)S(1)}, f32[8,4096]{1,0:T(8,128)S(1)}, u32[]{:S(2)}, u32[]{:S(2)}) collective-permute-start(f32[8,4096]{1,0:T(8,128)S(1)} %get-tuple-element.26.own_im), channel_id=1, source_target_pairs={{0,128},{1,385},{2,130},{3,387},{4,132},{5,389},{6,134},{7,391},{8... | collective-permute-start | bytes 393224 | tf_op jit(solution)/shard_map/ppermute | solution.py:414
  120.2 3.2 %collective-permute-start.8 = (f32[2,8,4096]{2,1,0:T(8,128)S(1)}, f32[2,8,4096]{2,1,0:T(8,128)S(1)}, u32[]{:S(2)}, u32[]{:S(2)}) collective-permute-start(f32[2,8,4096]{2,1,0:T(8,128)S(1)} %get-tuple-element.27), channel_id=1, source_target_pairs={{128,0},{385,1},{130,2},{387,3},{132,4},{389,5},{134,6},{391,7},{1... | collective-permute-start | bytes 786440 | tf_op jit(solution)/shard_map/ppermute | solution.py:415
  123.4 0.0 collective-permute-done.4.near_re
  123.4 4.2 %collective-permute-start.5 = (f32[8,4096]{1,0:T(8,128)S(1)}, f32[8,4096]{1,0:T(8,128)S(1)}, u32[]{:S(2)}, u32[]{:S(2)}) collective-permute-start(f32[8,4096]{1,0:T(8,128)S(1)} %collective-permute-done.4.near_re), channel_id=1, source_target_pairs={{0,128},{1,385},{2,130},{3,387},{4,132},{5,389},{6,134},{7,391},{8... | collective-permute-start | bytes 393224 | tf_op jit(solution)/shard_map/ppermute | solution.py:416
  127.6 0.0 collective-permute-done.6.near_im
  127.7 3.7 %collective-permute-start.7 = (f32[8,4096]{1,0:T(8,128)S(1)}, f32[8,4096]{1,0:T(8,128)S(1)}, u32[]{:S(2)}, u32[]{:S(2)}) collective-permute-start(f32[8,4096]{1,0:T(8,128)S(1)} %collective-permute-done.6.near_im), channel_id=1, source_target_pairs={{0,128},{1,385},{2,130},{3,387},{4,132},{5,389},{6,134},{7,391},{8... | collective-permute-start | bytes 393224 | tf_op jit(solution)/shard_map/ppermute | solution.py:417
  131.4 0.0 copy-done
  131.4 1.0 finish_first.1
  132.4 4.4 %collective-permute-done.5.far_re = f32[8,4096]{1,0:T(8,128)S(1)} collective-permute-done((f32[8,4096]{1,0:T(8,128)S(1)}, f32[8,4096]{1,0:T(8,128)S(1)}, u32[]{:S(2)}, u32[]{:S(2)}) %collective-permute-start.5) | collective-permute-done | bytes 131104 | tf_op jit(solution)/shard_map/ppermute | solution.py:416
  136.8 2.0 %collective-permute-done.7.far_im = f32[8,4096]{1,0:T(8,128)S(1)} collective-permute-done((f32[8,4096]{1,0:T(8,128)S(1)}, f32[8,4096]{1,0:T(8,128)S(1)}, u32[]{:S(2)}, u32[]{:S(2)}) %collective-permute-start.7) | collective-permute-done | bytes 131104 | tf_op jit(solution)/shard_map/ppermute | solution.py:417
  138.9 0.0 collective-permute-done.8.other
  138.9 1.0 finish_last.1
Async XLA Ops:
  18.8 31.6 %copy-start.7 = (f32[1,32,4096]{2,1,0:T(8,128)S(1)}, f32[1,32,4096]{2,1,0:T(8,128)}, u32[]{:S(2)}) copy-start(f32[1,32,4096]{2,1,0:T(8,128)} %param.10) | copy-start | bytes 1572868
  18.9 43.3 %all-to-all-start = ((f32[128,16,128]{2,1,0:T(8,128)}), f32[128,16,128]{2,1,0:T(8,128)S(1)}, u32[]{:S(2)}, u32[]{:S(2)}) async-start(f32[128,16,128]{2,1,0:T(8,128)} %bitcast.15), calls=%async_computation | async-start | bytes 2097152 | tf_op jit(solution)/shard_map/all_to_all | solution.py:398
  33.2 18.6 %collective-permute-start = (s32[8,4096]{1,0:T(8,128)}, s32[8,4096]{1,0:T(8,128)}, u32[]{:S(2)}, u32[]{:S(2)}) collective-permute-start(s32[8,4096]{1,0:T(8,128)} %get-tuple-element.17), channel_id=1, source_target_pairs={{0,128},{1,385},{2,130},{3,387},{4,132},{5,389},{6,134},{7,391},{8... | collective-permute-start | bytes 393224 | tf_op jit(solution)/shard_map/ppermute | solution.py:400
  43.0 22.2 %collective-permute-start.2 = (s32[8,4096]{1,0:T(8,128)}, s32[8,4096]{1,0:T(8,128)S(1)}, u32[]{:S(2)}, u32[]{:S(2)}) collective-permute-start(s32[8,4096]{1,0:T(8,128)} %get-tuple-element.18), channel_id=1, source_target_pairs={{0,128},{128,256},{256,384},{384,0},{1,129},{129,257},{257,385},{3... | collective-permute-start | bytes 393224 | tf_op jit(solution)/shard_map/ppermute | solution.py:399
  44.9 20.3 %collective-permute-start.3 = (s32[8,4096]{1,0:T(8,128)}, s32[8,4096]{1,0:T(8,128)S(1)}, u32[]{:S(2)}, u32[]{:S(2)}) collective-permute-start(s32[8,4096]{1,0:T(8,128)} %get-tuple-element.19), channel_id=1, source_target_pairs={{128,0},{256,128},{384,256},{0,384},{129,1},{257,129},{385,257},{1... | collective-permute-start | bytes 393224 | tf_op jit(solution)/shard_map/ppermute | solution.py:401
  51.2 10.9 %copy-start.6 = (bf16[2,256,256]{2,1,0:T(8,128)(2,1)S(1)}, bf16[2,256,256]{2,1,0:T(8,128)(2,1)}, u32[]{:S(2)}) copy-start(bf16[2,256,256]{2,1,0:T(8,128)(2,1)} %constant.20.clone.inner) | copy-start | bytes 786436
  51.6 10.5 %copy-start.4 = (f32[2,520,128]{2,1,0:T(8,128)S(1)}, f32[2,520,128]{2,1,0:T(8,128)}, u32[]{:S(2)}) copy-start(f32[2,520,128]{2,1,0:T(8,128)} %constant.23.clone.tw) | copy-start | bytes 1597444
  51.6 10.5 %copy-start.5 = (bf16[2,256,256]{2,1,0:T(8,128)(2,1)S(1)}, bf16[2,256,256]{2,1,0:T(8,128)(2,1)}, u32[]{:S(2)}) copy-start(bf16[2,256,256]{2,1,0:T(8,128)(2,1)} %constant.21.clone.block) | copy-start | bytes 786436
  51.9 13.4 %collective-permute-start.1 = (s32[8,4096]{1,0:T(8,128)}, s32[8,4096]{1,0:T(8,128)S(1)}, u32[]{:S(2)}, u32[]{:S(2)}) collective-permute-start(s32[8,4096]{1,0:T(8,128)} %collective-permute-done), channel_id=1, source_target_pairs={{0,128},{1,385},{2,130},{3,387},{4,132},{5,389},{6,134},{7,391},{8... | collective-permute-start | bytes 393224 | tf_op jit(solution)/shard_map/ppermute | solution.py:400
  65.2 47.9 %copy-start.1 = (bf16[2,256,256]{2,1,0:T(8,128)(2,1)S(1)}, bf16[2,256,256]{2,1,0:T(8,128)(2,1)}, u32[]{:S(2)}) copy-start(bf16[2,256,256]{2,1,0:T(8,128)(2,1)} %constant.19.clone.left) | copy-start | bytes 786436
  65.3 47.9 %copy-start.2 = (f32[2,32,128]{2,1,0:T(8,128)S(1)}, f32[2,32,128]{2,1,0:T(8,128)}, u32[]{:S(2)}) copy-start(f32[2,32,128]{2,1,0:T(8,128)} %constant.22.clone.tw) | copy-start | bytes 98308
  65.3 47.9 %copy-start.3 = (s32[8,4096]{1,0:T(8,128)S(1)}, s32[8,4096]{1,0:T(8,128)}, u32[]{:S(2)}) copy-start(s32[8,4096]{1,0:T(8,128)} %get-tuple-element.21.c0) | copy-start | bytes 393220
  113.2 18.2 %copy-start = (f32[2,32,4096]{2,1,0:T(8,128)S(1)}, f32[2,32,4096]{2,1,0:T(8,128)}, u32[]{:S(2)}) copy-start(f32[2,32,4096]{2,1,0:T(8,128)} %obj.5) | copy-start | bytes 3145732
  114.3 9.1 %collective-permute-start.4 = (f32[8,4096]{1,0:T(8,128)S(1)}, f32[8,4096]{1,0:T(8,128)S(1)}, u32[]{:S(2)}, u32[]{:S(2)}) collective-permute-start(f32[8,4096]{1,0:T(8,128)S(1)} %get-tuple-element.25.own_re), channel_id=1, source_target_pairs={{0,128},{1,385},{2,130},{3,387},{4,132},{5,389},{6,134},{7,391},{8... | collective-permute-start | bytes 393224 | tf_op jit(solution)/shard_map/ppermute | solution.py:413
  117.2 10.4 %collective-permute-start.6 = (f32[8,4096]{1,0:T(8,128)S(1)}, f32[8,4096]{1,0:T(8,128)S(1)}, u32[]{:S(2)}, u32[]{:S(2)}) collective-permute-start(f32[8,4096]{1,0:T(8,128)S(1)} %get-tuple-element.26.own_im), channel_id=1, source_target_pairs={{0,128},{1,385},{2,130},{3,387},{4,132},{5,389},{6,134},{7,391},{8... | collective-permute-start | bytes 393224 | tf_op jit(solution)/shard_map/ppermute | solution.py:414
  120.2 18.6 %collective-permute-start.8 = (f32[2,8,4096]{2,1,0:T(8,128)S(1)}, f32[2,8,4096]{2,1,0:T(8,128)S(1)}, u32[]{:S(2)}, u32[]{:S(2)}) collective-permute-start(f32[2,8,4096]{2,1,0:T(8,128)S(1)} %get-tuple-element.27), channel_id=1, source_target_pairs={{128,0},{385,1},{130,2},{387,3},{132,4},{389,5},{134,6},{391,7},{1... | collective-permute-start | bytes 786440 | tf_op jit(solution)/shard_map/ppermute | solution.py:415
  123.4 13.4 %collective-permute-start.5 = (f32[8,4096]{1,0:T(8,128)S(1)}, f32[8,4096]{1,0:T(8,128)S(1)}, u32[]{:S(2)}, u32[]{:S(2)}) collective-permute-start(f32[8,4096]{1,0:T(8,128)S(1)} %collective-permute-done.4.near_re), channel_id=1, source_target_pairs={{0,128},{1,385},{2,130},{3,387},{4,132},{5,389},{6,134},{7,391},{8... | collective-permute-start | bytes 393224 | tf_op jit(solution)/shard_map/ppermute | solution.py:416
  127.7 11.2 %collective-permute-start.7 = (f32[8,4096]{1,0:T(8,128)S(1)}, f32[8,4096]{1,0:T(8,128)S(1)}, u32[]{:S(2)}, u32[]{:S(2)}) collective-permute-start(f32[8,4096]{1,0:T(8,128)S(1)} %collective-permute-done.6.near_im), channel_id=1, source_target_pairs={{0,128},{1,385},{2,130},{3,387},{4,132},{5,389},{6,134},{7,391},{8... | collective-permute-start | bytes 393224 | tf_op jit(solution)/shard_map/ppermute | solution.py:417

commit v10 on v9

--- a/solution.py
+++ b/solution.py
@@ -144,20 +144,14 @@
     return jnp.where(code >= 2, -a, a), jnp.where((code == 1) | (code == 2), -b, b)
 
 
-def rows_forward(index, obj, code, every, left, tw, out, c0, c2, c1, c3, mid, xs, buf, sems, code_sems):
+def rows_forward(index, obj, code, left, tw, out, c0, c2, c1, c3, mid, xs):
     m = pl.program_id(0)
-
-    def code_copy(s, c):
-        row = pl.multiple_of(lax.rem(index[0] + s, MASKS) * OCT, OCT)
-        return pltpu.make_async_copy(every.at[0, pl.ds(row, OCT), :], c, code_sems.at[s])
-
-    def out_copy(step):
-        return pltpu.make_async_copy(buf.at[step], out.at[:, step], sems.at[step])
-
-    @pl.when(m == 0)
-    def _():
-        for s, c in enumerate((c0, c1, c2, c3)):
-            code_copy(s, c).start()
+    shift = lax.rem(m + MASKS - index[0], MASKS)
+    for s, c in enumerate((c0, c1, c2, c3)):
+
+        @pl.when(shift == s)
+        def _():
+            c[...] = code[0]
 
     def load(p):
         cols = slice(LANES * p, LANES * p + LANES)
@@ -172,17 +166,9 @@
     y = dot3((left[0], left[1]), split(xs[...]), NT)
     for ri in range(2):
         for h in range(2):
-            buf[m, :, ri * 2 + h, :] = y[
+            out[pl.ds(ri * 8 + 2 * m + h, LANES, stride=16), :] = y[
                 LANES * ri : LANES * ri + LANES, LANES * h : LANES * h + LANES
             ]
-    out_copy(m).start()
-
-    @pl.when(m == MASKS - 1)
-    def _():
-        for s, c in enumerate((c0, c1, c2, c3)):
-            code_copy(s, c).wait()
-        for step in range(MASKS):
-            out_copy(step).wait()
 
 
 def columns(rec, inten, inner, block, tw, out, s):
@@ -194,7 +180,7 @@
         x = jnp.concatenate(
             [
                 jnp.concatenate(
-                    [rec[pl.ds(m * 4 + ri * 2 + h, LANES, stride=16), :] for h in range(2)], axis=1
+                    [rec[pl.ds(ri * 8 + 2 * m + h, LANES, stride=16), :] for h in range(2)], axis=1
                 )
                 for ri in range(2)
             ],
@@ -362,27 +348,23 @@
     sent, c0, c2, c1, c3 = pl.pallas_call(
         rows_forward,
         name="rows_forward",
-        out_shape=(sds((LANES, MASKS, 4, LANES), F32),) + (rows8,) * MASKS,
+        out_shape=(sds((2048, LANES), F32),) + (rows8,) * MASKS,
         grid=(MASKS,),
         in_specs=[
             pl.BlockSpec(memory_space=pltpu.SMEM),
             pl.BlockSpec((2, OCT, N), octet),
             pl.BlockSpec((1, OCT, N), octet),
-            pl.BlockSpec(memory_space=pl.ANY),
             pl.BlockSpec((2, 256, 256), lambda m: (0, 0, 0)),
             pl.BlockSpec((2, SHORT, LANES), lambda m: (0, 0, 0)),
         ],
-        out_specs=(pl.BlockSpec(memory_space=pl.ANY),) * (1 + MASKS),
+        out_specs=(pl.BlockSpec((2048, LANES), flat),) + (pl.BlockSpec((OCT, N), flat),) * MASKS,
         scratch_shapes=[
             pltpu.VMEM((2, SHORT, OCT, LANES), F32),
             pltpu.VMEM((256, 256), F32),
-            pltpu.VMEM((MASKS, LANES, 4, LANES), F32),
-            pltpu.SemaphoreType.DMA((MASKS,)),
-            pltpu.SemaphoreType.DMA((MASKS,)),
         ],
         compiler_params=pltpu.CompilerParams(vmem_limit_bytes=60 << 20),
         cost_estimate=pl.CostEstimate(flops=1 << 29, bytes_accessed=3 << 20, transcendentals=0),
-    )(index, object_field, phases, phases, t["left"], t["row_tw"])
+    )(index, object_field, phases, t["left"], t["row_tw"])
     inten = intensity.reshape(2, 16, 8, 4, LANES).transpose(3, 0, 4, 1, 2).reshape(4, 256, LANES)
     up = [(i, (i + 1) % MASKS) for i in range(MASKS)]
     down = [((i + 1) % MASKS, i) for i in range(MASKS)]

time: 141 us -> 127 us (0.901)
  Pallas kernels: 24.4 us -> 10.8 us
    pallas_call x1, Pallas kernels: 18.2 us -> 4.6 us  [body(): pl.pallas_call(rows_forward, name='rows_forward', out_shape=(sds((2048, L...]
where the time goes in v10:
time: 127 us; the launch traced here: 126 us
  starting transfers between devices  50.5 us (40%)
  blocking collectives  47.9 us (38%)
  waiting for transfers between devices  14.8 us (12%)
  Pallas kernels  10.8 us (9%)
  local copies, waits for them, and re-layouts  1.42 us (1%)
    all_to_all x1, blocking collectives, body(): exchange(back.reshape(512, 4, LANES), ('mask', 'rows'), axis_index_groups...  47.9 us
    all_to_all x1, starting transfers between devices, body(): exchange(sent.reshape(LANES, 16, LANES), 'rows', axis_index_groups=[order])  14.4 us
    ppermute x2, starting transfers between devices, body(): g2 = lax.ppermute(lax.ppermute(c2, both, ring), both, ring)  11.7 us
    all_to_all x1, waiting for transfers between devices, body(): exchange(sent.reshape(LANES, 16, LANES), 'rows', axis_index_groups=[order])  8.34 us
    ppermute x1, starting transfers between devices, body(): g3 = lax.ppermute(c3, 'mask', down)  5.47 us
    pallas_call x1, Pallas kernels, body(): pl.pallas_call(rows_forward, name='rows_forward', out_shape=(sds((2048, L...  4.6 us
    ppermute x1, waiting for transfers between devices, body(): far_re = lax.ppermute(near_re, both, ring)  4.41 us
    ppermute x1, starting transfers between devices, body(): far_re = lax.ppermute(near_re, both, ring)  4.23 us
  transfers between devices with their start and end apart: 10, of which 3 were waited for; matrix products, arithmetic and copies ran while one was open for 1% of the time, Pallas kernels for 3%

profile of v10, /device:TPU:1, one launch (start us, length us, event | category | flops | bytes accessed | tf_op | source)
XLA Modules:
  0.0 126.3 jit_solution(11928352429423882962)
XLA Ops:
  0.6 4.6 %rows_forward.1 = (f32[2048,128]{1,0:T(8,128)}, s32[8,4096]{1,0:T(8,128)}, s32[8,4096]{1,0:T(8,128)}, s32[8,4096]{1,0:T(8,128)}, s32[8,4096]{1,0:T(8,128)}) custom-call(s32[1]{0:T(128)} %bitcast.index, f32[2,32,4096]{2,1,0:T(8,128)} %obj.5, s32[1,32,4096]{2,1,0:T(8,128)} %code.1, bf16[2,256,256]{2,1,0:T(8,128)(2,1)} %constant.19.clone.left, ...), custom_call_target="tpu_custom_call" | custom-call | flops 536870912 | bytes 3145728 | tf_op jit(solution)/shard_map/rows_forward/pallas_call | solution.py:348
  5.2 0.0 copy-start.7
  5.2 14.4 %all-to-all-start = ((f32[128,16,128]{2,1,0:T(8,128)}), f32[128,16,128]{2,1,0:T(8,128)S(1)}, u32[]{:S(2)}, u32[]{:S(2)}) async-start(f32[128,16,128]{2,1,0:T(8,128)} %bitcast.15), calls=%async_computation | async-start | bytes 2097152 | tf_op jit(solution)/shard_map/all_to_all | solution.py:380
  19.6 9.8 %collective-permute-start = (s32[8,4096]{1,0:T(8,128)}, s32[8,4096]{1,0:T(8,128)}, u32[]{:S(2)}, u32[]{:S(2)}) collective-permute-start(s32[8,4096]{1,0:T(8,128)} %get-tuple-element.17), channel_id=1, source_target_pairs={{0,128},{1,385},{2,130},{3,387},{4,132},{5,389},{6,134},{7,391},{8... | collective-permute-start | bytes 393224 | tf_op jit(solution)/shard_map/ppermute | solution.py:382
  29.4 1.9 %collective-permute-start.2 = (s32[8,4096]{1,0:T(8,128)}, s32[8,4096]{1,0:T(8,128)S(1)}, u32[]{:S(2)}, u32[]{:S(2)}) collective-permute-start(s32[8,4096]{1,0:T(8,128)} %get-tuple-element.18), channel_id=1, source_target_pairs={{0,128},{128,256},{256,384},{384,0},{1,129},{129,257},{257,385},{3... | collective-permute-start | bytes 393224 | tf_op jit(solution)/shard_map/ppermute | solution.py:381
  31.3 5.5 %collective-permute-start.3 = (s32[8,4096]{1,0:T(8,128)}, s32[8,4096]{1,0:T(8,128)S(1)}, u32[]{:S(2)}, u32[]{:S(2)}) collective-permute-start(s32[8,4096]{1,0:T(8,128)} %get-tuple-element.19), channel_id=1, source_target_pairs={{128,0},{256,128},{384,256},{0,384},{129,1},{257,129},{385,257},{1... | collective-permute-start | bytes 393224 | tf_op jit(solution)/shard_map/ppermute | solution.py:383
  36.8 0.0 copy-done.7
  36.8 0.4 reshape.32
  37.2 0.4 copy.16
  37.6 0.0 copy-start.4
  37.6 0.4 reshape.33
  38.0 0.0 copy-start.1
  38.0 0.0 copy-start.3
  38.0 0.2 copy.14.inten
  38.2 0.0 collective-permute-done
  38.2 1.9 %collective-permute-start.1 = (s32[8,4096]{1,0:T(8,128)}, s32[8,4096]{1,0:T(8,128)S(1)}, u32[]{:S(2)}, u32[]{:S(2)}) collective-permute-start(s32[8,4096]{1,0:T(8,128)} %collective-permute-done), channel_id=1, source_target_pairs={{0,128},{1,385},{2,130},{3,387},{4,132},{5,389},{6,134},{7,391},{8... | collective-permute-start | bytes 393224 | tf_op jit(solution)/shard_map/ppermute | solution.py:382
  40.2 8.3 %all-to-all-done = f32[128,16,128]{2,1,0:T(8,128)S(1)} async-done(((f32[128,16,128]{2,1,0:T(8,128)}), f32[128,16,128]{2,1,0:T(8,128)S(1)}, u32[]{:S(2)}, u32[]{:S(2)}) %all-to-all-start) | async-done | bytes 1048608 | tf_op jit(solution)/shard_map/all_to_all | solution.py:380
  48.5 0.0 copy-done.4
  48.5 0.0 copy-done.1
  48.5 0.0 copy-done.3
  48.5 3.1 %columns.1 = f32[2048,128]{1,0:T(8,128)S(1)} custom-call(f32[2048,128]{1,0:T(8,128)S(1)} %bitcast.11, f32[4,256,128]{2,1,0:T(8,128)S(1)} %copy.14.inten, bf16[2,256,256]{2,1,0:T(8,128)(2,1)S(1)} %copy-done.4, bf16[2,256,256]{2,1,0:T(8,128)(2,1)S(1)} %copy-done.3, f32[2,520,128]{2,1,0:T(8,128)S(1)} %copy-done.1), custom_call_target="tpu_custom_call" | custom-call | flops 1610612736 | bytes 3145728 | tf_op jit(solution)/shard_map/columns/pallas_call | solution.py:384
  51.6 0.0 collective-permute-done.2.c1
  51.6 0.0 collective-permute-done.3.c3
  51.6 0.0 collective-permute-done.1.c2
  51.6 0.0 copy-start.2
  51.6 0.0 copy-start.5
  51.7 0.0 copy-start.6
  51.7 47.9 %all_to_all.10 = f32[512,4,128]{2,1,0:T(4,128)S(1)} all-to-all(f32[512,4,128]{2,1,0:T(4,128)S(1)} %bitcast.12), channel_id=1, replica_groups={{0,128,256,384,2,130,258,386,4,132,260,388,6,134,262,390,8,136,264,392,..., dimensions={0} | all-to-all | bytes 2097152 | tf_op jit(solution)/shard_map/all_to_all | solution.py:389
  99.6 0.0 copy-start
  99.6 0.0 copy-done.2
  99.6 0.0 copy-done.5
  99.6 0.0 copy-done.6
  99.6 1.1 rows_back.1
  100.7 2.9 %collective-permute-start.4 = (f32[8,4096]{1,0:T(8,128)S(1)}, f32[8,4096]{1,0:T(8,128)S(1)}, u32[]{:S(2)}, u32[]{:S(2)}) collective-permute-start(f32[8,4096]{1,0:T(8,128)S(1)} %get-tuple-element.25.own_re), channel_id=1, source_target_pairs={{0,128},{1,385},{2,130},{3,387},{4,132},{5,389},{6,134},{7,391},{8... | collective-permute-start | bytes 393224 | tf_op jit(solution)/shard_map/ppermute | solution.py:395
  103.6 3.0 %collective-permute-start.6 = (f32[8,4096]{1,0:T(8,128)S(1)}, f32[8,4096]{1,0:T(8,128)S(1)}, u32[]{:S(2)}, u32[]{:S(2)}) collective-permute-start(f32[8,4096]{1,0:T(8,128)S(1)} %get-tuple-element.26.own_im), channel_id=1, source_target_pairs={{0,128},{1,385},{2,130},{3,387},{4,132},{5,389},{6,134},{7,391},{8... | collective-permute-start | bytes 393224 | tf_op jit(solution)/shard_map/ppermute | solution.py:396
  106.6 3.2 %collective-permute-start.8 = (f32[2,8,4096]{2,1,0:T(8,128)S(1)}, f32[2,8,4096]{2,1,0:T(8,128)S(1)}, u32[]{:S(2)}, u32[]{:S(2)}) collective-permute-start(f32[2,8,4096]{2,1,0:T(8,128)S(1)} %get-tuple-element.27), channel_id=1, source_target_pairs={{128,0},{385,1},{130,2},{387,3},{132,4},{389,5},{134,6},{391,7},{1... | collective-permute-start | bytes 786440 | tf_op jit(solution)/shard_map/ppermute | solution.py:397
  109.8 0.0 collective-permute-done.4.near_re
  109.8 4.2 %collective-permute-start.5 = (f32[8,4096]{1,0:T(8,128)S(1)}, f32[8,4096]{1,0:T(8,128)S(1)}, u32[]{:S(2)}, u32[]{:S(2)}) collective-permute-start(f32[8,4096]{1,0:T(8,128)S(1)} %collective-permute-done.4.near_re), channel_id=1, source_target_pairs={{0,128},{1,385},{2,130},{3,387},{4,132},{5,389},{6,134},{7,391},{8... | collective-permute-start | bytes 393224 | tf_op jit(solution)/shard_map/ppermute | solution.py:398
  114.0 0.0 collective-permute-done.6.near_im
  114.1 3.7 %collective-permute-start.7 = (f32[8,4096]{1,0:T(8,128)S(1)}, f32[8,4096]{1,0:T(8,128)S(1)}, u32[]{:S(2)}, u32[]{:S(2)}) collective-permute-start(f32[8,4096]{1,0:T(8,128)S(1)} %collective-permute-done.6.near_im), channel_id=1, source_target_pairs={{0,128},{1,385},{2,130},{3,387},{4,132},{5,389},{6,134},{7,391},{8... | collective-permute-start | bytes 393224 | tf_op jit(solution)/shard_map/ppermute | solution.py:399
  117.8 0.0 copy-done
  117.8 1.0 finish_first.1
  118.8 4.4 %collective-permute-done.5.far_re = f32[8,4096]{1,0:T(8,128)S(1)} collective-permute-done((f32[8,4096]{1,0:T(8,128)S(1)}, f32[8,4096]{1,0:T(8,128)S(1)}, u32[]{:S(2)}, u32[]{:S(2)}) %collective-permute-start.5) | collective-permute-done | bytes 131104 | tf_op jit(solution)/shard_map/ppermute | solution.py:398
  123.2 2.0 %collective-permute-done.7.far_im = f32[8,4096]{1,0:T(8,128)S(1)} collective-permute-done((f32[8,4096]{1,0:T(8,128)S(1)}, f32[8,4096]{1,0:T(8,128)S(1)}, u32[]{:S(2)}, u32[]{:S(2)}) %collective-permute-start.7) | collective-permute-done | bytes 131104 | tf_op jit(solution)/shard_map/ppermute | solution.py:399
  125.3 0.0 collective-permute-done.8.other
  125.3 1.0 finish_last.1
Async XLA Ops:
  5.2 31.6 %copy-start.7 = (f32[1,32,4096]{2,1,0:T(8,128)S(1)}, f32[1,32,4096]{2,1,0:T(8,128)}, u32[]{:S(2)}) copy-start(f32[1,32,4096]{2,1,0:T(8,128)} %param.10) | copy-start | bytes 1572868
  5.2 43.3 %all-to-all-start = ((f32[128,16,128]{2,1,0:T(8,128)}), f32[128,16,128]{2,1,0:T(8,128)S(1)}, u32[]{:S(2)}, u32[]{:S(2)}) async-start(f32[128,16,128]{2,1,0:T(8,128)} %bitcast.15), calls=%async_computation | async-start | bytes 2097152 | tf_op jit(solution)/shard_map/all_to_all | solution.py:380
  19.6 18.6 %collective-permute-start = (s32[8,4096]{1,0:T(8,128)}, s32[8,4096]{1,0:T(8,128)}, u32[]{:S(2)}, u32[]{:S(2)}) collective-permute-start(s32[8,4096]{1,0:T(8,128)} %get-tuple-element.17), channel_id=1, source_target_pairs={{0,128},{1,385},{2,130},{3,387},{4,132},{5,389},{6,134},{7,391},{8... | collective-permute-start | bytes 393224 | tf_op jit(solution)/shard_map/ppermute | solution.py:382
  29.4 22.2 %collective-permute-start.2 = (s32[8,4096]{1,0:T(8,128)}, s32[8,4096]{1,0:T(8,128)S(1)}, u32[]{:S(2)}, u32[]{:S(2)}) collective-permute-start(s32[8,4096]{1,0:T(8,128)} %get-tuple-element.18), channel_id=1, source_target_pairs={{0,128},{128,256},{256,384},{384,0},{1,129},{129,257},{257,385},{3... | collective-permute-start | bytes 393224 | tf_op jit(solution)/shard_map/ppermute | solution.py:381
  31.3 20.3 %collective-permute-start.3 = (s32[8,4096]{1,0:T(8,128)}, s32[8,4096]{1,0:T(8,128)S(1)}, u32[]{:S(2)}, u32[]{:S(2)}) collective-permute-start(s32[8,4096]{1,0:T(8,128)} %get-tuple-element.19), channel_id=1, source_target_pairs={{128,0},{256,128},{384,256},{0,384},{129,1},{257,129},{385,257},{1... | collective-permute-start | bytes 393224 | tf_op jit(solution)/shard_map/ppermute | solution.py:383
  37.6 10.9 %copy-start.4 = (bf16[2,256,256]{2,1,0:T(8,128)(2,1)S(1)}, bf16[2,256,256]{2,1,0:T(8,128)(2,1)}, u32[]{:S(2)}) copy-start(bf16[2,256,256]{2,1,0:T(8,128)(2,1)} %constant.20.clone.inner) | copy-start | bytes 786436
  38.0 10.5 %copy-start.1 = (f32[2,520,128]{2,1,0:T(8,128)S(1)}, f32[2,520,128]{2,1,0:T(8,128)}, u32[]{:S(2)}) copy-start(f32[2,520,128]{2,1,0:T(8,128)} %constant.23.clone.tw) | copy-start | bytes 1597444
  38.0 10.5 %copy-start.3 = (bf16[2,256,256]{2,1,0:T(8,128)(2,1)S(1)}, bf16[2,256,256]{2,1,0:T(8,128)(2,1)}, u32[]{:S(2)}) copy-start(bf16[2,256,256]{2,1,0:T(8,128)(2,1)} %constant.21.clone.block) | copy-start | bytes 786436
  38.2 13.4 %collective-permute-start.1 = (s32[8,4096]{1,0:T(8,128)}, s32[8,4096]{1,0:T(8,128)S(1)}, u32[]{:S(2)}, u32[]{:S(2)}) collective-permute-start(s32[8,4096]{1,0:T(8,128)} %collective-permute-done), channel_id=1, source_target_pairs={{0,128},{1,385},{2,130},{3,387},{4,132},{5,389},{6,134},{7,391},{8... | collective-permute-start | bytes 393224 | tf_op jit(solution)/shard_map/ppermute | solution.py:382
  51.6 48.0 %copy-start.2 = (bf16[2,256,256]{2,1,0:T(8,128)(2,1)S(1)}, bf16[2,256,256]{2,1,0:T(8,128)(2,1)}, u32[]{:S(2)}) copy-start(bf16[2,256,256]{2,1,0:T(8,128)(2,1)} %constant.19.clone.left) | copy-start | bytes 786436
  51.6 47.9 %copy-start.5 = (f32[2,32,128]{2,1,0:T(8,128)S(1)}, f32[2,32,128]{2,1,0:T(8,128)}, u32[]{:S(2)}) copy-start(f32[2,32,128]{2,1,0:T(8,128)} %constant.22.clone.tw) | copy-start | bytes 98308
  51.7 47.9 %copy-start.6 = (s32[8,4096]{1,0:T(8,128)S(1)}, s32[8,4096]{1,0:T(8,128)}, u32[]{:S(2)}) copy-start(s32[8,4096]{1,0:T(8,128)} %get-tuple-element.21.c0) | copy-start | bytes 393220
  99.6 18.2 %copy-start = (f32[2,32,4096]{2,1,0:T(8,128)S(1)}, f32[2,32,4096]{2,1,0:T(8,128)}, u32[]{:S(2)}) copy-start(f32[2,32,4096]{2,1,0:T(8,128)} %obj.5) | copy-start | bytes 3145732
  100.7 9.1 %collective-permute-start.4 = (f32[8,4096]{1,0:T(8,128)S(1)}, f32[8,4096]{1,0:T(8,128)S(1)}, u32[]{:S(2)}, u32[]{:S(2)}) collective-permute-start(f32[8,4096]{1,0:T(8,128)S(1)} %get-tuple-element.25.own_re), channel_id=1, source_target_pairs={{0,128},{1,385},{2,130},{3,387},{4,132},{5,389},{6,134},{7,391},{8... | collective-permute-start | bytes 393224 | tf_op jit(solution)/shard_map/ppermute | solution.py:395
  103.6 10.5 %collective-permute-start.6 = (f32[8,4096]{1,0:T(8,128)S(1)}, f32[8,4096]{1,0:T(8,128)S(1)}, u32[]{:S(2)}, u32[]{:S(2)}) collective-permute-start(f32[8,4096]{1,0:T(8,128)S(1)} %get-tuple-element.26.own_im), channel_id=1, source_target_pairs={{0,128},{1,385},{2,130},{3,387},{4,132},{5,389},{6,134},{7,391},{8... | collective-permute-start | bytes 393224 | tf_op jit(solution)/shard_map/ppermute | solution.py:396
  106.6 18.6 %collective-permute-start.8 = (f32[2,8,4096]{2,1,0:T(8,128)S(1)}, f32[2,8,4096]{2,1,0:T(8,128)S(1)}, u32[]{:S(2)}, u32[]{:S(2)}) collective-permute-start(f32[2,8,4096]{2,1,0:T(8,128)S(1)} %get-tuple-element.27), channel_id=1, source_target_pairs={{128,0},{385,1},{130,2},{387,3},{132,4},{389,5},{134,6},{391,7},{1... | collective-permute-start | bytes 786440 | tf_op jit(solution)/shard_map/ppermute | solution.py:397
  109.8 13.4 %collective-permute-start.5 = (f32[8,4096]{1,0:T(8,128)S(1)}, f32[8,4096]{1,0:T(8,128)S(1)}, u32[]{:S(2)}, u32[]{:S(2)}) collective-permute-start(f32[8,4096]{1,0:T(8,128)S(1)} %collective-permute-done.4.near_re), channel_id=1, source_target_pairs={{0,128},{1,385},{2,130},{3,387},{4,132},{5,389},{6,134},{7,391},{8... | collective-permute-start | bytes 393224 | tf_op jit(solution)/shard_map/ppermute | solution.py:398
  114.1 11.2 %collective-permute-start.7 = (f32[8,4096]{1,0:T(8,128)S(1)}, f32[8,4096]{1,0:T(8,128)S(1)}, u32[]{:S(2)}, u32[]{:S(2)}) collective-permute-start(f32[8,4096]{1,0:T(8,128)S(1)} %collective-permute-done.6.near_im), channel_id=1, source_target_pairs={{0,128},{1,385},{2,130},{3,387},{4,132},{5,389},{6,134},{7,391},{8... | collective-permute-start | bytes 393224 | tf_op jit(solution)/shard_map/ppermute | solution.py:399

commit v11 on v10

--- a/solution.py
+++ b/solution.py
@@ -144,12 +144,12 @@
     return jnp.where(code >= 2, -a, a), jnp.where((code == 1) | (code == 2), -b, b)
 
 
-def rows_forward(index, obj, code, left, tw, out, c0, c2, c1, c3, mid, xs):
+def rows_forward(index, obj, code, left, tw, out, c2, c1, c3, mid, xs):
     m = pl.program_id(0)
     shift = lax.rem(m + MASKS - index[0], MASKS)
-    for s, c in enumerate((c0, c1, c2, c3)):
-
-        @pl.when(shift == s)
+    for s, c in enumerate((c1, c2, c3)):
+
+        @pl.when(shift == s + 1)
         def _():
             c[...] = code[0]
 
@@ -345,10 +345,10 @@
     octet = lambda m: (0, m, 0)
     flat = lambda m: (0, 0)
     rows8 = sds((OCT, N), jnp.int32)
-    sent, c0, c2, c1, c3 = pl.pallas_call(
+    sent, c2, c1, c3 = pl.pallas_call(
         rows_forward,
         name="rows_forward",
-        out_shape=(sds((2048, LANES), F32),) + (rows8,) * MASKS,
+        out_shape=(sds((2048, LANES), F32),) + (rows8,) * 3,
         grid=(MASKS,),
         in_specs=[
             pl.BlockSpec(memory_space=pltpu.SMEM),
@@ -357,7 +357,7 @@
             pl.BlockSpec((2, 256, 256), lambda m: (0, 0, 0)),
             pl.BlockSpec((2, SHORT, LANES), lambda m: (0, 0, 0)),
         ],
-        out_specs=(pl.BlockSpec((2048, LANES), flat),) + (pl.BlockSpec((OCT, N), flat),) * MASKS,
+        out_specs=(pl.BlockSpec((2048, LANES), flat),) + (pl.BlockSpec((OCT, N), flat),) * 3,
         scratch_shapes=[
             pltpu.VMEM((2, SHORT, OCT, LANES), F32),
             pltpu.VMEM((256, 256), F32),
@@ -381,11 +381,12 @@
     g1 = lax.ppermute(c1, "mask", up)
     g2 = lax.ppermute(lax.ppermute(c2, both, ring), both, ring)
     g3 = lax.ppermute(c3, "mask", down)
+    c0 = lax.dynamic_slice_in_dim(phases[0], index[0] * OCT, OCT)
     back = call(
         columns, "columns", sds((2048, LANES), F32), 5,
         [pltpu.VMEM((4, 2, 2, LANES, LANES), F32)], 3 << 29,
     )(rec.reshape(2048, LANES), inten, t["inner"], t["block"], t["col_tw"])
-    back, g2, g1, g3 = lax.optimization_barrier((back, g2, g1, g3))
+    back, g2, g1, g3, c0 = lax.optimization_barrier((back, g2, g1, g3, c0))
     rec = exchange(back.reshape(512, 4, LANES), ("mask", "rows"), axis_index_groups=[every])
     half = sds((OCT, N), F32)
     part, own_re, own_im = call(

time: 127 us -> 127 us (level)
  waiting for transfers between devices: 14.8 us -> 11.7 us
  local copies, waits for them, and re-layouts: 1.42 us -> 4.24 us
    all_to_all x1, waiting for transfers between devices: 8.34 us -> 5.24 us  [body(): exchange(sent.reshape(LANES, 16, LANES), 'rows', axis_index_groups=[order])]
    reshape x4, local copies, waits for them, and re-layouts: 1.37 us -> 3.27 us  [body(): intensity.reshape(2, 16, 8, 4, LANES).transpose(3, 0, 4, 1, 2)]
  transfers between devices with their start and end apart: 10 -> 10, of which waited for: 3 -> 3; matrix products, arithmetic and copies ran while one was open for 1% -> 3% of each run, Pallas kernels for 3% -> 3%
where the time goes in v11:
time: 127 us; the launch traced here: 126 us
  starting transfers between devices  50.5 us (40%)
  blocking collectives  48.2 us (38%)
  waiting for transfers between devices  11.7 us (9%)
  Pallas kernels  10.8 us (9%)
  local copies, waits for them, and re-layouts  4.24 us (3%)
    all_to_all x1, blocking collectives, body(): exchange(back.reshape(512, 4, LANES), ('mask', 'rows'), axis_index_groups...  48.2 us
    all_to_all x1, starting transfers between devices, body(): exchange(sent.reshape(LANES, 16, LANES), 'rows', axis_index_groups=[order])  14.4 us
    ppermute x2, starting transfers between devices, body(): g2 = lax.ppermute(lax.ppermute(c2, both, ring), both, ring)  11.7 us
    ppermute x1, starting transfers between devices, body(): g3 = lax.ppermute(c3, 'mask', down)  5.47 us
    all_to_all x1, waiting for transfers between devices, body(): exchange(sent.reshape(LANES, 16, LANES), 'rows', axis_index_groups=[order])  5.24 us
    pallas_call x1, Pallas kernels, body(): pl.pallas_call(rows_forward, name='rows_forward', out_shape=(sds((2048, L...  4.57 us
    ppermute x1, waiting for transfers between devices, body(): far_re = lax.ppermute(near_re, both, ring)  4.41 us
    ppermute x1, starting transfers between devices, body(): far_re = lax.ppermute(near_re, both, ring)  4.23 us
  transfers between devices with their start and end apart: 10, of which 3 were waited for; matrix products, arithmetic and copies ran while one was open for 3% of the time, Pallas kernels for 3%

profile of v11, /device:TPU:1, one launch (start us, length us, event | category | flops | bytes accessed | tf_op | source)
XLA Modules:
  0.0 126.3 jit_solution(13191734744058702807)
XLA Ops:
  0.6 4.6 %rows_forward.1 = (f32[2048,128]{1,0:T(8,128)}, s32[8,4096]{1,0:T(8,128)}, s32[8,4096]{1,0:T(8,128)}, s32[8,4096]{1,0:T(8,128)}) custom-call(s32[1]{0:T(128)} %bitcast.index, f32[2,32,4096]{2,1,0:T(8,128)} %obj.5, s32[1,32,4096]{2,1,0:T(8,128)} %code.1, bf16[2,256,256]{2,1,0:T(8,128)(2,1)} %constant.26.clone.left, f32[2,32,128]{2,1,0:T(8,128)} %constant.29.clone.tw), custom_call_target="tpu_custom_call" | custom-call | flops 536870912 | bytes 3145728 | tf_op jit(solution)/shard_map/rows_forward/pallas_call | solution.py:348
  5.2 0.0 copy-start.7
  5.2 0.0 copy-start.6
  5.2 14.4 %all-to-all-start = ((f32[128,16,128]{2,1,0:T(8,128)}), f32[128,16,128]{2,1,0:T(8,128)S(1)}, u32[]{:S(2)}, u32[]{:S(2)}) async-start(f32[128,16,128]{2,1,0:T(8,128)} %bitcast.17), calls=%async_computation | async-start | bytes 2097152 | tf_op jit(solution)/shard_map/all_to_all | solution.py:380
  19.6 9.8 %collective-permute-start = (s32[8,4096]{1,0:T(8,128)}, s32[8,4096]{1,0:T(8,128)S(1)}, u32[]{:S(2)}, u32[]{:S(2)}) collective-permute-start(s32[8,4096]{1,0:T(8,128)} %get-tuple-element.17), channel_id=1, source_target_pairs={{0,128},{1,385},{2,130},{3,387},{4,132},{5,389},{6,134},{7,391},{8... | collective-permute-start | bytes 393224 | tf_op jit(solution)/shard_map/ppermute | solution.py:382
  29.4 0.0 copy-done.8
  29.4 1.9 %collective-permute-start.2 = (s32[8,4096]{1,0:T(8,128)S(1)}, s32[8,4096]{1,0:T(8,128)S(1)}, u32[]{:S(2)}, u32[]{:S(2)}) collective-permute-start(s32[8,4096]{1,0:T(8,128)S(1)} %copy-done.8), channel_id=1, source_target_pairs={{0,128},{128,256},{256,384},{384,0},{1,129},{129,257},{257,385},{3... | collective-permute-start | bytes 393224 | tf_op jit(solution)/shard_map/ppermute | solution.py:381
  31.3 0.0 copy-done.7
  31.3 5.5 %collective-permute-start.3 = (s32[8,4096]{1,0:T(8,128)S(1)}, s32[8,4096]{1,0:T(8,128)S(1)}, u32[]{:S(2)}, u32[]{:S(2)}) collective-permute-start(s32[8,4096]{1,0:T(8,128)S(1)} %copy-done.7), channel_id=1, source_target_pairs={{128,0},{256,128},{384,256},{0,384},{129,1},{257,129},{385,257},{1... | collective-permute-start | bytes 393224 | tf_op jit(solution)/shard_map/ppermute | solution.py:383
  36.8 0.9 dynamic-slice_bitcast_fusion.c0
  37.7 0.0 copy-done.6
  37.7 0.4 reshape.33
  38.1 0.4 copy.16
  38.5 0.0 copy-start.4
  38.5 1.2 reshape.34
  39.7 0.0 copy-start.1
  39.7 0.0 copy-start.3
  39.7 1.3 %copy.14.inten = f32[4,256,128]{2,1,0:T(8,128)S(1)} copy(f32[4,256,128]{1,2,0:T(8,128)} %reshape.34) | data formatting | bytes 1048576 | tf_op jit(solution)/shard_map/reshape | solution.py:368
  41.1 0.0 collective-permute-done
  41.1 1.9 %collective-permute-start.1 = (s32[8,4096]{1,0:T(8,128)S(1)}, s32[8,4096]{1,0:T(8,128)S(1)}, u32[]{:S(2)}, u32[]{:S(2)}) collective-permute-start(s32[8,4096]{1,0:T(8,128)S(1)} %collective-permute-done), channel_id=1, source_target_pairs={{0,128},{1,385},{2,130},{3,387},{4,132},{5,389},{6,134},{7,391},{8... | collective-permute-start | bytes 393224 | tf_op jit(solution)/shard_map/ppermute | solution.py:382
  43.0 5.2 %all-to-all-done = f32[128,16,128]{2,1,0:T(8,128)S(1)} async-done(((f32[128,16,128]{2,1,0:T(8,128)}), f32[128,16,128]{2,1,0:T(8,128)S(1)}, u32[]{:S(2)}, u32[]{:S(2)}) %all-to-all-start) | async-done | bytes 1048608 | tf_op jit(solution)/shard_map/all_to_all | solution.py:380
  48.2 0.0 copy-done.4
  48.2 0.0 copy-done.1
  48.2 0.0 copy-done.3
  48.2 3.1 %columns.1 = f32[2048,128]{1,0:T(8,128)S(1)} custom-call(f32[2048,128]{1,0:T(8,128)S(1)} %bitcast.13, f32[4,256,128]{2,1,0:T(8,128)S(1)} %copy.14.inten, bf16[2,256,256]{2,1,0:T(8,128)(2,1)S(1)} %copy-done.4, bf16[2,256,256]{2,1,0:T(8,128)(2,1)S(1)} %copy-done.3, f32[2,520,128]{2,1,0:T(8,128)S(1)} %copy-done.1), custom_call_target="tpu_custom_call" | custom-call | flops 1610612736 | bytes 3145728 | tf_op jit(solution)/shard_map/columns/pallas_call | solution.py:385
  51.3 0.0 collective-permute-done.2.c1
  51.3 0.0 collective-permute-done.3.c3
  51.3 0.0 collective-permute-done.1.c2
  51.4 0.0 copy-start.2
  51.4 0.0 copy-start.5
  51.4 48.2 %all_to_all.10 = f32[512,4,128]{2,1,0:T(4,128)S(1)} all-to-all(f32[512,4,128]{2,1,0:T(4,128)S(1)} %bitcast.14), channel_id=1, replica_groups={{0,128,256,384,2,130,258,386,4,132,260,388,6,134,262,390,8,136,264,392,..., dimensions={0} | all-to-all | bytes 2097152 | tf_op jit(solution)/shard_map/all_to_all | solution.py:390
  99.6 0.0 copy-start
  99.6 0.0 copy-done.2
  99.6 0.0 copy-done.5
  99.6 1.1 rows_back.1
  100.7 2.9 %collective-permute-start.4 = (f32[8,4096]{1,0:T(8,128)S(1)}, f32[8,4096]{1,0:T(8,128)S(1)}, u32[]{:S(2)}, u32[]{:S(2)}) collective-permute-start(f32[8,4096]{1,0:T(8,128)S(1)} %get-tuple-element.25.own_re), channel_id=1, source_target_pairs={{0,128},{1,385},{2,130},{3,387},{4,132},{5,389},{6,134},{7,391},{8... | collective-permute-start | bytes 393224 | tf_op jit(solution)/shard_map/ppermute | solution.py:396
  103.6 3.0 %collective-permute-start.6 = (f32[8,4096]{1,0:T(8,128)S(1)}, f32[8,4096]{1,0:T(8,128)S(1)}, u32[]{:S(2)}, u32[]{:S(2)}) collective-permute-start(f32[8,4096]{1,0:T(8,128)S(1)} %get-tuple-element.26.own_im), channel_id=1, source_target_pairs={{0,128},{1,385},{2,130},{3,387},{4,132},{5,389},{6,134},{7,391},{8... | collective-permute-start | bytes 393224 | tf_op jit(solution)/shard_map/ppermute | solution.py:397
  106.6 3.2 %collective-permute-start.8 = (f32[2,8,4096]{2,1,0:T(8,128)S(1)}, f32[2,8,4096]{2,1,0:T(8,128)S(1)}, u32[]{:S(2)}, u32[]{:S(2)}) collective-permute-start(f32[2,8,4096]{2,1,0:T(8,128)S(1)} %get-tuple-element.27), channel_id=1, source_target_pairs={{128,0},{385,1},{130,2},{387,3},{132,4},{389,5},{134,6},{391,7},{1... | collective-permute-start | bytes 786440 | tf_op jit(solution)/shard_map/ppermute | solution.py:398
  109.8 0.0 collective-permute-done.4.near_re
  109.8 4.2 %collective-permute-start.5 = (f32[8,4096]{1,0:T(8,128)S(1)}, f32[8,4096]{1,0:T(8,128)S(1)}, u32[]{:S(2)}, u32[]{:S(2)}) collective-permute-start(f32[8,4096]{1,0:T(8,128)S(1)} %collective-permute-done.4.near_re), channel_id=1, source_target_pairs={{0,128},{1,385},{2,130},{3,387},{4,132},{5,389},{6,134},{7,391},{8... | collective-permute-start | bytes 393224 | tf_op jit(solution)/shard_map/ppermute | solution.py:399
  114.0 0.0 collective-permute-done.6.near_im
  114.0 3.7 %collective-permute-start.7 = (f32[8,4096]{1,0:T(8,128)S(1)}, f32[8,4096]{1,0:T(8,128)S(1)}, u32[]{:S(2)}, u32[]{:S(2)}) collective-permute-start(f32[8,4096]{1,0:T(8,128)S(1)} %collective-permute-done.6.near_im), channel_id=1, source_target_pairs={{0,128},{1,385},{2,130},{3,387},{4,132},{5,389},{6,134},{7,391},{8... | collective-permute-start | bytes 393224 | tf_op jit(solution)/shard_map/ppermute | solution.py:400
  117.7 0.0 copy-done
  117.8 1.0 finish_first.1
  118.8 4.4 %collective-permute-done.5.far_re = f32[8,4096]{1,0:T(8,128)S(1)} collective-permute-done((f32[8,4096]{1,0:T(8,128)S(1)}, f32[8,4096]{1,0:T(8,128)S(1)}, u32[]{:S(2)}, u32[]{:S(2)}) %collective-permute-start.5) | collective-permute-done | bytes 131104 | tf_op jit(solution)/shard_map/ppermute | solution.py:399
  123.2 2.0 %collective-permute-done.7.far_im = f32[8,4096]{1,0:T(8,128)S(1)} collective-permute-done((f32[8,4096]{1,0:T(8,128)S(1)}, f32[8,4096]{1,0:T(8,128)S(1)}, u32[]{:S(2)}, u32[]{:S(2)}) %collective-permute-start.7) | collective-permute-done | bytes 131104 | tf_op jit(solution)/shard_map/ppermute | solution.py:400
  125.3 0.0 collective-permute-done.8.other
  125.3 1.0 finish_last.1
  (1 shorter events, 0.0 us)
Async XLA Ops:
  5.2 24.2 %copy-start.8 = (s32[8,4096]{1,0:T(8,128)S(1)}, s32[8,4096]{1,0:T(8,128)}, u32[]{:S(2)}) copy-start(s32[8,4096]{1,0:T(8,128)} %get-tuple-element.18) | copy-start | bytes 393220
  5.2 26.1 %copy-start.7 = (s32[8,4096]{1,0:T(8,128)S(1)}, s32[8,4096]{1,0:T(8,128)}, u32[]{:S(2)}) copy-start(s32[8,4096]{1,0:T(8,128)} %get-tuple-element.19) | copy-start | bytes 393220
  5.2 32.5 %copy-start.6 = (f32[1,32,4096]{2,1,0:T(8,128)S(1)}, f32[1,32,4096]{2,1,0:T(8,128)}, u32[]{:S(2)}) copy-start(f32[1,32,4096]{2,1,0:T(8,128)} %param.10) | copy-start | bytes 1572868
  5.2 43.0 %all-to-all-start = ((f32[128,16,128]{2,1,0:T(8,128)}), f32[128,16,128]{2,1,0:T(8,128)S(1)}, u32[]{:S(2)}, u32[]{:S(2)}) async-start(f32[128,16,128]{2,1,0:T(8,128)} %bitcast.17), calls=%async_computation | async-start | bytes 2097152 | tf_op jit(solution)/shard_map/all_to_all | solution.py:380
  19.6 21.5 %collective-permute-start = (s32[8,4096]{1,0:T(8,128)}, s32[8,4096]{1,0:T(8,128)S(1)}, u32[]{:S(2)}, u32[]{:S(2)}) collective-permute-start(s32[8,4096]{1,0:T(8,128)} %get-tuple-element.17), channel_id=1, source_target_pairs={{0,128},{1,385},{2,130},{3,387},{4,132},{5,389},{6,134},{7,391},{8... | collective-permute-start | bytes 393224 | tf_op jit(solution)/shard_map/ppermute | solution.py:382
  29.4 21.9 %collective-permute-start.2 = (s32[8,4096]{1,0:T(8,128)S(1)}, s32[8,4096]{1,0:T(8,128)S(1)}, u32[]{:S(2)}, u32[]{:S(2)}) collective-permute-start(s32[8,4096]{1,0:T(8,128)S(1)} %copy-done.8), channel_id=1, source_target_pairs={{0,128},{128,256},{256,384},{384,0},{1,129},{129,257},{257,385},{3... | collective-permute-start | bytes 393224 | tf_op jit(solution)/shard_map/ppermute | solution.py:381
  31.3 20.0 %collective-permute-start.3 = (s32[8,4096]{1,0:T(8,128)S(1)}, s32[8,4096]{1,0:T(8,128)S(1)}, u32[]{:S(2)}, u32[]{:S(2)}) collective-permute-start(s32[8,4096]{1,0:T(8,128)S(1)} %copy-done.7), channel_id=1, source_target_pairs={{128,0},{256,128},{384,256},{0,384},{129,1},{257,129},{385,257},{1... | collective-permute-start | bytes 393224 | tf_op jit(solution)/shard_map/ppermute | solution.py:383
  38.5 9.7 %copy-start.4 = (bf16[2,256,256]{2,1,0:T(8,128)(2,1)S(1)}, bf16[2,256,256]{2,1,0:T(8,128)(2,1)}, u32[]{:S(2)}) copy-start(bf16[2,256,256]{2,1,0:T(8,128)(2,1)} %constant.27.clone.inner) | copy-start | bytes 786436
  39.7 8.5 %copy-start.1 = (f32[2,520,128]{2,1,0:T(8,128)S(1)}, f32[2,520,128]{2,1,0:T(8,128)}, u32[]{:S(2)}) copy-start(f32[2,520,128]{2,1,0:T(8,128)} %constant.30.clone.tw) | copy-start | bytes 1597444
  39.7 8.5 %copy-start.3 = (bf16[2,256,256]{2,1,0:T(8,128)(2,1)S(1)}, bf16[2,256,256]{2,1,0:T(8,128)(2,1)}, u32[]{:S(2)}) copy-start(bf16[2,256,256]{2,1,0:T(8,128)(2,1)} %constant.28.clone.block) | copy-start | bytes 786436
  41.1 10.3 %collective-permute-start.1 = (s32[8,4096]{1,0:T(8,128)S(1)}, s32[8,4096]{1,0:T(8,128)S(1)}, u32[]{:S(2)}, u32[]{:S(2)}) collective-permute-start(s32[8,4096]{1,0:T(8,128)S(1)} %collective-permute-done), channel_id=1, source_target_pairs={{0,128},{1,385},{2,130},{3,387},{4,132},{5,389},{6,134},{7,391},{8... | collective-permute-start | bytes 393224 | tf_op jit(solution)/shard_map/ppermute | solution.py:382
  51.4 48.2 %copy-start.2 = (bf16[2,256,256]{2,1,0:T(8,128)(2,1)S(1)}, bf16[2,256,256]{2,1,0:T(8,128)(2,1)}, u32[]{:S(2)}) copy-start(bf16[2,256,256]{2,1,0:T(8,128)(2,1)} %constant.26.clone.left) | copy-start | bytes 786436
  51.4 48.2 %copy-start.5 = (f32[2,32,128]{2,1,0:T(8,128)S(1)}, f32[2,32,128]{2,1,0:T(8,128)}, u32[]{:S(2)}) copy-start(f32[2,32,128]{2,1,0:T(8,128)} %constant.29.clone.tw) | copy-start | bytes 98308
  99.6 18.2 %copy-start = (f32[2,32,4096]{2,1,0:T(8,128)S(1)}, f32[2,32,4096]{2,1,0:T(8,128)}, u32[]{:S(2)}) copy-start(f32[2,32,4096]{2,1,0:T(8,128)} %obj.5) | copy-start | bytes 3145732
  100.7 9.1 %collective-permute-start.4 = (f32[8,4096]{1,0:T(8,128)S(1)}, f32[8,4096]{1,0:T(8,128)S(1)}, u32[]{:S(2)}, u32[]{:S(2)}) collective-permute-start(f32[8,4096]{1,0:T(8,128)S(1)} %get-tuple-element.25.own_re), channel_id=1, source_target_pairs={{0,128},{1,385},{2,130},{3,387},{4,132},{5,389},{6,134},{7,391},{8... | collective-permute-start | bytes 393224 | tf_op jit(solution)/shard_map/ppermute | solution.py:396
  103.6 10.5 %collective-permute-start.6 = (f32[8,4096]{1,0:T(8,128)S(1)}, f32[8,4096]{1,0:T(8,128)S(1)}, u32[]{:S(2)}, u32[]{:S(2)}) collective-permute-start(f32[8,4096]{1,0:T(8,128)S(1)} %get-tuple-element.26.own_im), channel_id=1, source_target_pairs={{0,128},{1,385},{2,130},{3,387},{4,132},{5,389},{6,134},{7,391},{8... | collective-permute-start | bytes 393224 | tf_op jit(solution)/shard_map/ppermute | solution.py:397
  106.6 18.6 %collective-permute-start.8 = (f32[2,8,4096]{2,1,0:T(8,128)S(1)}, f32[2,8,4096]{2,1,0:T(8,128)S(1)}, u32[]{:S(2)}, u32[]{:S(2)}) collective-permute-start(f32[2,8,4096]{2,1,0:T(8,128)S(1)} %get-tuple-element.27), channel_id=1, source_target_pairs={{128,0},{385,1},{130,2},{387,3},{132,4},{389,5},{134,6},{391,7},{1... | collective-permute-start | bytes 786440 | tf_op jit(solution)/shard_map/ppermute | solution.py:398
  109.8 13.4 %collective-permute-start.5 = (f32[8,4096]{1,0:T(8,128)S(1)}, f32[8,4096]{1,0:T(8,128)S(1)}, u32[]{:S(2)}, u32[]{:S(2)}) collective-permute-start(f32[8,4096]{1,0:T(8,128)S(1)} %collective-permute-done.4.near_re), channel_id=1, source_target_pairs={{0,128},{1,385},{2,130},{3,387},{4,132},{5,389},{6,134},{7,391},{8... | collective-permute-start | bytes 393224 | tf_op jit(solution)/shard_map/ppermute | solution.py:399
  114.0 11.2 %collective-permute-start.7 = (f32[8,4096]{1,0:T(8,128)S(1)}, f32[8,4096]{1,0:T(8,128)S(1)}, u32[]{:S(2)}, u32[]{:S(2)}) collective-permute-start(f32[8,4096]{1,0:T(8,128)S(1)} %collective-permute-done.6.near_im), channel_id=1, source_target_pairs={{0,128},{1,385},{2,130},{3,387},{4,132},{5,389},{6,134},{7,391},{8... | collective-permute-start | bytes 393224 | tf_op jit(solution)/shard_map/ppermute | solution.py:400
